TPU v7x, 128 devices: a whole 4x4x4 slice. The times are simulated.
128 devices in a mesh: gy: 16 (over z_hi, x, core), gz: 8 (over z_lo, y).
Axes of the slice: x: 4, y: 4, z: 4 (z_hi: 2, z_lo: 2; z = z_hi * 2 + z_lo), core: 2. Of those that a mesh axis runs over, the one named last changes fastest.
Arguments:
- reference_image: bfloat16 [64, 1024, 4096], P(None, 'gy', 'gz'), may hold values from -6 to 6
- deformed: bfloat16 [64, 1024, 4096], P(None, 'gy', 'gz'), may hold values from -12 to 12
- displacement: bfloat16 [3, 64, 1024, 4096], P(None, None, 'gy', 'gz'), may hold values from -1 to 1
- plane_factors: float32 [2, 32, 8, 128], P(None, None, None, 'gy'), may hold values from -2.5 to 2.5
- depth_factors: float32 [2, 32, 4096], P(None, None, 'gz'), may hold values from -6 to 6
Outputs:
- residual: bfloat16 [64, 1024, 4096], P(None, 'gy', 'gz')
- step_plane: float32 [2, 32, 8, 128], P(None, None, None, 'gy')
- step_depth: float32 [2, 32, 4096], P(None, None, 'gz')
All inputs are finite; a program needn't handle non-finite values.
Results may differ from a plain program's by a relative error of at most 0.0004.
Values may be sent and summed in bfloat16 or wider, within the bound.
A program may use at most 256 MiB of HBM per device.

v0:
```python
import jax
import jax.numpy as jnp
from jax import lax
from jax.sharding import PartitionSpec as P

RANK = 32
KNOT = 8


epsilon = 1e-06
damping = 0.01
highest = lax.Precision.HIGHEST


def extended(cells, sides, width):
    for axis, dim in sides:
        count = lax.axis_size(axis)
        ends = count - 1
        head = lax.slice_in_dim(cells, 0, width, axis=dim)
        tail = lax.slice_in_dim(cells, cells.shape[dim] - width, cells.shape[dim], axis=dim)
        cells = jnp.concatenate(
            [
                lax.ppermute(tail, axis, [(i, (i + 1) % count) for i in range(ends)]),
                cells,
                lax.ppermute(head, axis, [((i + 1) % count, i) for i in range(ends)]),
            ],
            axis=dim,
        )
    return cells


def tent_weights(shift):
    moved = shift.astype(jnp.float32)
    return [jnp.maximum(0.0, 1.0 - jnp.abs(moved - offset)) for offset in (-1.0, 0.0, 1.0)]


def warp_image(padded, displacement):
    depth_x, width_y, width_z = displacement.shape[1:]
    weight_x = tent_weights(displacement[0])
    weight_y = tent_weights(displacement[1])
    weight_z = tent_weights(displacement[2])
    summed = jnp.zeros((depth_x, width_y, width_z), jnp.float32)
    for along_x in range(3):
        for along_y in range(3):
            partial_z = jnp.zeros((depth_x, width_y, width_z), jnp.float32)
            for along_z in range(3):
                window = padded[
                    along_x : along_x + depth_x,
                    along_y : along_y + width_y,
                    along_z : along_z + width_z,
                ]
                partial_z = partial_z + weight_z[along_z] * window.astype(jnp.float32)
            summed = summed + weight_x[along_x] * weight_y[along_y] * partial_z
    return summed


def expand_nodes(nodes):
    return jnp.repeat(jnp.repeat(nodes, KNOT, axis=2), KNOT, axis=3)


def reduce_nodes(field):
    leading = field.shape[:-2]
    depth_x, width_y = field.shape[-2:]
    shaped = field.reshape(leading + (depth_x // KNOT, KNOT, width_y // KNOT, KNOT))
    return jnp.sum(shaped, axis=(-3, -1))


def contract_rank(left, right):
    return lax.dot_general(left, right, (((0,), (0,)), ((), ())), precision=highest)


def contract_cells(left, right):
    return jnp.dot(left, right, precision=highest)


def contract_depth(left, right):
    return lax.dot_general(left, right, (((1,), (1,)), ((), ())), precision=highest)


def strip_terms(image, padded, displacement, plane_voxels, depth_factors):
    depth_x, width_y, width_z = image.shape
    cells = depth_x * width_y
    warped = warp_image(padded, displacement).reshape(cells, width_z)
    values = image.astype(jnp.float32).reshape(cells, width_z)
    flat_plane = plane_voxels.reshape(2, plane_voxels.shape[1], cells)
    contrast = contract_rank(flat_plane[0], depth_factors[0])
    brightness = contract_rank(flat_plane[1], depth_factors[1])
    misfit = warped - contrast * values - brightness
    product = misfit * values
    squares = values * values
    grad_depth = -jnp.stack(
        [contract_cells(flat_plane[0], product), contract_cells(flat_plane[1], misfit)]
    )
    level_sum = jnp.sum(flat_plane[1] * flat_plane[1], axis=1)
    first_depth = contract_cells(flat_plane[0] * flat_plane[0], squares)
    grad_voxels = -jnp.stack(
        [contract_depth(depth_factors[0], product), contract_depth(depth_factors[1], misfit)]
    )
    diag_voxels = contract_depth(depth_factors[0] * depth_factors[0], squares)
    grad_plane = reduce_nodes(grad_voxels.reshape(2, -1, depth_x, width_y))
    first_diag = reduce_nodes(diag_voxels.reshape(-1, depth_x, width_y))
    depth_level = KNOT * KNOT * jnp.sum(depth_factors[1] * depth_factors[1], axis=1)
    squared_sum = jnp.sum(misfit * misfit)
    residual = misfit.reshape(depth_x, width_y, width_z).astype(jnp.bfloat16)
    return (
        residual,
        squared_sum,
        grad_plane,
        first_diag,
        depth_level,
        grad_depth,
        first_depth,
        level_sum,
    )


def local(reference_image, deformed, displacement, plane_factors, depth_factors):
    rimmed = extended(deformed, (("gy", 1), ("gz", 2)), 1)
    padded = jnp.pad(rimmed, ((1, 1), (0, 0), (0, 0)))
    plane_voxels = expand_nodes(plane_factors)
    (
        residual,
        local_energy,
        grad_plane,
        first_diag,
        depth_level,
        grad_depth,
        first_depth,
        level_sum,
    ) = strip_terms(reference_image, padded, displacement, plane_voxels, depth_factors)
    nodes_x = plane_factors.shape[2]
    nodes_y = plane_factors.shape[3] * lax.axis_size("gy")
    full_z = depth_factors.shape[2] * lax.axis_size("gz")
    energy = lax.psum(local_energy, ("gy", "gz"))
    grad_plane, first_diag, depth_level = lax.psum((grad_plane, first_diag, depth_level), "gz")
    diag_plane = jnp.stack(
        [first_diag, jnp.broadcast_to(depth_level[:, None, None], first_diag.shape)]
    )
    lam_plane = damping * RANK * energy / (nodes_x * nodes_y)
    lam_depth = damping * energy / full_z
    step_plane = -grad_plane / (diag_plane + lam_plane + epsilon)
    grad_depth, first_depth, level_sum = lax.psum((grad_depth, first_depth, level_sum), "gy")
    diag_depth = jnp.stack([first_depth, jnp.broadcast_to(level_sum[:, None], first_depth.shape)])
    step_depth = -grad_depth / (diag_depth + lam_depth + epsilon)
    return (residual, step_plane, step_depth)


def solution(mesh):
    placed = (
        P(None, "gy", "gz"),
        P(None, "gy", "gz"),
        P(None, None, "gy", "gz"),
        P(None, None, None, "gy"),
        P(None, None, "gz"),
    )
    return jax.shard_map(
        local,
        mesh=mesh,
        in_specs=placed,
        out_specs=(P(None, "gy", "gz"), P(None, None, None, "gy"), P(None, None, "gz")),
        check_vma=False,
    )
```

profile of v0, /device:TPU:1, one launch (start us, length us, event | category | flops | bytes accessed | tf_op | source)
XLA Modules:
  0.0 611.7 jit_solution(7184010167852653225)
XLA Ops:
  7.2 1.4 fusion.133
  8.7 4.5 collective-permute-start
  13.2 2.2 collective-permute-start.1
  15.4 9.0 %fusion.132 = (bf16[1,64,64,512]{3,2,1,0:T(8,128)(2,1)}, bf16[1,64,64,512]{3,2,1,0:T(8,128)(2,1)}, bf16[1,64,64,512]{3,2,1,0:T(8,128)(2,1)}) fusion(bf16[3,64,64,512]{3,2,1,0:T(8,128)(2,1)} %param.7), kind=kLoop, calls=%fused_computation.173 | loop fusion | bytes 25165824 | tf_op jit(solution)/shard_map/slice | solution.py:41
  24.9 8.8 %fusion.124 = f32[4096,512]{1,0:T(8,128)} fusion(f32[32,4096]{0,1:T(8,128)S(1)} %bitcast.293, f32[2,32,512]{2,1,0:T(8,128)S(1)} %copy-done.5), kind=kOutput, calls=%fused_computation.159 | convolution fusion | flops 805306368 | bytes 10551296 | tf_op jit(solution)/shard_map/dot_general | solution.py:69
  35.0 7.4 %convolution_reduce_fusion = f32[32,8,8]{0,2,1:T(8,128)} fusion(f32[8,8,8,8,512]{4,3,2,1,0:T(8,128)S(1)} %bitcast.291, f32[2,32,512]{2,1,0:T(8,128)S(1)} %copy-done.5), kind=kOutput, calls=%fused_computation.139 | convolution fusion | flops 805451776 | bytes 8462336 | tf_op jit(solution)/shard_map/dot_general | solution.py:77
  42.7 5.7 convolution_bitcast_fusion.2
  48.9 13.0 %copy.49 = bf16[64,64,512]{1,0,2:T(8,128)(2,1)} copy(bf16[64,64,512]{2,1,0:T(8,128)(2,1)} %param.6) | data formatting | bytes 8388608 | tf_op args[1]
  62.1 12.7 %copy.48 = bf16[64,1,512]{1,0,2:T(8,128)(2,1)} copy(bf16[64,1,512]{2,0,1:T(8,128)(2,1)S(1)} %collective-permute-done) | data formatting | bytes 131072 | tf_op jit(solution)/shard_map/ppermute | solution.py:23
  74.7 12.7 %copy.50 = bf16[64,1,512]{1,0,2:T(8,128)(2,1)} copy(bf16[64,1,512]{2,0,1:T(8,128)(2,1)S(1)} %collective-permute-done.1) | data formatting | bytes 131072 | tf_op jit(solution)/shard_map/ppermute | solution.py:25
  88.3 3.2 collective-permute-start.2
  91.5 1.3 collective-permute-start.3
  93.1 13.4 %copy.61 = bf16[1,64,64,512]{2,1,3,0:T(8,128)(2,1)} copy(bf16[1,64,64,512]{3,2,1,0:T(8,128)(2,1)} %get-tuple-element.14) | data formatting | bytes 8388608
  106.5 13.0 %copy.62 = bf16[1,64,64,512]{2,1,3,0:T(8,128)(2,1)} copy(bf16[1,64,64,512]{3,2,1,0:T(8,128)(2,1)} %get-tuple-element.13) | data formatting | bytes 8388608
  119.5 12.9 %copy.63 = bf16[1,64,64,512]{2,1,3,0:T(8,128)(2,1)} copy(bf16[1,64,64,512]{3,2,1,0:T(8,128)(2,1)} %get-tuple-element.12) | data formatting | bytes 8388608
  132.4 34.2 %psum.55 = f32[32]{0:T(128)S(1)} all-reduce(f32[32]{0:T(128)S(1)} %broadcast_reduce_fusion), channel_id=1, replica_groups=mesh['gy'=16,'gz'=8] {'gy'}, use_global_device_ids=true, to_apply=%region_11.12 | all-reduce | flops 32 | bytes 256 | tf_op jit(solution)/shard_map/psum | solution.py:142
  166.6 24.1 %maximum_maximum_fusion = (bf16[64,66,513]{1,0,2:T(8,128)(2,1)S(1)}, bf16[64,66,513]{1,0,2:T(8,128)(2,1)}) fusion(bf16[64,1,512]{1,0,2:T(8,128)(2,1)} %copy.50, bf16[64,64,512]{1,0,2:T(8,128)(2,1)} %copy.49, bf16[64,1,512]{1,0,2:T(8,128)(2,1)} %copy.48, bf16[64,66,1]{1,0,2:T(8,128)(2,1)S(1)} %collective-permute-done.2, ...), kind=kLoop, calls=%fused_computation.126 | loop fusion | flops 34670592 | bytes 13009920 | tf_op jit(solution)/shard_map/concatenate | solution.py:21
  190.7 24.0 %select_maximum_fusion = bf16[66,66,514]{1,0,2:T(8,128)(2,1)S(1)} fusion(bf16[64,66,1]{1,0,2:T(8,128)(2,1)S(1)} %collective-permute-done.3, bf16[64,66,1]{1,0,2:T(8,128)(2,1)S(1)} %collective-permute-done.2, bf16[64,1,512]{1,0,2:T(8,128)(2,1)} %copy.50, bf16[64,64,512]{1,0,2:T(8,128)(2,1)} %copy.49, bf16[64,1,512]{1,0,2:T(8,128)(2,1)} %copy.48), kind=kLoop, calls=%fused_computation.119 | loop fusion | flops 40301712 | bytes 8820240 | tf_op jit(solution)/shard_map/concatenate | solution.py:21
  214.7 119.0 %fusion.15 = f32[64,64,512]{1,0,2:T(8,128)} fusion(bf16[1,64,64,512]{2,1,3,0:T(8,128)(2,1)} %copy.61, bf16[1,64,64,512]{2,1,3,0:T(8,128)(2,1)} %copy.62, bf16[1,64,64,512]{2,1,3,0:T(8,128)(2,1)} %copy.63, bf16[64,64,512]{1,0,2:T(8,128)(2,1)} %copy.49, bf16[66,66,514]{1,0,2:T(8,128)(2,1)S(1)} %select_maximum_fusion, ...), kind=kLoop, calls=%fused_computation.26 | loop fusion | flops 293601280 | bytes 125960192 | tf_op jit(solution)/shard_map/add | solution.py:53
  333.8 12.7 %copy.56 = f32[64,64,512]{2,1,0:T(8,128)} copy(f32[64,64,512]{1,0,2:T(8,128)} %fusion.15) | data formatting | bytes 16777216 | tf_op jit(solution)/shard_map/add | solution.py:53
  346.5 1.6 broadcast_in_dim.32
  348.2 17.3 %multiply_reduce_fusion = (f32[]{:T(128)}, f32[4096,512]{1,0:T(8,128)}, bf16[4096,512]{1,0:T(8,128)(2,1)}, f32[4096,512]{1,0:T(8,128)S(1)}) fusion(bf16[64,64,512]{2,1,0:T(8,128)(2,1)} %param.5, f32[32,4096]{0,1:T(8,128)} %bitcast.295, f32[2,32,512]{2,1,0:T(8,128)S(1)} %copy-done.5, f32[4096,512]{1,0:T(8,128)} %fusion.124, f32[64,64,512]{2,1,0:T(8,128)} %copy.56), kind=kOutput, calls=%fused_computation.135 | convolution fusion | flops 822083584 | bytes 42532868 | tf_op jit(solution)/shard_map/dot_general | solution.py:69
  365.4 10.2 %convolution_bitcast_fusion.4 = f32[1,32,512]{2,1,0:T(8,128)S(1)} fusion(f32[4096,512]{1,0:T(8,128)} %get-tuple-element.16, f32[32,4096]{0,1:T(8,128)S(1)} %bitcast.294), kind=kOutput, calls=%fused_computation.142 | convolution fusion | flops 805306368 | bytes 8978432 | tf_op jit(solution)/shard_map/dot_general | solution.py:73
  375.7 7.7 %convolution_bitcast_fusion.1 = f32[32,4096]{1,0:T(8,128)S(1)} fusion(f32[4096,512]{1,0:T(8,128)S(1)} %copy-done, f32[2,32,512]{2,1,0:T(8,128)S(1)} %copy-done.5), kind=kOutput, calls=%fused_computation.137 | convolution fusion | flops 805306368 | bytes 8978432 | tf_op jit(solution)/shard_map/dot_general | solution.py:77
  383.4 5.3 convolution_bitcast_fusion.3
  388.7 8.0 %convolution_bitcast_fusion = f32[32,4096]{1,0:T(8,128)S(1)} fusion(f32[4096,512]{1,0:T(8,128)S(1)} %get-tuple-element.22, f32[2,32,512]{2,1,0:T(8,128)S(1)} %copy-done.5), kind=kOutput, calls=%fused_computation.136 | convolution fusion | flops 805306368 | bytes 8978432 | tf_op jit(solution)/shard_map/dot_general | solution.py:77
  396.7 71.6 %psum.52 = f32[]{:T(128)} all-reduce(f32[]{:T(128)} %get-tuple-element.15), channel_id=1, replica_groups=mesh['gy'=16,'gz'=8] {'gy','gz'}, use_global_device_ids=true, to_apply=%region_7.8 | all-reduce | flops 1 | bytes 8 | tf_op jit(solution)/shard_map/psum | solution.py:134
  468.9 2.0 copy.58
  470.9 2.2 maximum_reduce_fusion
  475.1 26.7 %all-reduce.2 = (f32[32]{0:T(128)S(1)}, f32[1,32,8,8]{1,3,2,0:T(8,128)S(1)}, f32[2,32,8,8]{1,3,2,0:T(8,128)S(1)}) all-reduce(f32[32]{0:T(128)S(1)} %copy-done.8, f32[1,32,8,8]{1,3,2,0:T(8,128)S(1)} %bitcast.303, f32[2,32,8,8]{1,3,2,0:T(8,128)S(1)} %neg.13), channel_id=1, replica_groups=mesh['gy'=16,'gz'=8] {'gz'}, use_global_device_ids=true, to_apply=%region_5.6 | all-reduce | flops 6176 | bytes 49408 | tf_op jit(solution)/shard_map/psum | solution.py:135
  502.5 100.3 %all-reduce.5.cloned.1.call-done = (f32[1,32,512]{2,1,0:T(8,128)}, f32[2,32,512]{2,1,0:T(8,128)}) async-done(((f32[1,32,512]{2,1,0:T(8,128)}, f32[2,32,512]{2,1,0:T(8,128)}), (f32[1,32,512]{2,1,0:T(8,128)}, f32[2,32,512]{2,1,0:T(8,128)})) %all-reduce.5.cloned.1.call-update) | async-done | bytes 196624 | tf_op jit(solution)/shard_map/psum | solution.py:142
  602.8 1.6 fusion.116
  (44 shorter events, 6.0 us)
Async XLA Ops:
  7.2 17.3 %copy-start.7 = (f32[2,32,8,8]{1,3,2,0:T(8,128)S(1)}, f32[2,32,8,8]{1,3,2,0:T(8,128)}, u32[]{:S(2)}) copy-start(f32[2,32,8,8]{1,3,2,0:T(8,128)} %param.8) | copy-start | bytes 49156
  7.2 17.3 %copy-start.5 = (f32[2,32,512]{2,1,0:T(8,128)S(1)}, f32[2,32,512]{2,1,0:T(8,128)}, u32[]{:S(2)}) copy-start(f32[2,32,512]{2,1,0:T(8,128)} %param.9) | copy-start | bytes 393220
  7.2 595.6 %all-reduce.5.cloned.1.call-start = ((), (), s32[]{:S(2)}) async-start(), calls=%async_computation | async-start | bytes 393216 | tf_op jit(solution)/shard_map/psum | solution.py:142
  8.7 53.3 %collective-permute-start = (bf16[64,1,512]{2,0,1:T(8,128)(2,1)S(1)}, bf16[64,1,512]{2,0,1:T(8,128)(2,1)S(1)}, u32[]{:S(2)}, u32[]{:S(2)}) collective-permute-start(bf16[64,1,512]{2,0,1:T(8,128)(2,1)S(1)} %copy.64), channel_id=1, source_target_pairs={{0,8},{8,16},{16,24},{24,32},{32,40},{40,48},{48,56},{56,64},{64,7... | collective-permute-start | bytes 196616 | tf_op jit(solution)/shard_map/ppermute | solution.py:23
  13.2 20.5 %copy-start.4 = (bf16[64,64,512]{2,1,0:T(8,128)(2,1)S(1)}, bf16[64,64,512]{2,1,0:T(8,128)(2,1)}, u32[]{:S(2)}) copy-start(bf16[64,64,512]{2,1,0:T(8,128)(2,1)} %param.5) | copy-start | bytes 12582916
  13.2 61.5 %collective-permute-start.1 = (bf16[64,1,512]{2,0,1:T(8,128)(2,1)S(1)}, bf16[64,1,512]{2,0,1:T(8,128)(2,1)S(1)}, u32[]{:S(2)}, u32[]{:S(2)}) collective-permute-start(bf16[64,1,512]{2,0,1:T(8,128)(2,1)S(1)} %copy.65), channel_id=1, source_target_pairs={{8,0},{16,8},{24,16},{32,24},{40,32},{48,40},{56,48},{64,56},{72,6... | collective-permute-start | bytes 196616 | tf_op jit(solution)/shard_map/ppermute | solution.py:25
  24.9 8.8 %copy-start.1 = (f32[32,64,8,8]{0,3,2,1:T(8,128)}, f32[32,64,8,8]{0,3,2,1:T(8,128)S(1)}, u32[]{:S(2)}) copy-start(f32[32,64,8,8]{0,3,2,1:T(8,128)S(1)} %broadcast_in_dim.28) | copy-start | bytes 1572868
  88.3 78.3 %collective-permute-start.2 = (bf16[64,66,1]{1,0,2:T(8,128)(2,1)S(1)}, bf16[64,66,1]{1,0,2:T(8,128)(2,1)S(1)}, u32[]{:S(2)}, u32[]{:S(2)}) collective-permute-start(bf16[64,66,1]{1,0,2:T(8,128)(2,1)S(1)} %get-tuple-element.10), channel_id=1, source_target_pairs={{0,1},{1,2},{2,3},{3,4},{4,5},{5,6},{6,7},{8,9},{9,10},{10,11},{11... | collective-permute-start | bytes 25352 | tf_op jit(solution)/shard_map/ppermute | solution.py:23
  91.5 75.1 %collective-permute-start.3 = (bf16[64,66,1]{1,0,2:T(8,128)(2,1)S(1)}, bf16[64,66,1]{1,0,2:T(8,128)(2,1)S(1)}, u32[]{:S(2)}, u32[]{:S(2)}) collective-permute-start(bf16[64,66,1]{1,0,2:T(8,128)(2,1)S(1)} %get-tuple-element.11), channel_id=1, source_target_pairs={{1,0},{2,1},{3,2},{4,3},{5,4},{6,5},{7,6},{9,8},{10,9},{11,10},{12... | collective-permute-start | bytes 25352 | tf_op jit(solution)/shard_map/ppermute | solution.py:25
  348.1 17.3 %copy-start.2 = (f32[32,64,8,8]{0,3,2,1:T(8,128)S(1)}, f32[32,64,8,8]{0,3,2,1:T(8,128)}, u32[]{:S(2)}) copy-start(f32[32,64,8,8]{0,3,2,1:T(8,128)} %copy-done.1) | copy-start | bytes 1572868
  365.4 10.2 %copy-start = (f32[4096,512]{1,0:T(8,128)S(1)}, f32[4096,512]{1,0:T(8,128)}, u32[]{:S(2)}) copy-start(f32[4096,512]{1,0:T(8,128)} %get-tuple-element.16) | copy-start | bytes 25165828
  365.4 18.0 %copy-start.3 = (f32[32,64,8,8]{0,3,2,1:T(8,128)S(1)}, f32[32,64,8,8]{0,3,2,1:T(8,128)}, u32[]{:S(2)}) copy-start(f32[32,64,8,8]{0,3,2,1:T(8,128)} %broadcast_in_dim.32) | copy-start | bytes 1572868
  383.4 91.7 %copy-start.6 = (f32[32,8,8]{0,2,1:T(8,128)S(1)}, f32[32,8,8]{0,2,1:T(8,128)}, u32[]{:S(2)}) copy-start(f32[32,8,8]{0,2,1:T(8,128)} %convolution_reduce_fusion) | copy-start | bytes 24580
  383.4 91.7 %copy-start.8 = (f32[32]{0:T(128)S(1)}, f32[32]{0:T(128)}, u32[]{:S(2)}) copy-start(f32[32]{0:T(128)} %broadcast_multiply_fusion) | copy-start | bytes 388
Sparse Core Ops, SparseCore 0:
  475.2 127.5 all-reduce.4
where the time goes:
time: 621 us; the launch traced here: 612 us
  other arithmetic  175 us (28%)
  blocking collectives  133 us (21%)
  local copies, waits for them, and re-layouts  106 us (17%)
  waiting for transfers between devices  100 us (16%)
  matrix products  70.3 us (11%)
  between operations  16.1 us (3%)
  starting transfers between devices  11.2 us (2%)
    add x1, other arithmetic, warp_image(): summed = summed + weight_x[along_x] * weight_y[along_y] * partial_z  119 us
    psum x1, waiting for transfers between devices, local(): lax.psum((grad_depth, first_depth, level_sum), 'gy')  100 us
    psum x1, blocking collectives, local(): energy = lax.psum(local_energy, ('gy', 'gz'))  71.6 us
    unnamed x24, local copies, waits for them, and re-layouts  52.3 us
    concatenate x2, other arithmetic, extended(): jnp.concatenate([lax.ppermute(tail, axis, [(i, (i + 1) % count) for i in...  48.1 us
    psum x1, blocking collectives, local(): lax.psum((grad_depth, first_depth, level_sum), 'gy')  34.2 us
    psum x1, blocking collectives, local(): lax.psum((grad_plane, first_diag, depth_level), 'gz')  26.7 us
    dot_general x2, matrix products, contract_rank(): lax.dot_general(left, right, (((0,), (0,)), ((), ())), precision=highest)  26.1 us
  transfers between devices with their start and end apart: 5, of which 1 were waited for; matrix products, arithmetic and copies ran while one was open for 16% of the time, Pallas kernels for 0%

commit v1 on v0

v1 whole, which is shorter than its diff:
```python
import jax
import jax.numpy as jnp
from jax import lax
from jax.experimental import pallas as pl
from jax.experimental.pallas import tpu as pltpu
from jax.sharding import PartitionSpec as P

RANK = 32
KNOT = 8

epsilon = 1e-06
damping = 0.01
highest = lax.Precision.HIGHEST

ROWS = 16
LANES = 256


def neighbours(part, axis, forward):
    count = lax.axis_size(axis)
    if forward:
        pairs = [(i, i + 1) for i in range(count - 1)]
    else:
        pairs = [(i + 1, i) for i in range(count - 1)]
    return lax.ppermute(part, axis, pairs)


def padded_deformed(deformed):
    depth_x, width_y, width_z = deformed.shape
    low_y = neighbours(deformed[:, width_y - 1 :, :], "gy", True)
    high_y = neighbours(deformed[:, :1, :], "gy", False)
    gap_y = jnp.zeros((depth_x, 6, width_z), deformed.dtype)
    rimmed = jnp.concatenate([deformed, high_y, gap_y, low_y], axis=1)
    low_z = neighbours(rimmed[:, :, width_z - 1 :], "gz", True)
    high_z = neighbours(rimmed[:, :, :1], "gz", False)
    gap_z = jnp.zeros((depth_x, rimmed.shape[1], 126), deformed.dtype)
    return jnp.concatenate([rimmed, high_z, gap_z, low_z], axis=2)


def lerp(base, other, weight):
    return base + weight * (other - base)


def strip_kernel(dpad_ref, disp_ref, image_ref, contrast_ref, bright_ref,
                 res_ref, prod_ref, mis_ref, sq_ref, energy_ref, shifts_ref):
    block = pl.program_id(0)
    depth_x = dpad_ref.shape[0]
    pad_y, pad_z = dpad_ref.shape[1], dpad_ref.shape[2]
    width_y, width_z = image_ref.shape[1], image_ref.shape[2]

    def source_plane(p, carry):
        plane_x = block * KNOT - 1 + p
        valid = jnp.logical_and(plane_x >= 0, plane_x < depth_x)
        safe = jnp.clip(plane_x, 0, depth_x - 1)
        plane = dpad_ref[safe].astype(jnp.float32)
        plane = jnp.where(valid, plane, 0.0)
        by_y = (pltpu.roll(plane, 1, 0), plane, pltpu.roll(plane, pad_y - 1, 0))
        for b in range(3):
            rows = by_y[b][:width_y]
            by_z = (pltpu.roll(rows, 1, 1), rows, pltpu.roll(rows, pad_z - 1, 1))
            for c in range(3):
                shifts_ref[p, 3 * b + c] = by_z[c][:, :width_z]
        return carry

    lax.fori_loop(0, KNOT + 2, source_plane, 0)

    chunks_y = width_y // ROWS
    chunks_z = width_z // LANES

    def chunk(k, energy):
        r0 = pl.multiple_of((k // chunks_z) * ROWS, ROWS)
        c0 = pl.multiple_of((k % chunks_z) * LANES, LANES)
        rs = pl.ds(r0, ROWS)
        cs = pl.ds(c0, LANES)
        contrast = contrast_ref[0, rs, cs]
        bright = bright_ref[0, rs, cs]

        def plane(xl, acc):
            prod_acc, mis_acc, sq_acc, e_acc = acc

            def src(a, b, c):
                return shifts_ref[xl + 1 + a, 3 * (b + 1) + (c + 1), rs, cs]

            sx = disp_ref[0, xl, rs, cs].astype(jnp.float32)
            sy = disp_ref[1, xl, rs, cs].astype(jnp.float32)
            sz = disp_ref[2, xl, rs, cs].astype(jnp.float32)
            gx, gy, gz = sx > 0, sy > 0, sz > 0
            ax, ay, az = jnp.abs(sx), jnp.abs(sy), jnp.abs(sz)
            xs = {}
            for b in (-1, 0, 1):
                for c in (-1, 0, 1):
                    xs[b, c] = jnp.where(gx, src(1, b, c), src(-1, b, c))
            y0 = {c: jnp.where(gy, src(0, 1, c), src(0, -1, c)) for c in (-1, 0, 1)}
            y1 = {c: jnp.where(gy, xs[1, c], xs[-1, c]) for c in (-1, 0, 1)}
            centre = src(0, 0, 0)
            z00 = jnp.where(gz, src(0, 0, 1), src(0, 0, -1))
            z01 = jnp.where(gz, y0[1], y0[-1])
            z10 = jnp.where(gz, xs[0, 1], xs[0, -1])
            z11 = jnp.where(gz, y1[1], y1[-1])
            l00 = lerp(centre, z00, az)
            l01 = lerp(y0[0], z01, az)
            l10 = lerp(xs[0, 0], z10, az)
            l11 = lerp(y1[0], z11, az)
            m0 = lerp(l00, l01, ay)
            m1 = lerp(l10, l11, ay)
            warped = lerp(m0, m1, ax)
            values = image_ref[xl, rs, cs].astype(jnp.float32)
            misfit = warped - contrast * values - bright
            res_ref[xl, rs, cs] = misfit.astype(res_ref.dtype)
            return (prod_acc + misfit * values, mis_acc + misfit,
                    sq_acc + values * values, e_acc + misfit * misfit)

        zero = jnp.zeros((ROWS, LANES), jnp.float32)
        prod_acc, mis_acc, sq_acc, e_acc = lax.fori_loop(
            0, KNOT, plane, (zero, zero, zero, energy))
        prod_ref[0, rs, cs] = prod_acc
        mis_ref[0, rs, cs] = mis_acc
        sq_ref[0, rs, cs] = sq_acc
        return e_acc

    energy = lax.fori_loop(0, chunks_y * chunks_z, chunk,
                           jnp.zeros((ROWS, LANES), jnp.float32))
    energy_ref[0] = energy


def strip_sums(dpad, displacement, image, contrast_y, bright_y):
    depth_x, width_y, width_z = image.shape
    nodes = depth_x // KNOT
    f32 = jnp.float32
    block_sum = jax.ShapeDtypeStruct((nodes, width_y, width_z), f32)
    node_spec = pl.BlockSpec((1, width_y, width_z), lambda i: (i, 0, 0))
    return pl.pallas_call(
        strip_kernel,
        grid=(nodes,),
        in_specs=[
            pl.BlockSpec(memory_space=pltpu.VMEM),
            pl.BlockSpec((3, KNOT, width_y, width_z), lambda i: (0, i, 0, 0)),
            pl.BlockSpec((KNOT, width_y, width_z), lambda i: (i, 0, 0)),
            node_spec,
            node_spec,
        ],
        out_specs=[
            pl.BlockSpec((KNOT, width_y, width_z), lambda i: (i, 0, 0)),
            node_spec,
            node_spec,
            node_spec,
            pl.BlockSpec((1, ROWS, LANES), lambda i: (i, 0, 0)),
        ],
        out_shape=[
            jax.ShapeDtypeStruct(image.shape, jnp.bfloat16),
            block_sum,
            block_sum,
            block_sum,
            jax.ShapeDtypeStruct((nodes, ROWS, LANES), f32),
        ],
        scratch_shapes=[pltpu.VMEM((KNOT + 2, 9, width_y, width_z), f32)],
        compiler_params=pltpu.CompilerParams(
            dimension_semantics=("arbitrary",), vmem_limit_bytes=60 * 1024 * 1024),
    )(dpad, displacement, image, contrast_y, bright_y)


def node_sums(field):
    nodes, width_y, width_z = field.shape
    return field.reshape(nodes, width_y // KNOT, KNOT, width_z).sum(axis=2)


def local(reference_image, deformed, displacement, plane_factors, depth_factors):
    dpad = padded_deformed(deformed)
    fields = jnp.einsum("krij,krz->kijz", plane_factors, depth_factors, precision=highest)
    fields = jnp.repeat(fields, KNOT, axis=2)
    residual, prod, mis, sq, energy_parts = strip_sums(
        dpad, displacement, reference_image, fields[0], fields[1])
    prod, mis, sq = node_sums(prod), node_sums(mis), node_sums(sq)
    local_energy = jnp.sum(energy_parts)

    first, second = plane_factors[0], plane_factors[1]
    grad_depth = -jnp.stack([
        jnp.einsum("rij,ijz->rz", first, prod, precision=highest),
        jnp.einsum("rij,ijz->rz", second, mis, precision=highest)])
    first_depth = jnp.einsum("rij,ijz->rz", first * first, sq, precision=highest)
    level_sum = KNOT * KNOT * jnp.sum(second * second, axis=(1, 2))
    grad_plane = -jnp.stack([
        jnp.einsum("rz,ijz->rij", depth_factors[0], prod, precision=highest),
        jnp.einsum("rz,ijz->rij", depth_factors[1], mis, precision=highest)])
    first_diag = jnp.einsum("rz,ijz->rij", depth_factors[0] * depth_factors[0], sq, precision=highest)
    depth_level = KNOT * KNOT * jnp.sum(depth_factors[1] * depth_factors[1], axis=1)

    grad_plane, first_diag, depth_level, row_energy = lax.psum(
        (grad_plane, first_diag, depth_level, local_energy), "gz")
    grad_depth, first_depth, level_sum, energy = lax.psum(
        (grad_depth, first_depth, level_sum, row_energy), "gy")

    nodes_x = plane_factors.shape[2]
    nodes_y = plane_factors.shape[3] * lax.axis_size("gy")
    full_z = depth_factors.shape[2] * lax.axis_size("gz")
    diag_plane = jnp.stack(
        [first_diag, jnp.broadcast_to(depth_level[:, None, None], first_diag.shape)])
    lam_plane = damping * RANK * energy / (nodes_x * nodes_y)
    lam_depth = damping * energy / full_z
    step_plane = -grad_plane / (diag_plane + lam_plane + epsilon)
    diag_depth = jnp.stack([first_depth, jnp.broadcast_to(level_sum[:, None], first_depth.shape)])
    step_depth = -grad_depth / (diag_depth + lam_depth + epsilon)
    return (residual, step_plane, step_depth)


def solution(mesh):
    placed = (
        P(None, "gy", "gz"),
        P(None, "gy", "gz"),
        P(None, None, "gy", "gz"),
        P(None, None, None, "gy"),
        P(None, None, "gz"),
    )
    return jax.shard_map(
        local,
        mesh=mesh,
        in_specs=placed,
        out_specs=(P(None, "gy", "gz"), P(None, None, None, "gy"), P(None, None, "gz")),
        check_vma=False,
    )
```

time: 621 us -> 310 us (0.50); the launches traced: 612 us -> 308 us
  other arithmetic: 175 us -> 15.9 us
  local copies, waits for them, and re-layouts: 106 us -> 5.5 us
  matrix products: 70.3 us -> 3.43 us
  blocking collectives: 133 us -> 71.8 us
  Pallas kernels: 0 us -> 50.6 us
  waiting for transfers between devices: 100 us -> 134 us
    add x1 -> x0, other arithmetic: 119 us -> none  [warp_image(): summed = summed + weight_x[along_x] * weight_y[along_y] * partial_z]
    dot_general x8 -> x7, matrix products: 70.3 us -> 3.43 us  [the longest x1 1.3 us: local(): jnp.einsum('krij,krz->kijz', plane_factors, depth_factors, precision=high...]
    psum x3 -> x2, blocking collectives: 133 us -> 71.8 us  [the longest x1 41.8 us: local(): lax.psum((grad_depth, first_depth, level_sum, row_energy), 'gy')]
    unnamed x24 -> x10, local copies, waits for them, and re-layouts: 52.3 us -> 0.03 us
    pallas_call x0 -> x1, Pallas kernels: none -> 50.6 us  [strip_sums(): pl.pallas_call(strip_kernel, grid=(nodes,), in_specs=[pl.BlockSpec(memory...]
    concatenate x2 -> x1, other arithmetic: 48.1 us -> 7.21 us  [padded_deformed(): return jnp.concatenate([rimmed, high_z, gap_z, low_z], axis=2)]
    psum x1, waiting for transfers between devices: 100 us -> 134 us  [local(): lax.psum((grad_depth, first_depth, level_sum, row_energy), 'gy')]
    ppermute x2, local copies, waits for them, and re-layouts: 25.3 us -> 1.13 us  [neighbours(): return lax.ppermute(part, axis, pairs)]
  transfers between devices with their start and end apart: 5 -> 5, of which waited for: 1 -> 2; matrix products, arithmetic and copies ran while one was open for 16% -> 2% of each run, Pallas kernels for 0% -> 0%
where the time goes in v1:
time: 310 us; the launch traced here: 308 us
  waiting for transfers between devices  134 us (43%)
  blocking collectives  71.8 us (23%)
  Pallas kernels  50.6 us (16%)
  other arithmetic  15.9 us (5%)
  between operations  15.6 us (5%)
  starting transfers between devices  11.7 us (4%)
  local copies, waits for them, and re-layouts  5.5 us (2%)
  matrix products  3.43 us (1%)
    psum x1, waiting for transfers between devices, local(): lax.psum((grad_depth, first_depth, level_sum, row_energy), 'gy')  134 us
    pallas_call x1, Pallas kernels, strip_sums(): pl.pallas_call(strip_kernel, grid=(nodes,), in_specs=[pl.BlockSpec(memory...  50.6 us
    psum x1, blocking collectives, local(): lax.psum((grad_depth, first_depth, level_sum, row_energy), 'gy')  41.8 us
    psum x1, blocking collectives, local(): lax.psum((grad_plane, first_diag, depth_level, local_energy), 'gz')  30 us
    ppermute x4, starting transfers between devices, neighbours(): return lax.ppermute(part, axis, pairs)  11.7 us
    concatenate x1, other arithmetic, padded_deformed(): return jnp.concatenate([rimmed, high_z, gap_z, low_z], axis=2)  7.21 us
  transfers between devices with their start and end apart: 5, of which 2 were waited for; matrix products, arithmetic and copies ran while one was open for 2% of the time, Pallas kernels for 0%

profile of v1, /device:TPU:1, one launch (start us, length us, event | category | flops | bytes accessed | tf_op | source)
XLA Modules:
  0.0 308.5 jit_solution(15794673505721768607)
XLA Ops:
  7.2 1.6 fusion.19
  8.8 3.3 %collective-permute-start = (bf16[64,1,512]{2,1,0:T(2,128)(2,1)S(1)}, bf16[64,1,512]{2,1,0:T(2,128)(2,1)S(1)}, u32[]{:S(2)}, u32[]{:S(2)}) collective-permute-start(bf16[64,1,512]{2,1,0:T(2,128)(2,1)S(1)} %get-tuple-element.23), channel_id=1, source_target_pairs={{8,0},{16,8},{24,16},{32,24},{40,32},{48,40},{56,48},{64,56},{72,6... | collective-permute-start | bytes 196616 | tf_op jit(solution)/shard_map/ppermute | solution.py:25
  12.1 3.1 %collective-permute-start.1 = (bf16[64,1,512]{2,1,0:T(2,128)(2,1)S(1)}, bf16[64,1,512]{2,1,0:T(2,128)(2,1)S(1)}, u32[]{:S(2)}, u32[]{:S(2)}) collective-permute-start(bf16[64,1,512]{2,1,0:T(2,128)(2,1)S(1)} %get-tuple-element.24), channel_id=1, source_target_pairs={{0,8},{8,16},{16,24},{24,32},{32,40},{40,48},{48,56},{56,64},{64,7... | collective-permute-start | bytes 196616 | tf_op jit(solution)/shard_map/ppermute | solution.py:25
  15.2 1.0 fusion.8
  16.2 1.3 fusion.2
  17.5 1.6 broadcast_bitcast_fusion
  19.2 0.8 pad_maximum_fusion.4
  20.1 0.5 copy.8
  20.5 1.3 collective-permute-start.2
  21.8 0.5 copy.9
  22.3 4.0 %collective-permute-start.3 = (bf16[64,72,1]{1,0,2:T(8,128)(2,1)S(1)}, bf16[64,72,1]{1,0,2:T(8,128)(2,1)S(1)}, u32[]{:S(2)}, u32[]{:S(2)}) collective-permute-start(bf16[64,72,1]{1,0,2:T(8,128)(2,1)S(1)} %copy.9), channel_id=1, source_target_pairs={{0,1},{1,2},{2,3},{3,4},{4,5},{5,6},{6,7},{8,9},{9,10},{10,11},{11... | collective-permute-start | bytes 27656 | tf_op jit(solution)/shard_map/ppermute | solution.py:25
  26.4 0.6 copy.10
  27.0 0.2 collective-permute-done.3
  27.2 0.6 copy.11
  27.7 7.2 %pad_maximum_fusion.dpad_ref = bf16[64,72,640]{2,1,0:T(8,128)(2,1)} fusion(bf16[64,72,1]{2,1,0:T(8,128)(2,1)S(1)} %copy.11, bf16[64,72,1]{2,1,0:T(8,128)(2,1)S(1)} %copy.10, bf16[64,1,512]{2,1,0:T(2,128)(2,1)S(1)} %collective-permute-done.1, bf16[64,6,512]{2,1,0:T(8,128)(2,1)S(1)} %broadcast_in_dim.17, bf16[64,1,512]{2,1,0:T(2,128)(2,1)S(1)} %collective-permute-done, ...), kind=kLoop, calls=%fused_computation | loop fusion | flops 41287680 | bytes 10636544 | tf_op jit(solution)/shard_map/concatenate | solution.py:37
  34.9 50.6 %shard_map.76 = (bf16[64,64,512]{2,1,0:T(8,128)(2,1)}, f32[8,64,512]{2,1,0:T(8,128)}, f32[8,64,512]{2,1,0:T(8,128)}, f32[8,64,512]{2,1,0:T(8,128)}, f32[8,16,256]{2,1,0:T(8,128)}) custom-call(bf16[64,72,640]{2,1,0:T(8,128)(2,1)} %pad_maximum_fusion.dpad_ref, bf16[3,64,64,512]{3,2,1,0:T(8,128)(2,1)} %disp_ref.1, bf16[64,64,512]{2,1,0:T(8,128)(2,1)} %image_ref.1, ...), custom_call_target="tpu_custom_call" | custom-call | tf_op jit(solution)/shard_map/pallas_call | solution.py:132
  85.6 1.6 bitcast_reduce_fusion.1
  87.1 0.3 convolution_bitcast_fusion.1
  87.4 0.3 convolution_bitcast_fusion.4
  87.7 1.5 bitcast_reduce_fusion.2
  89.2 0.3 convolution_bitcast_fusion.2
  89.4 0.2 convolution_bitcast_fusion.5
  89.7 0.3 bitcast_reduce_fusion
  90.0 0.9 convolution_bitcast_fusion
  90.8 0.2 convolution_bitcast_fusion.3
  91.1 0.6 reduce_sum.58
  91.8 30.0 %all-reduce.2 = (f32[32]{0:T(128)S(1)}, f32[1,32,8,8]{1,3,2,0:T(8,128)S(1)}, f32[2,32,8,8]{1,3,2,0:T(8,128)S(1)}, f32[]{:T(128)}) all-reduce(f32[32]{0:T(128)S(1)} %broadcast_multiply_fusion.1, f32[1,32,8,8]{1,3,2,0:T(8,128)S(1)} %convolution_bitcast_fusion.3, ...), channel_id=1, replica_groups=mesh['gy'=16,'gz'=8] {'gz'}, use_global_device_ids=true, to_apply=%region_6.0 | all-reduce | flops 6177 | bytes 49416 | tf_op jit(solution)/shard_map/psum | solution.py:188
  121.7 41.8 %all-reduce = (f32[]{:T(128)}, f32[32]{0:T(128)S(1)}) all-reduce(f32[]{:T(128)} %get-tuple-element.20, f32[32]{0:T(128)S(1)} %broadcast_multiply_fusion), channel_id=1, replica_groups=mesh['gy'=16,'gz'=8] {'gy'}, use_global_device_ids=true, to_apply=%region_9.0 | all-reduce | flops 33 | bytes 264 | tf_op jit(solution)/shard_map/psum | solution.py:190
  164.8 0.7 maximum_negate_fusion
  165.5 0.7 fusion.5
  166.2 133.7 %all-reduce.5.cloned.1.call-done = (f32[1,32,512]{2,1,0:T(8,128)}, f32[2,32,512]{2,1,0:T(8,128)}) async-done(((f32[1,32,512]{2,1,0:T(8,128)}, f32[2,32,512]{2,1,0:T(8,128)}), (f32[1,32,512]{2,1,0:T(8,128)}, f32[2,32,512]{2,1,0:T(8,128)})) %all-reduce.5.cloned.1.call-update) | async-done | bytes 196624 | tf_op jit(solution)/shard_map/psum | solution.py:190
  300.0 1.6 fusion.1
  (25 shorter events, 0.3 us)
Async XLA Ops:
  7.2 12.0 %copy-start.3 = (f32[2,32,8,8]{1,3,2,0:T(8,128)S(1)}, f32[2,32,8,8]{1,3,2,0:T(8,128)}, u32[]{:S(2)}) copy-start(f32[2,32,8,8]{1,3,2,0:T(8,128)} %param.8) | copy-start | bytes 49156
  7.2 292.7 %all-reduce.5.cloned.1.call-start = ((), (), s32[]{:S(2)}) async-start(), calls=%async_computation | async-start | bytes 393216 | tf_op jit(solution)/shard_map/psum | solution.py:190
  7.2 12.0 %copy-start = (bf16[64,64,512]{2,1,0:T(8,128)(2,1)S(1)}, bf16[64,64,512]{2,1,0:T(8,128)(2,1)}, u32[]{:S(2)}) copy-start(bf16[64,64,512]{2,1,0:T(8,128)(2,1)} %param.6) | copy-start | bytes 12582916
  8.8 10.4 %collective-permute-start = (bf16[64,1,512]{2,1,0:T(2,128)(2,1)S(1)}, bf16[64,1,512]{2,1,0:T(2,128)(2,1)S(1)}, u32[]{:S(2)}, u32[]{:S(2)}) collective-permute-start(bf16[64,1,512]{2,1,0:T(2,128)(2,1)S(1)} %get-tuple-element.23), channel_id=1, source_target_pairs={{8,0},{16,8},{24,16},{32,24},{40,32},{48,40},{56,48},{64,56},{72,6... | collective-permute-start | bytes 196616 | tf_op jit(solution)/shard_map/ppermute | solution.py:25
  12.1 7.0 %collective-permute-start.1 = (bf16[64,1,512]{2,1,0:T(2,128)(2,1)S(1)}, bf16[64,1,512]{2,1,0:T(2,128)(2,1)S(1)}, u32[]{:S(2)}, u32[]{:S(2)}) collective-permute-start(bf16[64,1,512]{2,1,0:T(2,128)(2,1)S(1)} %get-tuple-element.24), channel_id=1, source_target_pairs={{0,8},{8,16},{16,24},{24,32},{32,40},{40,48},{48,56},{56,64},{64,7... | collective-permute-start | bytes 196616 | tf_op jit(solution)/shard_map/ppermute | solution.py:25
  20.5 5.9 %collective-permute-start.2 = (bf16[64,72,1]{1,0,2:T(8,128)(2,1)S(1)}, bf16[64,72,1]{1,0,2:T(8,128)(2,1)S(1)}, u32[]{:S(2)}, u32[]{:S(2)}) collective-permute-start(bf16[64,72,1]{1,0,2:T(8,128)(2,1)S(1)} %copy.8), channel_id=1, source_target_pairs={{1,0},{2,1},{3,2},{4,3},{5,4},{6,5},{7,6},{9,8},{10,9},{11,10},{12... | collective-permute-start | bytes 27656 | tf_op jit(solution)/shard_map/ppermute | solution.py:25
  22.3 4.8 %collective-permute-start.3 = (bf16[64,72,1]{1,0,2:T(8,128)(2,1)S(1)}, bf16[64,72,1]{1,0,2:T(8,128)(2,1)S(1)}, u32[]{:S(2)}, u32[]{:S(2)}) collective-permute-start(bf16[64,72,1]{1,0,2:T(8,128)(2,1)S(1)} %copy.9), channel_id=1, source_target_pairs={{0,1},{1,2},{2,3},{3,4},{4,5},{5,6},{6,7},{8,9},{9,10},{10,11},{11... | collective-permute-start | bytes 27656 | tf_op jit(solution)/shard_map/ppermute | solution.py:25
  34.9 52.5 %copy-start.1 = (f32[2,32,512]{2,1,0:T(8,128)S(1)}, f32[2,32,512]{2,1,0:T(8,128)}, u32[]{:S(2)}) copy-start(f32[2,32,512]{2,1,0:T(8,128)} %param.9) | copy-start | bytes 393220
  85.5 4.1 %copy-start.2 = (f32[8,64,512]{2,1,0:T(8,128)S(1)}, f32[8,64,512]{2,1,0:T(8,128)}, u32[]{:S(2)}) copy-start(f32[8,64,512]{2,1,0:T(8,128)} %get-tuple-element.11) | copy-start | bytes 3145732
  85.6 5.6 %copy-start.4 = (f32[8,16,256]{2,1,0:T(8,128)S(1)}, f32[8,16,256]{2,1,0:T(8,128)}, u32[]{:S(2)}) copy-start(f32[8,16,256]{2,1,0:T(8,128)} %get-tuple-element.12) | copy-start | bytes 393220
Sparse Core Ops, SparseCore 0:
  165.7 134.2 all-reduce.4

commit v2 on v1

--- a/solution.py
+++ b/solution.py
@@ -1,3 +1,5 @@
+import functools
+
 import jax
 import jax.numpy as jnp
 from jax import lax
@@ -164,6 +166,92 @@
     return field.reshape(nodes, width_y // KNOT, KNOT, width_z).sum(axis=2)
 
 
+def gather_sum_kernel(axis, n, part_ref, out_ref, landed, summed, gathered,
+                      send_one, recv_one, send_two, recv_two):
+    me = lax.axis_index(axis)
+    barrier = pltpu.get_barrier_semaphore()
+    for d in range(1, n):
+        pl.semaphore_signal(barrier, inc=1, device_id={axis: lax.rem(me + d, n)},
+                            device_id_type=pl.DeviceIdType.MESH)
+    pl.semaphore_wait(barrier, n - 1)
+
+    def scatter(d):
+        target = lax.rem(me + d, n)
+        return pltpu.make_async_remote_copy(
+            src_ref=part_ref.at[target], dst_ref=landed.at[me],
+            send_sem=send_one.at[target], recv_sem=recv_one.at[me],
+            device_id={axis: target}, device_id_type=pl.DeviceIdType.MESH)
+
+    def arrival(d, buffer, sem, source_ref):
+        source = lax.rem(me + n - d, n)
+        return pltpu.make_async_remote_copy(
+            src_ref=source_ref, dst_ref=buffer.at[source],
+            send_sem=sem.at[source], recv_sem=sem.at[source],
+            device_id={axis: source}, device_id_type=pl.DeviceIdType.MESH)
+
+    outgoing = [scatter(d) for d in range(1, n)]
+    for copy in outgoing:
+        copy.start()
+    total = part_ref[me]
+    for d in range(1, n):
+        arrival(d, landed, recv_one, part_ref.at[0]).wait_recv()
+        total = total + landed[lax.rem(me + n - d, n)]
+    summed[...] = total
+    for copy in outgoing:
+        copy.wait_send()
+
+    def gather(d):
+        target = lax.rem(me + d, n)
+        return pltpu.make_async_remote_copy(
+            src_ref=summed, dst_ref=gathered.at[me],
+            send_sem=send_two.at[target], recv_sem=recv_two.at[me],
+            device_id={axis: target}, device_id_type=pl.DeviceIdType.MESH)
+
+    outgoing = [gather(d) for d in range(1, n)]
+    for copy in outgoing:
+        copy.start()
+    out_ref[me] = total
+    for d in range(1, n):
+        arrival(d, gathered, recv_two, summed).wait_recv()
+        source = lax.rem(me + n - d, n)
+        out_ref[source] = gathered[source]
+    for copy in outgoing:
+        copy.wait_send()
+
+
+def gather_sum(parts, axis, tag):
+    n = lax.axis_size(axis)
+    chunk = parts.shape[1:]
+    return pl.pallas_call(
+        functools.partial(gather_sum_kernel, axis, n),
+        out_shape=jax.ShapeDtypeStruct(parts.shape, parts.dtype),
+        in_specs=[pl.BlockSpec(memory_space=pltpu.VMEM)],
+        out_specs=pl.BlockSpec(memory_space=pltpu.VMEM),
+        scratch_shapes=[
+            pltpu.VMEM(parts.shape, parts.dtype),
+            pltpu.VMEM(chunk, parts.dtype),
+            pltpu.VMEM(parts.shape, parts.dtype),
+            pltpu.SemaphoreType.DMA((n,)),
+            pltpu.SemaphoreType.DMA((n,)),
+            pltpu.SemaphoreType.DMA((n,)),
+            pltpu.SemaphoreType.DMA((n,)),
+        ],
+        compiler_params=pltpu.CompilerParams(collective_id=tag, has_side_effects=True),
+    )(parts)
+
+
+def all_sum(main, extras, axis, tag):
+    n = lax.axis_size(axis)
+    rows = -(-main.shape[0] // (n * 128))
+    main = jnp.pad(main, (0, n * rows * 128 - main.shape[0])).reshape(n, rows, 128)
+    tail = jnp.pad(extras, (0, 128 - extras.shape[0]))
+    tail = jnp.broadcast_to(tail, (n, 1, 128))
+    spare = -(-(rows + 1) // 8) * 8 - rows - 1
+    parts = jnp.concatenate([main, tail, jnp.zeros((n, spare, 128), main.dtype)], axis=1)
+    summed = gather_sum(parts, axis, tag)
+    return summed[:, :rows].reshape(-1), summed[0, rows]
+
+
 def local(reference_image, deformed, displacement, plane_factors, depth_factors):
     dpad = padded_deformed(deformed)
     fields = jnp.einsum("krij,krz->kijz", plane_factors, depth_factors, precision=highest)
@@ -185,10 +273,18 @@
     first_diag = jnp.einsum("rz,ijz->rij", depth_factors[0] * depth_factors[0], sq, precision=highest)
     depth_level = KNOT * KNOT * jnp.sum(depth_factors[1] * depth_factors[1], axis=1)
 
-    grad_plane, first_diag, depth_level, row_energy = lax.psum(
-        (grad_plane, first_diag, depth_level, local_energy), "gz")
-    grad_depth, first_depth, level_sum, energy = lax.psum(
-        (grad_depth, first_depth, level_sum, row_energy), "gy")
+    plane_terms = jnp.concatenate([grad_plane.reshape(-1), first_diag.reshape(-1)])
+    plane_terms, plane_extra = all_sum(
+        plane_terms, jnp.concatenate([depth_level, local_energy[None]]), "gz", 1)
+    grad_plane = plane_terms[: grad_plane.size].reshape(grad_plane.shape)
+    first_diag = plane_terms[grad_plane.size : grad_plane.size + first_diag.size].reshape(first_diag.shape)
+    depth_level, row_energy = plane_extra[:RANK], plane_extra[RANK]
+    depth_terms = jnp.concatenate([grad_depth.reshape(-1), first_depth.reshape(-1)])
+    depth_terms, depth_extra = all_sum(
+        depth_terms, jnp.concatenate([level_sum, row_energy[None]]), "gy", 2)
+    grad_depth = depth_terms[: grad_depth.size].reshape(grad_depth.shape)
+    first_depth = depth_terms[grad_depth.size : grad_depth.size + first_depth.size].reshape(first_depth.shape)
+    level_sum, energy = depth_extra[:RANK], depth_extra[RANK]
 
     nodes_x = plane_factors.shape[2]
     nodes_y = plane_factors.shape[3] * lax.axis_size("gy")

time: 310 us -> 137 us (0.44)
  waiting for transfers between devices: 134 us -> 0.04 us
  blocking collectives: 71.8 us -> 0 us
  Pallas kernels: 50.6 us -> 90.5 us
  between operations: 15.6 us -> 2.28 us
  local copies, waits for them, and re-layouts: 5.5 us -> 11.6 us
    psum x1 -> x0, waiting for transfers between devices: 134 us -> none  [local(): lax.psum((grad_depth, first_depth, level_sum, row_energy), 'gy')]
    psum x2 -> x0, blocking collectives: 71.8 us -> none  [the longest x1 41.8 us: local(): lax.psum((grad_depth, first_depth, level_sum, row_energy), 'gy')]
    pallas_call x0 -> x2, Pallas kernels: none -> 39.8 us  [gather_sum(): pl.pallas_call(functools.partial(gather_sum_kernel, axis, n), out_shape=j...]
    slice x0 -> x7, local copies, waits for them, and re-layouts: none -> 3.8 us  [the longest x1 1.33 us: local(): depth_level, row_energy = (plane_extra[:RANK], plane_extra[RANK])]
  transfers between devices with their start and end apart: 5 -> 4, of which waited for: 2 -> 0; matrix products, arithmetic and copies ran while one was open for 2% -> 4% of each run, Pallas kernels for 0% -> 0%
where the time goes in v2:
time: 137 us; the launch traced here: 136 us
  Pallas kernels  90.5 us (66%)
  other arithmetic  17.4 us (13%)
  starting transfers between devices  11.7 us (9%)
  local copies, waits for them, and re-layouts  11.6 us (8%)
  matrix products  2.81 us (2%)
  between operations  2.28 us (2%)
    pallas_call x1, Pallas kernels, strip_sums(): pl.pallas_call(strip_kernel, grid=(nodes,), in_specs=[pl.BlockSpec(memory...  50.6 us
    pallas_call x2, Pallas kernels, gather_sum(): pl.pallas_call(functools.partial(gather_sum_kernel, axis, n), out_shape=j...  39.8 us
    ppermute x4, starting transfers between devices, neighbours(): return lax.ppermute(part, axis, pairs)  11.7 us
    concatenate x1, other arithmetic, padded_deformed(): return jnp.concatenate([rimmed, high_z, gap_z, low_z], axis=2)  7.21 us
    reduce_sum x3, other arithmetic, node_sums(): return field.reshape(nodes, width_y // KNOT, KNOT, width_z).sum(axis=2)  3.31 us
  transfers between devices with their start and end apart: 4, of which 0 were waited for; matrix products, arithmetic and copies ran while one was open for 4% of the time, Pallas kernels for 0%

profile of v2, /device:TPU:1, one launch (start us, length us, event | category | flops | bytes accessed | tf_op | source)
XLA Modules:
  0.0 136.3 jit_solution(15527886981284526589)
XLA Ops:
  0.6 1.6 %fusion.20 = (bf16[64,1,512]{2,1,0:T(2,128)(2,1)S(1)}, bf16[64,1,512]{2,1,0:T(2,128)(2,1)S(1)}) fusion(bf16[64,64,512]{2,1,0:T(8,128)(2,1)} %param.6), kind=kLoop, calls=%fused_computation.57 | loop fusion | bytes 262144 | tf_op jit(solution)/shard_map/slice | solution.py:33
  2.2 3.3 %collective-permute-start = (bf16[64,1,512]{2,1,0:T(2,128)(2,1)S(1)}, bf16[64,1,512]{2,1,0:T(2,128)(2,1)S(1)}, u32[]{:S(2)}, u32[]{:S(2)}) collective-permute-start(bf16[64,1,512]{2,1,0:T(2,128)(2,1)S(1)} %get-tuple-element.24), channel_id=1, source_target_pairs={{8,0},{16,8},{24,16},{32,24},{40,32},{48,40},{56,48},{64,56},{72,6... | collective-permute-start | bytes 196616 | tf_op jit(solution)/shard_map/ppermute | solution.py:27
  5.5 3.1 %collective-permute-start.1 = (bf16[64,1,512]{2,1,0:T(2,128)(2,1)S(1)}, bf16[64,1,512]{2,1,0:T(2,128)(2,1)S(1)}, u32[]{:S(2)}, u32[]{:S(2)}) collective-permute-start(bf16[64,1,512]{2,1,0:T(2,128)(2,1)S(1)} %get-tuple-element.25), channel_id=1, source_target_pairs={{0,8},{8,16},{16,24},{24,32},{32,40},{40,48},{48,56},{56,64},{64,7... | collective-permute-start | bytes 196616 | tf_op jit(solution)/shard_map/ppermute | solution.py:27
  8.7 1.0 fusion.9
  9.6 1.3 fusion.4
  10.9 1.6 %broadcast_bitcast_fusion = (f32[8,64,512]{2,1,0:T(8,128)}, f32[8,64,512]{2,1,0:T(8,128)}) fusion(f32[8,8,512]{2,1,0:T(8,128)S(1)} %get-tuple-element.26, f32[8,8,512]{2,1,0:T(8,128)S(1)} %get-tuple-element.27), kind=kLoop, calls=%fused_computation.13 | loop fusion | bytes 2359296 | tf_op jit(solution)/shard_map/broadcast_in_dim | solution.py:258
  12.5 0.8 fusion.15
  13.4 0.8 pad_maximum_fusion.4
  14.2 0.5 copy.22
  14.7 1.3 collective-permute-start.2
  16.0 0.5 copy.23
  16.5 4.0 %collective-permute-start.3 = (bf16[64,72,1]{1,0,2:T(8,128)(2,1)S(1)}, bf16[64,72,1]{1,0,2:T(8,128)(2,1)S(1)}, u32[]{:S(2)}, u32[]{:S(2)}) collective-permute-start(bf16[64,72,1]{1,0,2:T(8,128)(2,1)S(1)} %copy.23), channel_id=1, source_target_pairs={{0,1},{1,2},{2,3},{3,4},{4,5},{5,6},{6,7},{8,9},{9,10},{10,11},{11... | collective-permute-start | bytes 27656 | tf_op jit(solution)/shard_map/ppermute | solution.py:27
  20.7 0.6 copy.24
  21.3 0.6 copy.25
  21.9 7.2 %pad_maximum_fusion.dpad_ref = bf16[64,72,640]{2,1,0:T(8,128)(2,1)} fusion(bf16[64,72,1]{2,1,0:T(8,128)(2,1)S(1)} %copy.25, bf16[64,72,1]{2,1,0:T(8,128)(2,1)S(1)} %copy.24, bf16[64,1,512]{2,1,0:T(2,128)(2,1)S(1)} %collective-permute-done.1, bf16[64,6,512]{2,1,0:T(8,128)(2,1)S(1)} %broadcast_in_dim.32, bf16[64,1,512]{2,1,0:T(2,128)(2,1)S(1)} %collective-permute-done, ...), kind=kLoop, calls=%fused_computation | loop fusion | flops 41287680 | bytes 10636544 | tf_op jit(solution)/shard_map/concatenate | solution.py:39
  29.1 50.6 %shard_map.76 = (bf16[64,64,512]{2,1,0:T(8,128)(2,1)}, f32[8,64,512]{2,1,0:T(8,128)}, f32[8,64,512]{2,1,0:T(8,128)}, f32[8,64,512]{2,1,0:T(8,128)}, f32[8,16,256]{2,1,0:T(8,128)}) custom-call(bf16[64,72,640]{2,1,0:T(8,128)(2,1)} %pad_maximum_fusion.dpad_ref, bf16[3,64,64,512]{3,2,1,0:T(8,128)(2,1)} %disp_ref.1, bf16[64,64,512]{2,1,0:T(8,128)(2,1)} %image_ref.1, ...), custom_call_target="tpu_custom_call" | custom-call | tf_op jit(solution)/shard_map/pallas_call | solution.py:134
  79.8 1.6 %bitcast_reduce_fusion.1 = f32[8,8,512]{2,1,0:T(8,128)S(1)} fusion(f32[8,64,512]{2,1,0:T(8,128)} %get-tuple-element.10), kind=kLoop, calls=%fused_computation.11 | loop fusion | flops 229376 | bytes 1179648 | tf_op jit(solution)/shard_map/reduce_sum | solution.py:166
  81.9 1.5 %bitcast_reduce_fusion.2 = f32[8,8,512]{2,1,0:T(8,128)S(1)} fusion(f32[8,64,512]{2,1,0:T(8,128)} %get-tuple-element.9), kind=kLoop, calls=%fused_computation.12 | loop fusion | flops 229376 | bytes 1179648 | tf_op jit(solution)/shard_map/reduce_sum | solution.py:166
  84.4 0.3 convolution_bitcast_fusion
  85.3 0.6 reduce_sum.58
  85.9 0.7 select_maximum_fusion.1
  86.6 0.7 maximum_maximum_fusion.1.part_ref
  87.3 14.9 %shard_map.77 = f32[8,8,128]{2,1,0:T(8,128)} custom-call(f32[8,8,128]{2,1,0:T(8,128)} %maximum_maximum_fusion.1.part_ref), custom_call_target="tpu_custom_call" | custom-call | tf_op jit(solution)/shard_map/pallas_call | solution.py:225
  102.2 1.3 slice.109
  103.7 0.7 select_maximum_fusion
  104.4 0.8 maximum_maximum_fusion.part_ref
  105.2 24.9 %shard_map.78 = f32[16,32,128]{2,1,0:T(8,128)} custom-call(f32[16,32,128]{2,1,0:T(8,128)} %maximum_maximum_fusion.part_ref), custom_call_target="tpu_custom_call" | custom-call | tf_op jit(solution)/shard_map/pallas_call | solution.py:225
  130.1 0.9 slice.112
  131.1 0.7 slice_bitcast_fusion.2
  131.8 1.3 slice.111
  134.8 0.8 copy.28
  135.6 0.7 fusion.2
  (52 shorter events, 3.0 us)
Async XLA Ops:
  0.6 12.7 %copy-start = (bf16[64,64,512]{2,1,0:T(8,128)(2,1)S(1)}, bf16[64,64,512]{2,1,0:T(8,128)(2,1)}, u32[]{:S(2)}) copy-start(bf16[64,64,512]{2,1,0:T(8,128)(2,1)} %param.6) | copy-start | bytes 12582916
  2.2 11.1 %collective-permute-start = (bf16[64,1,512]{2,1,0:T(2,128)(2,1)S(1)}, bf16[64,1,512]{2,1,0:T(2,128)(2,1)S(1)}, u32[]{:S(2)}, u32[]{:S(2)}) collective-permute-start(bf16[64,1,512]{2,1,0:T(2,128)(2,1)S(1)} %get-tuple-element.24), channel_id=1, source_target_pairs={{8,0},{16,8},{24,16},{32,24},{40,32},{48,40},{56,48},{64,56},{72,6... | collective-permute-start | bytes 196616 | tf_op jit(solution)/shard_map/ppermute | solution.py:27
  5.5 7.8 %collective-permute-start.1 = (bf16[64,1,512]{2,1,0:T(2,128)(2,1)S(1)}, bf16[64,1,512]{2,1,0:T(2,128)(2,1)S(1)}, u32[]{:S(2)}, u32[]{:S(2)}) collective-permute-start(bf16[64,1,512]{2,1,0:T(2,128)(2,1)S(1)} %get-tuple-element.25), channel_id=1, source_target_pairs={{0,8},{8,16},{16,24},{24,32},{32,40},{40,48},{48,56},{56,64},{64,7... | collective-permute-start | bytes 196616 | tf_op jit(solution)/shard_map/ppermute | solution.py:27
  14.7 6.0 %collective-permute-start.2 = (bf16[64,72,1]{1,0,2:T(8,128)(2,1)S(1)}, bf16[64,72,1]{1,0,2:T(8,128)(2,1)S(1)}, u32[]{:S(2)}, u32[]{:S(2)}) collective-permute-start(bf16[64,72,1]{1,0,2:T(8,128)(2,1)S(1)} %copy.22), channel_id=1, source_target_pairs={{1,0},{2,1},{3,2},{4,3},{5,4},{6,5},{7,6},{9,8},{10,9},{11,10},{12... | collective-permute-start | bytes 27656 | tf_op jit(solution)/shard_map/ppermute | solution.py:27
  16.5 4.8 %collective-permute-start.3 = (bf16[64,72,1]{1,0,2:T(8,128)(2,1)S(1)}, bf16[64,72,1]{1,0,2:T(8,128)(2,1)S(1)}, u32[]{:S(2)}, u32[]{:S(2)}) collective-permute-start(bf16[64,72,1]{1,0,2:T(8,128)(2,1)S(1)} %copy.23), channel_id=1, source_target_pairs={{0,1},{1,2},{2,3},{3,4},{4,5},{5,6},{6,7},{8,9},{9,10},{10,11},{11... | collective-permute-start | bytes 27656 | tf_op jit(solution)/shard_map/ppermute | solution.py:27
  29.1 52.2 %copy-start.1 = (f32[2,32,512]{2,1,0:T(8,128)S(1)}, f32[2,32,512]{2,1,0:T(8,128)}, u32[]{:S(2)}) copy-start(f32[2,32,512]{2,1,0:T(8,128)} %param.9) | copy-start | bytes 393220
  29.1 52.5 %copy-start.3 = (f32[2,32,8,8]{1,3,2,0:T(8,128)S(1)}, f32[2,32,8,8]{1,3,2,0:T(8,128)}, u32[]{:S(2)}) copy-start(f32[2,32,8,8]{1,3,2,0:T(8,128)} %param.8) | copy-start | bytes 49156
  79.7 4.1 %copy-start.2 = (f32[8,64,512]{2,1,0:T(8,128)S(1)}, f32[8,64,512]{2,1,0:T(8,128)}, u32[]{:S(2)}) copy-start(f32[8,64,512]{2,1,0:T(8,128)} %get-tuple-element.11) | copy-start | bytes 3145732
  81.6 3.6 %copy-start.4 = (f32[8,16,256]{2,1,0:T(8,128)S(1)}, f32[8,16,256]{2,1,0:T(8,128)}, u32[]{:S(2)}) copy-start(f32[8,16,256]{2,1,0:T(8,128)} %get-tuple-element.12) | copy-start | bytes 393220
  102.2 30.8 %copy-start.5 = (f32[8,8,128]{2,1,0:T(8,128)S(1)}, f32[8,8,128]{2,1,0:T(8,128)}, u32[]{:S(2)}) copy-start(f32[8,8,128]{2,1,0:T(8,128)} %shard_map.77) | copy-start | bytes 98308

commit v3 on v2

--- a/solution.py
+++ b/solution.py
@@ -27,44 +27,56 @@
     return lax.ppermute(part, axis, pairs)
 
 
-def padded_deformed(deformed):
+def halo_blocks(deformed):
     depth_x, width_y, width_z = deformed.shape
     low_y = neighbours(deformed[:, width_y - 1 :, :], "gy", True)
     high_y = neighbours(deformed[:, :1, :], "gy", False)
     gap_y = jnp.zeros((depth_x, 6, width_z), deformed.dtype)
-    rimmed = jnp.concatenate([deformed, high_y, gap_y, low_y], axis=1)
-    low_z = neighbours(rimmed[:, :, width_z - 1 :], "gz", True)
-    high_z = neighbours(rimmed[:, :, :1], "gz", False)
-    gap_z = jnp.zeros((depth_x, rimmed.shape[1], 126), deformed.dtype)
-    return jnp.concatenate([rimmed, high_z, gap_z, low_z], axis=2)
+    rows = jnp.concatenate([high_y, gap_y, low_y], axis=1)
+    first = jnp.concatenate([deformed[:, :, :1], rows[:, :, :1]], axis=1)
+    last = jnp.concatenate([deformed[:, :, width_z - 1 :], rows[:, :, width_z - 1 :]], axis=1)
+    low_z = neighbours(last, "gz", True)
+    high_z = neighbours(first, "gz", False)
+    gap_z = jnp.zeros((depth_x, first.shape[1], 126), deformed.dtype)
+    columns = jnp.concatenate([high_z, gap_z, low_z], axis=2)
+    return rows.astype(jnp.float32), columns.astype(jnp.float32)
 
 
 def lerp(base, other, weight):
     return base + weight * (other - base)
 
 
-def strip_kernel(dpad_ref, disp_ref, image_ref, contrast_ref, bright_ref,
-                 res_ref, prod_ref, mis_ref, sq_ref, energy_ref, shifts_ref):
+def strip_kernel(prev_ref, main_ref, next_ref, rows_ref, cols_ref, disp_ref, image_ref,
+                 contrast_ref, bright_ref,
+                 res_ref, prod_ref, mis_ref, sq_ref, energy_ref, pad_ref, shifts_ref):
     block = pl.program_id(0)
-    depth_x = dpad_ref.shape[0]
-    pad_y, pad_z = dpad_ref.shape[1], dpad_ref.shape[2]
+    depth_x = rows_ref.shape[0]
     width_y, width_z = image_ref.shape[1], image_ref.shape[2]
-
-    def source_plane(p, carry):
+    pad_y, pad_z = pad_ref.shape
+
+    def source_plane(p, plane):
         plane_x = block * KNOT - 1 + p
         valid = jnp.logical_and(plane_x >= 0, plane_x < depth_x)
         safe = jnp.clip(plane_x, 0, depth_x - 1)
-        plane = dpad_ref[safe].astype(jnp.float32)
-        plane = jnp.where(valid, plane, 0.0)
-        by_y = (pltpu.roll(plane, 1, 0), plane, pltpu.roll(plane, pad_y - 1, 0))
+        pad_ref[:width_y, :width_z] = plane.astype(jnp.float32)
+        pad_ref[width_y:, :width_z] = rows_ref[safe]
+        pad_ref[:, width_z:] = cols_ref[safe]
+        whole = jnp.where(valid, pad_ref[...], 0.0)
+        by_y = (pltpu.roll(whole, 1, 0), whole, pltpu.roll(whole, pad_y - 1, 0))
         for b in range(3):
-            rows = by_y[b][:width_y]
-            by_z = (pltpu.roll(rows, 1, 1), rows, pltpu.roll(rows, pad_z - 1, 1))
+            part = by_y[b][:width_y]
+            by_z = (pltpu.roll(part, 1, 1), part, pltpu.roll(part, pad_z - 1, 1))
             for c in range(3):
                 shifts_ref[p, 3 * b + c] = by_z[c][:, :width_z]
+
+    source_plane(0, prev_ref[0])
+
+    def inner_plane(p, carry):
+        source_plane(p, main_ref[p - 1])
         return carry
 
-    lax.fori_loop(0, KNOT + 2, source_plane, 0)
+    lax.fori_loop(1, KNOT + 1, inner_plane, 0)
+    source_plane(KNOT + 1, next_ref[0])
 
     chunks_y = width_y // ROWS
     chunks_z = width_z // LANES
@@ -125,24 +137,30 @@
     energy_ref[0] = energy
 
 
-def strip_sums(dpad, displacement, image, contrast_y, bright_y):
+def strip_sums(deformed, rows, cols, displacement, image, contrast_y, bright_y):
     depth_x, width_y, width_z = image.shape
     nodes = depth_x // KNOT
     f32 = jnp.float32
     block_sum = jax.ShapeDtypeStruct((nodes, width_y, width_z), f32)
     node_spec = pl.BlockSpec((1, width_y, width_z), lambda i: (i, 0, 0))
+    plane_spec = pl.BlockSpec((KNOT, width_y, width_z), lambda i: (i, 0, 0))
     return pl.pallas_call(
         strip_kernel,
         grid=(nodes,),
         in_specs=[
+            pl.BlockSpec((1, width_y, width_z), lambda i: (jnp.maximum(i * KNOT - 1, 0), 0, 0)),
+            plane_spec,
+            pl.BlockSpec((1, width_y, width_z),
+                         lambda i: (jnp.minimum(i * KNOT + KNOT, depth_x - 1), 0, 0)),
+            pl.BlockSpec(memory_space=pltpu.VMEM),
             pl.BlockSpec(memory_space=pltpu.VMEM),
             pl.BlockSpec((3, KNOT, width_y, width_z), lambda i: (0, i, 0, 0)),
-            pl.BlockSpec((KNOT, width_y, width_z), lambda i: (i, 0, 0)),
+            plane_spec,
             node_spec,
             node_spec,
         ],
         out_specs=[
-            pl.BlockSpec((KNOT, width_y, width_z), lambda i: (i, 0, 0)),
+            plane_spec,
             node_spec,
             node_spec,
             node_spec,
@@ -155,10 +173,13 @@
             block_sum,
             jax.ShapeDtypeStruct((nodes, ROWS, LANES), f32),
         ],
-        scratch_shapes=[pltpu.VMEM((KNOT + 2, 9, width_y, width_z), f32)],
+        scratch_shapes=[
+            pltpu.VMEM((width_y + rows.shape[1], width_z + cols.shape[2]), f32),
+            pltpu.VMEM((KNOT + 2, 9, width_y, width_z), f32),
+        ],
         compiler_params=pltpu.CompilerParams(
             dimension_semantics=("arbitrary",), vmem_limit_bytes=60 * 1024 * 1024),
-    )(dpad, displacement, image, contrast_y, bright_y)
+    )(deformed, deformed, deformed, rows, cols, displacement, image, contrast_y, bright_y)
 
 
 def node_sums(field):
@@ -253,11 +274,11 @@
 
 
 def local(reference_image, deformed, displacement, plane_factors, depth_factors):
-    dpad = padded_deformed(deformed)
+    rows, cols = halo_blocks(deformed)
     fields = jnp.einsum("krij,krz->kijz", plane_factors, depth_factors, precision=highest)
     fields = jnp.repeat(fields, KNOT, axis=2)
     residual, prod, mis, sq, energy_parts = strip_sums(
-        dpad, displacement, reference_image, fields[0], fields[1])
+        deformed, rows, cols, displacement, reference_image, fields[0], fields[1])
     prod, mis, sq = node_sums(prod), node_sums(mis), node_sums(sq)
     local_energy = jnp.sum(energy_parts)
 

time: 137 us -> 135 us (0.985)
  other arithmetic: 17.4 us -> 11.4 us
  local copies, waits for them, and re-layouts: 11.6 us -> 14.5 us
  Pallas kernels: 90.5 us -> 92.2 us
    concatenate x1 -> x3, other arithmetic: 7.21 us -> 1.49 us  [the longest x1 1.3 us: halo_blocks(): rows = jnp.concatenate([high_y, gap_y, low_y], axis=1)]
    pallas_call x1, Pallas kernels: 50.6 us -> 53 us  [strip_sums(): pl.pallas_call(strip_kernel, grid=(nodes,), in_specs=[pl.BlockSpec((1, wi...]
    convert_element_type x0 -> x1, other arithmetic: none -> 2.06 us  [halo_blocks(): return (rows.astype(jnp.float32), columns.astype(jnp.float32))]
    slice x3 -> x5, local copies, waits for them, and re-layouts: 2.55 us -> 4.43 us  [the longest x3 2.58 us: halo_blocks(): first = jnp.concatenate([deformed[:, :, :1], rows[:, :, :1]], axis=1)]
  transfers between devices with their start and end apart: 4 -> 4, of which waited for: 0 -> 0; matrix products, arithmetic and copies ran while one was open for 4% -> 5% of each run, Pallas kernels for 0% -> 0%
where the time goes in v3:
time: 135 us; the launch traced here: 134 us
  Pallas kernels  92.2 us (68%)
  local copies, waits for them, and re-layouts  14.5 us (11%)
  starting transfers between devices  11.8 us (9%)
  other arithmetic  11.4 us (8%)
  between operations  2.28 us (2%)
  matrix products  1.86 us (1%)
    pallas_call x1, Pallas kernels, strip_sums(): pl.pallas_call(strip_kernel, grid=(nodes,), in_specs=[pl.BlockSpec((1, wi...  53 us
    pallas_call x2, Pallas kernels, gather_sum(): pl.pallas_call(functools.partial(gather_sum_kernel, axis, n), out_shape=j...  39.3 us
    ppermute x4, starting transfers between devices, neighbours(): return lax.ppermute(part, axis, pairs)  11.8 us
    reduce_sum x3, other arithmetic, node_sums(): return field.reshape(nodes, width_y // KNOT, KNOT, width_z).sum(axis=2)  3.31 us
  transfers between devices with their start and end apart: 4, of which 0 were waited for; matrix products, arithmetic and copies ran while one was open for 5% of the time, Pallas kernels for 0%

profile of v3, /device:TPU:1, one launch (start us, length us, event | category | flops | bytes accessed | tf_op | source)
XLA Modules:
  0.0 134.1 jit_solution(7405991682160566163)
XLA Ops:
  0.6 1.4 %fusion.22 = (bf16[64,1,512]{2,1,0:T(2,128)(2,1)S(1)}, bf16[64,1,512]{2,1,0:T(2,128)(2,1)S(1)}) fusion(bf16[64,64,512]{2,1,0:T(8,128)(2,1)} %next_ref.1), kind=kLoop, calls=%fused_computation.58 | loop fusion | bytes 262144 | tf_op jit(solution)/shard_map/slice | solution.py:33
  2.0 3.3 %collective-permute-start = (bf16[64,1,512]{2,1,0:T(2,128)(2,1)S(1)}, bf16[64,1,512]{2,1,0:T(2,128)(2,1)S(1)}, u32[]{:S(2)}, u32[]{:S(2)}) collective-permute-start(bf16[64,1,512]{2,1,0:T(2,128)(2,1)S(1)} %get-tuple-element.24), channel_id=1, source_target_pairs={{8,0},{16,8},{24,16},{32,24},{40,32},{48,40},{56,48},{64,56},{72,6... | collective-permute-start | bytes 196616 | tf_op jit(solution)/shard_map/ppermute | solution.py:27
  5.4 3.2 %collective-permute-start.1 = (bf16[64,1,512]{2,1,0:T(2,128)(2,1)S(1)}, bf16[64,1,512]{2,1,0:T(2,128)(2,1)S(1)}, u32[]{:S(2)}, u32[]{:S(2)}) collective-permute-start(bf16[64,1,512]{2,1,0:T(2,128)(2,1)S(1)} %get-tuple-element.25), channel_id=1, source_target_pairs={{0,8},{8,16},{16,24},{24,32},{32,40},{40,48},{48,56},{56,64},{64,7... | collective-permute-start | bytes 196616 | tf_op jit(solution)/shard_map/ppermute | solution.py:27
  8.6 2.0 %fusion.21 = (bf16[64,64,1]{2,1,0:T(8,128)(2,1)S(1)}, bf16[64,64,1]{2,1,0:T(8,128)(2,1)S(1)}) fusion(bf16[64,64,512]{2,1,0:T(8,128)(2,1)} %next_ref.1), kind=kLoop, calls=%fused_computation.57 | loop fusion | bytes 32768 | tf_op jit(solution)/shard_map/slice | solution.py:36
  10.7 0.5 copy.34
  11.1 0.5 copy.35
  11.7 0.3 fusion.4
  12.2 1.6 %broadcast_bitcast_fusion = (f32[8,64,512]{2,1,0:T(8,128)}, f32[8,64,512]{2,1,0:T(8,128)}) fusion(f32[8,8,512]{2,1,0:T(8,128)S(1)} %get-tuple-element.30, f32[8,8,512]{2,1,0:T(8,128)S(1)} %get-tuple-element.31), kind=kLoop, calls=%fused_computation.10 | loop fusion | bytes 2359296 | tf_op jit(solution)/shard_map/broadcast_in_dim | solution.py:279
  13.9 1.3 pad_maximum_fusion
  15.3 0.4 copy.25
  15.8 1.3 collective-permute-start.2
  17.1 0.4 copy.27
  17.7 4.0 %collective-permute-start.3 = (bf16[64,72,1]{1,0,2:T(8,128)(2,1)S(1)}, bf16[64,72,1]{1,0,2:T(8,128)(2,1)S(1)}, u32[]{:S(2)}, u32[]{:S(2)}) collective-permute-start(bf16[64,72,1]{1,0,2:T(8,128)(2,1)S(1)} %pad_maximum_fusion.4), channel_id=1, source_target_pairs={{0,1},{1,2},{2,3},{3,4},{4,5},{5,6},{6,7},{8,9},{9,10},{10,11},{11... | collective-permute-start | bytes 27656 | tf_op jit(solution)/shard_map/ppermute | solution.py:27
  21.9 0.6 copy.28
  22.5 0.6 copy.29
  23.1 2.1 %maximum_convert_fusion.cols_ref = f32[64,72,128]{2,1,0:T(8,128)} fusion(bf16[64,72,1]{2,1,0:T(8,128)(2,1)S(1)} %copy.29, bf16[64,72,1]{2,1,0:T(8,128)(2,1)S(1)} %copy.28, bf16[128]{0:T(256)(128)(2,1)S(1)} %pad.32.clone), kind=kLoop, calls=%fused_computation | loop fusion | flops 3538944 | bytes 2377984 | tf_op jit(solution)/shard_map/convert_element_type | solution.py:42
  25.1 53.0 %shard_map.76 = (bf16[64,64,512]{2,1,0:T(8,128)(2,1)}, f32[8,64,512]{2,1,0:T(8,128)}, f32[8,64,512]{2,1,0:T(8,128)}, f32[8,64,512]{2,1,0:T(8,128)}, f32[8,16,256]{2,1,0:T(8,128)}) custom-call(bf16[64,64,512]{2,1,0:T(8,128)(2,1)} %next_ref.1, bf16[64,64,512]{2,1,0:T(8,128)(2,1)} %next_ref.1, bf16[64,64,512]{2,1,0:T(8,128)(2,1)} %next_ref.1, ...), custom_call_target="tpu_custom_call" | custom-call | tf_op jit(solution)/shard_map/pallas_call | solution.py:147
  78.1 1.6 %bitcast_reduce_fusion.1 = f32[8,8,512]{2,1,0:T(8,128)S(1)} fusion(f32[8,64,512]{2,1,0:T(8,128)} %get-tuple-element.10), kind=kLoop, calls=%fused_computation.7 | loop fusion | flops 229376 | bytes 1179648 | tf_op jit(solution)/shard_map/reduce_sum | solution.py:187
  80.2 1.5 %bitcast_reduce_fusion.2 = f32[8,8,512]{2,1,0:T(8,128)S(1)} fusion(f32[8,64,512]{2,1,0:T(8,128)} %get-tuple-element.9), kind=kLoop, calls=%fused_computation.8 | loop fusion | flops 229376 | bytes 1179648 | tf_op jit(solution)/shard_map/reduce_sum | solution.py:187
  83.6 0.6 reduce_sum.58
  84.2 0.7 select_maximum_fusion.1
  85.0 0.7 maximum_maximum_fusion.1.part_ref
  85.6 14.9 %shard_map.77 = f32[8,8,128]{2,1,0:T(8,128)} custom-call(f32[8,8,128]{2,1,0:T(8,128)} %maximum_maximum_fusion.1.part_ref), custom_call_target="tpu_custom_call" | custom-call | tf_op jit(solution)/shard_map/pallas_call | solution.py:246
  100.6 1.3 slice.117
  102.0 0.7 select_maximum_fusion
  102.7 0.8 maximum_maximum_fusion.part_ref
  103.5 24.4 %shard_map.78 = f32[16,32,128]{2,1,0:T(8,128)} custom-call(f32[16,32,128]{2,1,0:T(8,128)} %maximum_maximum_fusion.part_ref), custom_call_target="tpu_custom_call" | custom-call | tf_op jit(solution)/shard_map/pallas_call | solution.py:246
  127.9 0.9 slice.120
  128.8 0.7 slice_bitcast_fusion.2
  129.5 1.3 slice.119
  132.6 0.8 copy.32
  133.4 0.7 fusion.2
  (57 shorter events, 3.7 us)
Async XLA Ops:
  2.0 11.8 %collective-permute-start = (bf16[64,1,512]{2,1,0:T(2,128)(2,1)S(1)}, bf16[64,1,512]{2,1,0:T(2,128)(2,1)S(1)}, u32[]{:S(2)}, u32[]{:S(2)}) collective-permute-start(bf16[64,1,512]{2,1,0:T(2,128)(2,1)S(1)} %get-tuple-element.24), channel_id=1, source_target_pairs={{8,0},{16,8},{24,16},{32,24},{40,32},{48,40},{56,48},{64,56},{72,6... | collective-permute-start | bytes 196616 | tf_op jit(solution)/shard_map/ppermute | solution.py:27
  5.4 6.2 %copy-start = (f32[2,32,512]{2,1,0:T(8,128)S(1)}, f32[2,32,512]{2,1,0:T(8,128)}, u32[]{:S(2)}) copy-start(f32[2,32,512]{2,1,0:T(8,128)} %param.9) | copy-start | bytes 393220
  5.4 6.3 %copy-start.2 = (f32[2,32,8,8]{1,3,2,0:T(8,128)S(1)}, f32[2,32,8,8]{1,3,2,0:T(8,128)}, u32[]{:S(2)}) copy-start(f32[2,32,8,8]{1,3,2,0:T(8,128)} %param.8) | copy-start | bytes 49156
  5.4 8.5 %collective-permute-start.1 = (bf16[64,1,512]{2,1,0:T(2,128)(2,1)S(1)}, bf16[64,1,512]{2,1,0:T(2,128)(2,1)S(1)}, u32[]{:S(2)}, u32[]{:S(2)}) collective-permute-start(bf16[64,1,512]{2,1,0:T(2,128)(2,1)S(1)} %get-tuple-element.25), channel_id=1, source_target_pairs={{0,8},{8,16},{16,24},{24,32},{32,40},{40,48},{48,56},{56,64},{64,7... | collective-permute-start | bytes 196616 | tf_op jit(solution)/shard_map/ppermute | solution.py:27
  15.8 6.1 %collective-permute-start.2 = (bf16[64,72,1]{1,0,2:T(8,128)(2,1)S(1)}, bf16[64,72,1]{1,0,2:T(8,128)(2,1)S(1)}, u32[]{:S(2)}, u32[]{:S(2)}) collective-permute-start(bf16[64,72,1]{1,0,2:T(8,128)(2,1)S(1)} %pad_maximum_fusion.3), channel_id=1, source_target_pairs={{1,0},{2,1},{3,2},{4,3},{5,4},{6,5},{7,6},{9,8},{10,9},{11,10},{12... | collective-permute-start | bytes 27656 | tf_op jit(solution)/shard_map/ppermute | solution.py:27
  17.7 4.8 %collective-permute-start.3 = (bf16[64,72,1]{1,0,2:T(8,128)(2,1)S(1)}, bf16[64,72,1]{1,0,2:T(8,128)(2,1)S(1)}, u32[]{:S(2)}, u32[]{:S(2)}) collective-permute-start(bf16[64,72,1]{1,0,2:T(8,128)(2,1)S(1)} %pad_maximum_fusion.4), channel_id=1, source_target_pairs={{0,1},{1,2},{2,3},{3,4},{4,5},{5,6},{6,7},{8,9},{9,10},{10,11},{11... | collective-permute-start | bytes 27656 | tf_op jit(solution)/shard_map/ppermute | solution.py:27
  78.1 4.1 %copy-start.1 = (f32[8,64,512]{2,1,0:T(8,128)S(1)}, f32[8,64,512]{2,1,0:T(8,128)}, u32[]{:S(2)}) copy-start(f32[8,64,512]{2,1,0:T(8,128)} %get-tuple-element.11) | copy-start | bytes 3145732
  79.9 3.6 %copy-start.3 = (f32[8,16,256]{2,1,0:T(8,128)S(1)}, f32[8,16,256]{2,1,0:T(8,128)}, u32[]{:S(2)}) copy-start(f32[8,16,256]{2,1,0:T(8,128)} %get-tuple-element.12) | copy-start | bytes 393220
  100.6 30.2 %copy-start.4 = (f32[8,8,128]{2,1,0:T(8,128)S(1)}, f32[8,8,128]{2,1,0:T(8,128)}, u32[]{:S(2)}) copy-start(f32[8,8,128]{2,1,0:T(8,128)} %shard_map.77) | copy-start | bytes 98308

commit v4 on v3

--- a/solution.py
+++ b/solution.py
@@ -187,90 +187,114 @@
     return field.reshape(nodes, width_y // KNOT, KNOT, width_z).sum(axis=2)
 
 
-def gather_sum_kernel(axis, n, part_ref, out_ref, landed, summed, gathered,
-                      send_one, recv_one, send_two, recv_two):
-    me = lax.axis_index(axis)
+def exchange(axis, n, me, d, src, buffer, send_sem, recv_sem):
+    target = lax.rem(me + d, n)
+    return pltpu.make_async_remote_copy(
+        src_ref=src(target), dst_ref=buffer.at[me],
+        send_sem=send_sem.at[target], recv_sem=recv_sem.at[me],
+        device_id={axis: target}, device_id_type=pl.DeviceIdType.MESH)
+
+
+def arrival(axis, n, me, d, src_ref, buffer, sem):
+    source = lax.rem(me + n - d, n)
+    return pltpu.make_async_remote_copy(
+        src_ref=src_ref, dst_ref=buffer.at[source],
+        send_sem=sem.at[source], recv_sem=sem.at[source],
+        device_id={axis: source}, device_id_type=pl.DeviceIdType.MESH)
+
+
+def both_sums_kernel(nz, ny, plane_row, depth_row, plane_ref, depth_ref, plane_out, depth_out,
+                     plane_landed, depth_landed, plane_summed, depth_summed,
+                     plane_gathered, depth_gathered, sems):
+    mz, my = lax.axis_index("gz"), lax.axis_index("gy")
     barrier = pltpu.get_barrier_semaphore()
-    for d in range(1, n):
-        pl.semaphore_signal(barrier, inc=1, device_id={axis: lax.rem(me + d, n)},
+    for d in range(1, nz):
+        pl.semaphore_signal(barrier, inc=1, device_id={"gz": lax.rem(mz + d, nz)},
                             device_id_type=pl.DeviceIdType.MESH)
-    pl.semaphore_wait(barrier, n - 1)
-
-    def scatter(d):
-        target = lax.rem(me + d, n)
-        return pltpu.make_async_remote_copy(
-            src_ref=part_ref.at[target], dst_ref=landed.at[me],
-            send_sem=send_one.at[target], recv_sem=recv_one.at[me],
-            device_id={axis: target}, device_id_type=pl.DeviceIdType.MESH)
-
-    def arrival(d, buffer, sem, source_ref):
-        source = lax.rem(me + n - d, n)
-        return pltpu.make_async_remote_copy(
-            src_ref=source_ref, dst_ref=buffer.at[source],
-            send_sem=sem.at[source], recv_sem=sem.at[source],
-            device_id={axis: source}, device_id_type=pl.DeviceIdType.MESH)
-
-    outgoing = [scatter(d) for d in range(1, n)]
-    for copy in outgoing:
+    for d in range(1, ny):
+        pl.semaphore_signal(barrier, inc=1, device_id={"gy": lax.rem(my + d, ny)},
+                            device_id_type=pl.DeviceIdType.MESH)
+    pl.semaphore_wait(barrier, nz - 1 + ny - 1)
+    zs1, zr1, zs2, zr2, ys1, yr1, ys2, yr2 = sems
+
+    z_out = [exchange("gz", nz, mz, d, lambda t: plane_ref.at[t], plane_landed, zs1, zr1)
+             for d in range(1, nz)]
+    y_out = [exchange("gy", ny, my, d, lambda t: depth_ref.at[t], depth_landed, ys1, yr1)
+             for d in range(1, ny)]
+    for copy in z_out + y_out:
         copy.start()
-    total = part_ref[me]
-    for d in range(1, n):
-        arrival(d, landed, recv_one, part_ref.at[0]).wait_recv()
-        total = total + landed[lax.rem(me + n - d, n)]
-    summed[...] = total
-    for copy in outgoing:
+    depth_total = depth_ref[my]
+    for d in range(1, ny):
+        arrival("gy", ny, my, d, depth_ref.at[0], depth_landed, yr1).wait_recv()
+        depth_total = depth_total + depth_landed[lax.rem(my + ny - d, ny)]
+    depth_summed[...] = depth_total
+    plane_total = plane_ref[mz]
+    for d in range(1, nz):
+        arrival("gz", nz, mz, d, plane_ref.at[0], plane_landed, zr1).wait_recv()
+        plane_total = plane_total + plane_landed[lax.rem(mz + nz - d, nz)]
+    rows = lax.broadcasted_iota(jnp.int32, plane_total.shape, 0)
+    lanes = lax.broadcasted_iota(jnp.int32, plane_total.shape, 1)
+    slot = jnp.logical_and(rows == plane_row, lanes == RANK)
+    depth_slot = jnp.logical_and(
+        lax.broadcasted_iota(jnp.int32, depth_total.shape, 0) == depth_row,
+        lax.broadcasted_iota(jnp.int32, depth_total.shape, 1) == RANK)
+    column_energy = jnp.sum(jnp.where(depth_slot, depth_total, 0.0))
+    plane_total = jnp.where(slot, column_energy, plane_total)
+    plane_summed[...] = plane_total
+    for copy in z_out + y_out:
         copy.wait_send()
 
-    def gather(d):
-        target = lax.rem(me + d, n)
-        return pltpu.make_async_remote_copy(
-            src_ref=summed, dst_ref=gathered.at[me],
-            send_sem=send_two.at[target], recv_sem=recv_two.at[me],
-            device_id={axis: target}, device_id_type=pl.DeviceIdType.MESH)
-
-    outgoing = [gather(d) for d in range(1, n)]
-    for copy in outgoing:
+    z_out = [exchange("gz", nz, mz, d, lambda t: plane_summed, plane_gathered, zs2, zr2)
+             for d in range(1, nz)]
+    y_out = [exchange("gy", ny, my, d, lambda t: depth_summed, depth_gathered, ys2, yr2)
+             for d in range(1, ny)]
+    for copy in z_out + y_out:
         copy.start()
-    out_ref[me] = total
-    for d in range(1, n):
-        arrival(d, gathered, recv_two, summed).wait_recv()
-        source = lax.rem(me + n - d, n)
-        out_ref[source] = gathered[source]
-    for copy in outgoing:
+    plane_out[mz] = plane_total
+    depth_out[my] = depth_total
+    for d in range(1, nz):
+        arrival("gz", nz, mz, d, plane_summed, plane_gathered, zr2).wait_recv()
+        source = lax.rem(mz + nz - d, nz)
+        plane_out[source] = plane_gathered[source]
+    for d in range(1, ny):
+        arrival("gy", ny, my, d, depth_summed, depth_gathered, yr2).wait_recv()
+        source = lax.rem(my + ny - d, ny)
+        depth_out[source] = depth_gathered[source]
+    for copy in z_out + y_out:
         copy.wait_send()
 
 
-def gather_sum(parts, axis, tag):
-    n = lax.axis_size(axis)
-    chunk = parts.shape[1:]
-    return pl.pallas_call(
-        functools.partial(gather_sum_kernel, axis, n),
-        out_shape=jax.ShapeDtypeStruct(parts.shape, parts.dtype),
-        in_specs=[pl.BlockSpec(memory_space=pltpu.VMEM)],
-        out_specs=pl.BlockSpec(memory_space=pltpu.VMEM),
-        scratch_shapes=[
-            pltpu.VMEM(parts.shape, parts.dtype),
-            pltpu.VMEM(chunk, parts.dtype),
-            pltpu.VMEM(parts.shape, parts.dtype),
-            pltpu.SemaphoreType.DMA((n,)),
-            pltpu.SemaphoreType.DMA((n,)),
-            pltpu.SemaphoreType.DMA((n,)),
-            pltpu.SemaphoreType.DMA((n,)),
-        ],
-        compiler_params=pltpu.CompilerParams(collective_id=tag, has_side_effects=True),
-    )(parts)
-
-
-def all_sum(main, extras, axis, tag):
-    n = lax.axis_size(axis)
+def chunked(main, extras, n):
     rows = -(-main.shape[0] // (n * 128))
     main = jnp.pad(main, (0, n * rows * 128 - main.shape[0])).reshape(n, rows, 128)
     tail = jnp.pad(extras, (0, 128 - extras.shape[0]))
     tail = jnp.broadcast_to(tail, (n, 1, 128))
     spare = -(-(rows + 1) // 8) * 8 - rows - 1
-    parts = jnp.concatenate([main, tail, jnp.zeros((n, spare, 128), main.dtype)], axis=1)
-    summed = gather_sum(parts, axis, tag)
-    return summed[:, :rows].reshape(-1), summed[0, rows]
+    return jnp.concatenate([main, tail, jnp.zeros((n, spare, 128), main.dtype)], axis=1), rows
+
+
+def both_sums(plane_parts, depth_parts, plane_row, depth_row):
+    nz, ny = plane_parts.shape[0], depth_parts.shape[0]
+    f32 = jnp.float32
+    dma = pltpu.SemaphoreType.DMA
+    return pl.pallas_call(
+        functools.partial(both_sums_kernel, nz, ny, plane_row, depth_row),
+        out_shape=[jax.ShapeDtypeStruct(plane_parts.shape, f32),
+                   jax.ShapeDtypeStruct(depth_parts.shape, f32)],
+        in_specs=[pl.BlockSpec(memory_space=pltpu.VMEM)] * 2,
+        out_specs=[pl.BlockSpec(memory_space=pltpu.VMEM)] * 2,
+        scratch_shapes=[
+            pltpu.VMEM(plane_parts.shape, f32),
+            pltpu.VMEM(depth_parts.shape, f32),
+            pltpu.VMEM(plane_parts.shape[1:], f32),
+            pltpu.VMEM(depth_parts.shape[1:], f32),
+            pltpu.VMEM(plane_parts.shape, f32),
+            pltpu.VMEM(depth_parts.shape, f32),
+            [dma((nz,)), dma((nz,)), dma((nz,)), dma((nz,)),
+             dma((ny,)), dma((ny,)), dma((ny,)), dma((ny,))],
+        ],
+        compiler_params=pltpu.CompilerParams(collective_id=1, has_side_effects=True),
+    )(plane_parts, depth_parts)
 
 
 def local(reference_image, deformed, displacement, plane_factors, depth_factors):
@@ -294,18 +318,22 @@
     first_diag = jnp.einsum("rz,ijz->rij", depth_factors[0] * depth_factors[0], sq, precision=highest)
     depth_level = KNOT * KNOT * jnp.sum(depth_factors[1] * depth_factors[1], axis=1)
 
+    nz, ny = lax.axis_size("gz"), lax.axis_size("gy")
     plane_terms = jnp.concatenate([grad_plane.reshape(-1), first_diag.reshape(-1)])
-    plane_terms, plane_extra = all_sum(
-        plane_terms, jnp.concatenate([depth_level, local_energy[None]]), "gz", 1)
+    depth_terms = jnp.concatenate([grad_depth.reshape(-1), first_depth.reshape(-1)])
+    blank = jnp.zeros((), jnp.float32)
+    plane_parts, plane_rows = chunked(plane_terms, jnp.concatenate([depth_level, blank[None]]), nz)
+    depth_parts, depth_rows = chunked(depth_terms, jnp.concatenate([level_sum, local_energy[None]]), ny)
+    plane_summed, depth_summed = both_sums(plane_parts, depth_parts, plane_rows, depth_rows)
+    plane_terms = plane_summed[:, :plane_rows].reshape(-1)
+    depth_terms = depth_summed[:, :depth_rows].reshape(-1)
     grad_plane = plane_terms[: grad_plane.size].reshape(grad_plane.shape)
     first_diag = plane_terms[grad_plane.size : grad_plane.size + first_diag.size].reshape(first_diag.shape)
-    depth_level, row_energy = plane_extra[:RANK], plane_extra[RANK]
-    depth_terms = jnp.concatenate([grad_depth.reshape(-1), first_depth.reshape(-1)])
-    depth_terms, depth_extra = all_sum(
-        depth_terms, jnp.concatenate([level_sum, row_energy[None]]), "gy", 2)
     grad_depth = depth_terms[: grad_depth.size].reshape(grad_depth.shape)
     first_depth = depth_terms[grad_depth.size : grad_depth.size + first_depth.size].reshape(first_depth.shape)
-    level_sum, energy = depth_extra[:RANK], depth_extra[RANK]
+    depth_level = plane_summed[0, plane_rows, :RANK]
+    level_sum = depth_summed[0, depth_rows, :RANK]
+    energy = jnp.sum(plane_summed[:, plane_rows, RANK])
 
     nodes_x = plane_factors.shape[2]
     nodes_y = plane_factors.shape[3] * lax.axis_size("gy")

time: 135 us -> 121 us (0.90)
  Pallas kernels: 92.2 us -> 79.4 us
    pallas_call x2 -> x1, Pallas kernels: 39.3 us -> 26.5 us  [both_sums(): pl.pallas_call(functools.partial(both_sums_kernel, nz, ny, plane_row, dep...]
    slice x3 -> x1, local copies, waits for them, and re-layouts: 3.54 us -> 0.95 us  [local(): depth_terms = depth_summed[:, :depth_rows].reshape(-1)]
    reduce_sum x0 -> x1, other arithmetic: none -> 1.44 us  [local(): energy = jnp.sum(plane_summed[:, plane_rows, RANK])]
where the time goes in v4:
time: 121 us
  Pallas kernels  79.4 us (66%)
  local copies, waits for them, and re-layouts  13.4 us (11%)
  other arithmetic  12.2 us (10%)
  starting transfers between devices  11.7 us (10%)
  between operations  2.25 us (2%)
  matrix products  1.87 us (2%)
    pallas_call x1, Pallas kernels, strip_sums(): pl.pallas_call(strip_kernel, grid=(nodes,), in_specs=[pl.BlockSpec((1, wi...  53 us
    pallas_call x1, Pallas kernels, both_sums(): pl.pallas_call(functools.partial(both_sums_kernel, nz, ny, plane_row, dep...  26.5 us
    ppermute x4, starting transfers between devices, neighbours(): return lax.ppermute(part, axis, pairs)  11.7 us
    reduce_sum x3, other arithmetic, node_sums(): return field.reshape(nodes, width_y // KNOT, KNOT, width_z).sum(axis=2)  3.31 us
    slice x3, local copies, waits for them, and re-layouts, halo_blocks(): first = jnp.concatenate([deformed[:, :, :1], rows[:, :, :1]], axis=1)  2.58 us
  transfers between devices with their start and end apart: 4, of which 0 were waited for; matrix products, arithmetic and copies ran while one was open for 5% of the time, Pallas kernels for 0%

profile of v4, /device:TPU:1, one launch (start us, length us, event | category | flops | bytes accessed | tf_op | source)
XLA Modules:
  0.0 120.8 jit_solution(1104192643360905308)
XLA Ops:
  0.7 1.4 %fusion.22 = (bf16[64,1,512]{2,1,0:T(2,128)(2,1)S(1)}, bf16[64,1,512]{2,1,0:T(2,128)(2,1)S(1)}) fusion(bf16[64,64,512]{2,1,0:T(8,128)(2,1)} %next_ref.1), kind=kLoop, calls=%fused_computation.59 | loop fusion | bytes 262144 | tf_op jit(solution)/shard_map/slice | solution.py:33
  2.1 3.3 %collective-permute-start = (bf16[64,1,512]{2,1,0:T(2,128)(2,1)S(1)}, bf16[64,1,512]{2,1,0:T(2,128)(2,1)S(1)}, u32[]{:S(2)}, u32[]{:S(2)}) collective-permute-start(bf16[64,1,512]{2,1,0:T(2,128)(2,1)S(1)} %get-tuple-element.28), channel_id=1, source_target_pairs={{8,0},{16,8},{24,16},{32,24},{40,32},{48,40},{56,48},{64,56},{72,6... | collective-permute-start | bytes 196616 | tf_op jit(solution)/shard_map/ppermute | solution.py:27
  5.4 3.1 %collective-permute-start.1 = (bf16[64,1,512]{2,1,0:T(2,128)(2,1)S(1)}, bf16[64,1,512]{2,1,0:T(2,128)(2,1)S(1)}, u32[]{:S(2)}, u32[]{:S(2)}) collective-permute-start(bf16[64,1,512]{2,1,0:T(2,128)(2,1)S(1)} %get-tuple-element.29), channel_id=1, source_target_pairs={{0,8},{8,16},{16,24},{24,32},{32,40},{40,48},{48,56},{56,64},{64,7... | collective-permute-start | bytes 196616 | tf_op jit(solution)/shard_map/ppermute | solution.py:27
  8.5 2.0 %fusion.21 = (bf16[64,64,1]{2,1,0:T(8,128)(2,1)S(1)}, bf16[64,64,1]{2,1,0:T(8,128)(2,1)S(1)}) fusion(bf16[64,64,512]{2,1,0:T(8,128)(2,1)} %next_ref.1), kind=kLoop, calls=%fused_computation.58 | loop fusion | bytes 32768 | tf_op jit(solution)/shard_map/slice | solution.py:36
  10.6 0.4 fusion.4
  11.1 1.6 %broadcast_bitcast_fusion = (f32[8,64,512]{2,1,0:T(8,128)}, f32[8,64,512]{2,1,0:T(8,128)}) fusion(f32[8,8,512]{2,1,0:T(8,128)S(1)} %get-tuple-element.34, f32[8,8,512]{2,1,0:T(8,128)S(1)} %get-tuple-element.35), kind=kLoop, calls=%fused_computation.10 | loop fusion | bytes 2359296 | tf_op jit(solution)/shard_map/broadcast_in_dim | solution.py:303
  12.8 0.5 copy.34
  13.2 0.5 copy.35
  13.8 1.3 %pad_maximum_fusion = (bf16[64,8,512]{2,1,0:T(8,128)(2,1)S(1)}, f32[64,8,512]{2,1,0:T(8,128)}) fusion(bf16[64,1,512]{2,1,0:T(2,128)(2,1)S(1)} %collective-permute-done.1, bf16[64,1,512]{2,1,0:T(2,128)(2,1)S(1)} %collective-permute-done, bf16[8]{0:T(256)(128)(2,1)S(1)} %pad.39.clone), kind=kLoop, calls=%fused_computation.9 | loop fusion | flops 1835008 | bytes 1703952 | tf_op jit(solution)/shard_map/concatenate | solution.py:35
  15.2 0.4 copy.25
  15.7 1.3 %collective-permute-start.2 = (bf16[64,72,1]{1,0,2:T(8,128)(2,1)S(1)}, bf16[64,72,1]{1,0,2:T(8,128)(2,1)S(1)}, u32[]{:S(2)}, u32[]{:S(2)}) collective-permute-start(bf16[64,72,1]{1,0,2:T(8,128)(2,1)S(1)} %pad_maximum_fusion.3), channel_id=1, source_target_pairs={{1,0},{2,1},{3,2},{4,3},{5,4},{6,5},{7,6},{9,8},{10,9},{11,10},{12... | collective-permute-start | bytes 27656 | tf_op jit(solution)/shard_map/ppermute | solution.py:27
  17.0 0.4 copy.27
  17.6 4.0 %collective-permute-start.3 = (bf16[64,72,1]{1,0,2:T(8,128)(2,1)S(1)}, bf16[64,72,1]{1,0,2:T(8,128)(2,1)S(1)}, u32[]{:S(2)}, u32[]{:S(2)}) collective-permute-start(bf16[64,72,1]{1,0,2:T(8,128)(2,1)S(1)} %pad_maximum_fusion.4), channel_id=1, source_target_pairs={{0,1},{1,2},{2,3},{3,4},{4,5},{5,6},{6,7},{8,9},{9,10},{10,11},{11... | collective-permute-start | bytes 27656 | tf_op jit(solution)/shard_map/ppermute | solution.py:27
  21.9 0.6 copy.28
  22.5 0.6 copy.29
  23.0 2.1 %maximum_convert_fusion.cols_ref = f32[64,72,128]{2,1,0:T(8,128)} fusion(bf16[64,72,1]{2,1,0:T(8,128)(2,1)S(1)} %copy.29, bf16[64,72,1]{2,1,0:T(8,128)(2,1)S(1)} %copy.28, bf16[128]{0:T(256)(128)(2,1)S(1)} %pad.32.clone), kind=kLoop, calls=%fused_computation | loop fusion | flops 3538944 | bytes 2377984 | tf_op jit(solution)/shard_map/convert_element_type | solution.py:42
  25.1 53.0 %shard_map.76 = (bf16[64,64,512]{2,1,0:T(8,128)(2,1)}, f32[8,64,512]{2,1,0:T(8,128)}, f32[8,64,512]{2,1,0:T(8,128)}, f32[8,64,512]{2,1,0:T(8,128)}, f32[8,16,256]{2,1,0:T(8,128)}) custom-call(bf16[64,64,512]{2,1,0:T(8,128)(2,1)} %next_ref.1, bf16[64,64,512]{2,1,0:T(8,128)(2,1)} %next_ref.1, bf16[64,64,512]{2,1,0:T(8,128)(2,1)} %next_ref.1, ...), custom_call_target="tpu_custom_call" | custom-call | tf_op jit(solution)/shard_map/pallas_call | solution.py:147
  78.1 1.6 %bitcast_reduce_fusion.1 = f32[8,8,512]{2,1,0:T(8,128)S(1)} fusion(f32[8,64,512]{2,1,0:T(8,128)} %get-tuple-element.12), kind=kLoop, calls=%fused_computation.7 | loop fusion | flops 229376 | bytes 1179648 | tf_op jit(solution)/shard_map/reduce_sum | solution.py:187
  80.2 1.5 %bitcast_reduce_fusion.2 = f32[8,8,512]{2,1,0:T(8,128)S(1)} fusion(f32[8,64,512]{2,1,0:T(8,128)} %get-tuple-element.11), kind=kLoop, calls=%fused_computation.8 | loop fusion | flops 229376 | bytes 1179648 | tf_op jit(solution)/shard_map/reduce_sum | solution.py:187
  82.4 0.3 convolution_bitcast_fusion
  83.1 0.6 reduce_sum.68
  84.3 0.7 select_maximum_fusion
  85.0 0.8 maximum_maximum_fusion.depth_ref
  85.8 0.7 maximum_maximum_fusion.1.plane_ref
  86.5 26.5 %shard_map.77 = (f32[8,8,128]{2,1,0:T(8,128)}, f32[16,32,128]{2,1,0:T(8,128)}) custom-call(f32[8,8,128]{2,1,0:T(8,128)} %maximum_maximum_fusion.1.plane_ref, f32[16,32,128]{2,1,0:T(8,128)} %maximum_maximum_fusion.depth_ref), custom_call_target="tpu_custom_call" | custom-call | tf_op jit(solution)/shard_map/pallas_call | solution.py:280
  113.0 0.9 slice.103
  113.9 0.7 slice_bitcast_fusion.2
  114.6 1.4 %slice_reduce_fusion = f32[]{:T(128)} fusion(f32[8,8,128]{2,1,0:T(8,128)} %get-tuple-element.15), kind=kLoop, calls=%fused_computation.50 | loop fusion | flops 7 | bytes 36 | tf_op jit(solution)/shard_map/reduce_sum | solution.py:336
  116.1 0.7 slice_bitcast_fusion.3
  116.8 1.0 slice.98
  119.3 0.8 copy.32
  120.1 0.7 fusion.2
  (53 shorter events, 3.3 us)
Async XLA Ops:
  0.6 10.0 %copy-start.2 = (f32[2,32,8,8]{1,3,2,0:T(8,128)S(1)}, f32[2,32,8,8]{1,3,2,0:T(8,128)}, u32[]{:S(2)}) copy-start(f32[2,32,8,8]{1,3,2,0:T(8,128)} %param.8) | copy-start | bytes 49156
  0.6 10.0 %copy-start = (f32[2,32,512]{2,1,0:T(8,128)S(1)}, f32[2,32,512]{2,1,0:T(8,128)}, u32[]{:S(2)}) copy-start(f32[2,32,512]{2,1,0:T(8,128)} %param.9) | copy-start | bytes 393220
  2.1 11.7 %collective-permute-start = (bf16[64,1,512]{2,1,0:T(2,128)(2,1)S(1)}, bf16[64,1,512]{2,1,0:T(2,128)(2,1)S(1)}, u32[]{:S(2)}, u32[]{:S(2)}) collective-permute-start(bf16[64,1,512]{2,1,0:T(2,128)(2,1)S(1)} %get-tuple-element.28), channel_id=1, source_target_pairs={{8,0},{16,8},{24,16},{32,24},{40,32},{48,40},{56,48},{64,56},{72,6... | collective-permute-start | bytes 196616 | tf_op jit(solution)/shard_map/ppermute | solution.py:27
  5.4 8.3 %collective-permute-start.1 = (bf16[64,1,512]{2,1,0:T(2,128)(2,1)S(1)}, bf16[64,1,512]{2,1,0:T(2,128)(2,1)S(1)}, u32[]{:S(2)}, u32[]{:S(2)}) collective-permute-start(bf16[64,1,512]{2,1,0:T(2,128)(2,1)S(1)} %get-tuple-element.29), channel_id=1, source_target_pairs={{0,8},{8,16},{16,24},{24,32},{32,40},{40,48},{48,56},{56,64},{64,7... | collective-permute-start | bytes 196616 | tf_op jit(solution)/shard_map/ppermute | solution.py:27
  15.7 6.1 %collective-permute-start.2 = (bf16[64,72,1]{1,0,2:T(8,128)(2,1)S(1)}, bf16[64,72,1]{1,0,2:T(8,128)(2,1)S(1)}, u32[]{:S(2)}, u32[]{:S(2)}) collective-permute-start(bf16[64,72,1]{1,0,2:T(8,128)(2,1)S(1)} %pad_maximum_fusion.3), channel_id=1, source_target_pairs={{1,0},{2,1},{3,2},{4,3},{5,4},{6,5},{7,6},{9,8},{10,9},{11,10},{12... | collective-permute-start | bytes 27656 | tf_op jit(solution)/shard_map/ppermute | solution.py:27
  17.6 4.9 %collective-permute-start.3 = (bf16[64,72,1]{1,0,2:T(8,128)(2,1)S(1)}, bf16[64,72,1]{1,0,2:T(8,128)(2,1)S(1)}, u32[]{:S(2)}, u32[]{:S(2)}) collective-permute-start(bf16[64,72,1]{1,0,2:T(8,128)(2,1)S(1)} %pad_maximum_fusion.4), channel_id=1, source_target_pairs={{0,1},{1,2},{2,3},{3,4},{4,5},{5,6},{6,7},{8,9},{9,10},{10,11},{11... | collective-permute-start | bytes 27656 | tf_op jit(solution)/shard_map/ppermute | solution.py:27
  78.0 4.1 %copy-start.1 = (f32[8,64,512]{2,1,0:T(8,128)S(1)}, f32[8,64,512]{2,1,0:T(8,128)}, u32[]{:S(2)}) copy-start(f32[8,64,512]{2,1,0:T(8,128)} %get-tuple-element.13) | copy-start | bytes 3145732
  79.6 3.4 %copy-start.3 = (f32[8,16,256]{2,1,0:T(8,128)S(1)}, f32[8,16,256]{2,1,0:T(8,128)}, u32[]{:S(2)}) copy-start(f32[8,16,256]{2,1,0:T(8,128)} %get-tuple-element.14) | copy-start | bytes 393220

commit v5 on v4

--- a/solution.py
+++ b/solution.py
@@ -27,19 +27,37 @@
     return lax.ppermute(part, axis, pairs)
 
 
+def corner(part, step_y, step_z):
+    ny, nz = lax.axis_size("gy"), lax.axis_size("gz")
+    pairs = []
+    for gy in range(ny):
+        for gz in range(nz):
+            ty, tz = gy + step_y, gz + step_z
+            if 0 <= ty < ny and 0 <= tz < nz:
+                pairs.append((gy * nz + gz, ty * nz + tz))
+    return lax.ppermute(part, ("gy", "gz"), pairs)
+
+
 def halo_blocks(deformed):
     depth_x, width_y, width_z = deformed.shape
-    low_y = neighbours(deformed[:, width_y - 1 :, :], "gy", True)
-    high_y = neighbours(deformed[:, :1, :], "gy", False)
-    gap_y = jnp.zeros((depth_x, 6, width_z), deformed.dtype)
-    rows = jnp.concatenate([high_y, gap_y, low_y], axis=1)
-    first = jnp.concatenate([deformed[:, :, :1], rows[:, :, :1]], axis=1)
-    last = jnp.concatenate([deformed[:, :, width_z - 1 :], rows[:, :, width_z - 1 :]], axis=1)
-    low_z = neighbours(last, "gz", True)
-    high_z = neighbours(first, "gz", False)
-    gap_z = jnp.zeros((depth_x, first.shape[1], 126), deformed.dtype)
-    columns = jnp.concatenate([high_z, gap_z, low_z], axis=2)
-    return rows.astype(jnp.float32), columns.astype(jnp.float32)
+    f32 = jnp.float32
+    low_y = neighbours(deformed[:, width_y - 1, :], "gy", True)
+    high_y = neighbours(deformed[:, 0, :], "gy", False)
+    low_z = neighbours(deformed[:, :, width_z - 1], "gz", True)
+    high_z = neighbours(deformed[:, :, 0], "gz", False)
+    high_high = corner(deformed[:, 0, 0], -1, -1)
+    high_low = corner(deformed[:, 0, width_z - 1], -1, 1)
+    low_high = corner(deformed[:, width_y - 1, 0], 1, -1)
+    low_low = corner(deformed[:, width_y - 1, width_z - 1], 1, 1)
+    gap_y = jnp.zeros((depth_x, 6, width_z), f32)
+    rows = jnp.concatenate([high_y[:, None].astype(f32), gap_y, low_y[:, None].astype(f32)], axis=1)
+    gap = jnp.zeros((depth_x, 6), deformed.dtype)
+    side_high = jnp.concatenate([high_z, high_high[:, None], gap, low_high[:, None]], axis=1)
+    side_low = jnp.concatenate([low_z, high_low[:, None], gap, low_low[:, None]], axis=1)
+    lanes = lax.broadcasted_iota(jnp.int32, (1, 1, 128), 2)
+    cols = jnp.where(lanes == 0, side_high[:, :, None].astype(f32),
+                     jnp.where(lanes == 127, side_low[:, :, None].astype(f32), 0.0))
+    return rows, cols
 
 
 def lerp(base, other, weight):

time: 121 us -> 143 us (1.18)
  starting transfers between devices: 11.7 us -> 25.3 us
  Pallas kernels: 79.4 us -> 84.8 us
  other arithmetic: 12.2 us -> 14 us
    ppermute x0 -> x4, starting transfers between devices: none -> 12.8 us  [corner(): return lax.ppermute(part, ('gy', 'gz'), pairs)]
    pallas_call x1, Pallas kernels: 26.5 us -> 31.9 us  [both_sums(): pl.pallas_call(functools.partial(both_sums_kernel, nz, ny, plane_row, dep...]
    select_n x0 -> x1, other arithmetic: none -> 2.9 us  [halo_blocks(): jnp.where(lanes == 0, side_high[:, :, None].astype(f32), jnp.where(lanes...]
    convert_element_type x1, other arithmetic: 2.06 us -> 0.09 us  [halo_blocks(): side_high[:, :, None].astype(f32)]
    slice x5 -> x3, local copies, waits for them, and re-layouts: 4.47 us -> 5.8 us  [the longest x1 2.36 us: halo_blocks(): high_high = corner(deformed[:, 0, 0], -1, -1)]
  transfers between devices with their start and end apart: 4 -> 8, of which waited for: 0 -> 0; matrix products, arithmetic and copies ran while one was open for 5% -> 7% of each run, Pallas kernels for 0% -> 0%
where the time goes in v5:
time: 143 us
  Pallas kernels  84.8 us (59%)
  starting transfers between devices  25.3 us (18%)
  local copies, waits for them, and re-layouts  14.2 us (10%)
  other arithmetic  14 us (10%)
  between operations  2.32 us (2%)
  matrix products  1.86 us (1%)
    pallas_call x1, Pallas kernels, strip_sums(): pl.pallas_call(strip_kernel, grid=(nodes,), in_specs=[pl.BlockSpec((1, wi...  53 us
    pallas_call x1, Pallas kernels, both_sums(): pl.pallas_call(functools.partial(both_sums_kernel, nz, ny, plane_row, dep...  31.9 us
    ppermute x4, starting transfers between devices, corner(): return lax.ppermute(part, ('gy', 'gz'), pairs)  12.8 us
    ppermute x4, starting transfers between devices, neighbours(): return lax.ppermute(part, axis, pairs)  12.5 us
    reduce_sum x3, other arithmetic, node_sums(): return field.reshape(nodes, width_y // KNOT, KNOT, width_z).sum(axis=2)  4.49 us
    select_n x1, other arithmetic, halo_blocks(): jnp.where(lanes == 0, side_high[:, :, None].astype(f32), jnp.where(lanes...  2.9 us
  transfers between devices with their start and end apart: 8, of which 0 were waited for; matrix products, arithmetic and copies ran while one was open for 7% of the time, Pallas kernels for 0%

profile of v5, /device:TPU:1, one launch (start us, length us, event | category | flops | bytes accessed | tf_op | source)
XLA Modules:
  0.0 142.5 jit_solution(15435985193167987824)
XLA Ops:
  0.7 2.4 %slice_reduce_fusion.3 = (bf16[64]{0:T(256)(128)(2,1)S(1)}, bf16[64]{0:T(256)(128)(2,1)S(1)}, bf16[64]{0:T(256)(128)(2,1)S(1)}, bf16[64]{0:T(256)(128)(2,1)S(1)}) fusion(bf16[64,64,512]{2,1,0:T(8,128)(2,1)} %next_ref.1), kind=kLoop, calls=%fused_computation.49 | loop fusion | bytes 1024 | tf_op jit(solution)/shard_map/slice | solution.py:48
  3.0 1.3 collective-permute-start.3
  4.3 1.3 collective-permute-start.4
  5.6 4.6 %collective-permute-start.6 = (bf16[64]{0:T(256)(128)(2,1)S(1)}, bf16[64]{0:T(256)(128)(2,1)S(1)}, u32[]{:S(2)}, u32[]{:S(2)}) collective-permute-start(bf16[64]{0:T(256)(128)(2,1)S(1)} %get-tuple-element.28), channel_id=1, source_target_pairs={{8,1},{9,2},{10,3},{11,4},{12,5},{13,6},{14,7},{16,9},{17,10},{18,... | collective-permute-start | bytes 392 | tf_op jit(solution)/shard_map/ppermute | solution.py:38
  10.2 2.0 %fusion.20 = (bf16[64,64,1]{2,1,0:T(8,128)(2,1)S(1)}, bf16[64,64,1]{2,1,0:T(8,128)(2,1)S(1)}) fusion(bf16[64,64,512]{2,1,0:T(8,128)(2,1)} %next_ref.1), kind=kLoop, calls=%fused_computation.65 | loop fusion | bytes 32768 | tf_op jit(solution)/shard_map/slice | solution.py:47
  12.2 0.5 copy.54
  12.7 1.3 collective-permute-start.2
  14.0 0.5 copy.55
  14.5 5.6 %collective-permute-start.5 = (bf16[64,64]{1,0:T(8,128)(2,1)S(1)}, bf16[64,64]{1,0:T(8,128)(2,1)S(1)}, u32[]{:S(2)}, u32[]{:S(2)}) collective-permute-start(bf16[64,64]{1,0:T(8,128)(2,1)S(1)} %bitcast.111), channel_id=1, source_target_pairs={{0,1},{1,2},{2,3},{3,4},{4,5},{5,6},{6,7},{8,9},{9,10},{10,11},{11... | collective-permute-start | bytes 24584 | tf_op jit(solution)/shard_map/ppermute | solution.py:27
  20.1 1.4 fusion.21
  22.1 1.6 %broadcast_bitcast_fusion = (f32[8,64,512]{2,1,0:T(8,128)}, f32[8,64,512]{2,1,0:T(8,128)}) fusion(f32[8,8,512]{2,1,0:T(8,128)S(1)} %get-tuple-element.34, f32[8,8,512]{2,1,0:T(8,128)S(1)} %get-tuple-element.35), kind=kLoop, calls=%fused_computation.10 | loop fusion | bytes 2359296 | tf_op jit(solution)/shard_map/broadcast_in_dim | solution.py:321
  24.1 5.6 %collective-permute-start.7 = (bf16[64]{0:T(256)(128)(2,1)S(1)}, bf16[64]{0:T(256)(128)(2,1)S(1)}, u32[]{:S(2)}, u32[]{:S(2)}) collective-permute-start(bf16[64]{0:T(256)(128)(2,1)S(1)} %get-tuple-element.29), channel_id=1, source_target_pairs={{0,9},{1,10},{2,11},{3,12},{4,13},{5,14},{6,15},{8,17},{9,18},{10,... | collective-permute-start | bytes 392 | tf_op jit(solution)/shard_map/ppermute | solution.py:38
  29.9 1.9 %collective-permute-start = (bf16[64,512]{1,0:T(8,128)(2,1)S(1)}, bf16[64,512]{1,0:T(8,128)(2,1)S(1)}, u32[]{:S(2)}, u32[]{:S(2)}) collective-permute-start(bf16[64,512]{1,0:T(8,128)(2,1)S(1)} %bitcast.108), channel_id=1, source_target_pairs={{8,0},{16,8},{24,16},{32,24},{40,32},{48,40},{56,48},{64,56},{72,6... | collective-permute-start | bytes 196616 | tf_op jit(solution)/shard_map/ppermute | solution.py:27
  32.0 3.6 %collective-permute-start.1 = (bf16[64,512]{1,0:T(8,128)(2,1)S(1)}, bf16[64,512]{1,0:T(8,128)(2,1)S(1)}, u32[]{:S(2)}, u32[]{:S(2)}) collective-permute-start(bf16[64,512]{1,0:T(8,128)(2,1)S(1)} %bitcast.107), channel_id=1, source_target_pairs={{0,8},{8,16},{16,24},{24,32},{32,40},{40,48},{48,56},{56,64},{64,7... | collective-permute-start | bytes 196616 | tf_op jit(solution)/shard_map/ppermute | solution.py:27
  35.9 2.9 %select_select_fusion.cols_ref = f32[64,72,128]{2,1,0:T(8,128)} fusion(f32[64,72]{1,0:T(8,128)S(1)} %get-tuple-element.37, f32[64,72]{1,0:T(8,128)S(1)} %get-tuple-element.36, pred[128]{0:T(512)(128)(4,1)S(1)} %get-tuple-element.38, pred[128]{0:T(512)(128)(4,1)S(1)} %get-tuple-element.39), kind=kLoop, calls=%fused_computation | loop fusion | flops 1179648 | bytes 2396416 | tf_op jit(solution)/shard_map/jit(_where)/select_n | solution.py:58
  39.0 1.2 pad_maximum_fusion.rows_ref
  40.3 53.0 %shard_map.76 = (bf16[64,64,512]{2,1,0:T(8,128)(2,1)}, f32[8,64,512]{2,1,0:T(8,128)}, f32[8,64,512]{2,1,0:T(8,128)}, f32[8,64,512]{2,1,0:T(8,128)}, f32[8,16,256]{2,1,0:T(8,128)}) custom-call(bf16[64,64,512]{2,1,0:T(8,128)(2,1)} %next_ref.1, bf16[64,64,512]{2,1,0:T(8,128)(2,1)} %next_ref.1, bf16[64,64,512]{2,1,0:T(8,128)(2,1)} %next_ref.1, ...), custom_call_target="tpu_custom_call" | custom-call | tf_op jit(solution)/shard_map/pallas_call | solution.py:165
  93.2 1.5 %bitcast_reduce_fusion.1 = f32[8,8,512]{2,1,0:T(8,128)S(1)} fusion(f32[8,64,512]{2,1,0:T(8,128)} %get-tuple-element.12), kind=kLoop, calls=%fused_computation.8 | loop fusion | flops 229376 | bytes 1179648 | tf_op jit(solution)/shard_map/reduce_sum | solution.py:205
  95.3 1.5 %bitcast_reduce_fusion.2 = f32[8,8,512]{2,1,0:T(8,128)S(1)} fusion(f32[8,64,512]{2,1,0:T(8,128)} %get-tuple-element.11), kind=kLoop, calls=%fused_computation.9 | loop fusion | flops 229376 | bytes 1179648 | tf_op jit(solution)/shard_map/reduce_sum | solution.py:205
  97.3 1.5 %bitcast_reduce_fusion = f32[8,8,512]{2,1,0:T(8,128)S(1)} fusion(f32[8,64,512]{2,1,0:T(8,128)} %get-tuple-element.13), kind=kLoop, calls=%fused_computation.7 | loop fusion | flops 229376 | bytes 1179648 | tf_op jit(solution)/shard_map/reduce_sum | solution.py:205
  99.4 0.6 reduce_sum.68
  100.6 0.7 select_maximum_fusion
  101.3 0.8 maximum_maximum_fusion.depth_ref
  102.1 0.7 maximum_maximum_fusion.1.plane_ref
  102.8 31.9 %shard_map.77 = (f32[8,8,128]{2,1,0:T(8,128)}, f32[16,32,128]{2,1,0:T(8,128)}) custom-call(f32[8,8,128]{2,1,0:T(8,128)} %maximum_maximum_fusion.1.plane_ref, f32[16,32,128]{2,1,0:T(8,128)} %maximum_maximum_fusion.depth_ref), custom_call_target="tpu_custom_call" | custom-call | tf_op jit(solution)/shard_map/pallas_call | solution.py:298
  134.7 0.9 slice.111
  135.6 0.7 slice_bitcast_fusion.2
  136.3 1.4 %slice_reduce_fusion.4 = f32[]{:T(128)} fusion(f32[8,8,128]{2,1,0:T(8,128)} %get-tuple-element.15), kind=kLoop, calls=%fused_computation.56 | loop fusion | flops 7 | bytes 36 | tf_op jit(solution)/shard_map/reduce_sum | solution.py:354
  137.8 0.7 slice_bitcast_fusion.3
  138.5 1.0 slice.106
  141.0 0.8 copy.50
  141.8 0.7 fusion.2
  (63 shorter events, 4.1 us)
Async XLA Ops:
  0.6 20.9 %copy-start.1 = (f32[2,32,8,8]{1,3,2,0:T(8,128)S(1)}, f32[2,32,8,8]{1,3,2,0:T(8,128)}, u32[]{:S(2)}) copy-start(f32[2,32,8,8]{1,3,2,0:T(8,128)} %param.8) | copy-start | bytes 49156
  0.6 20.9 %copy-start = (f32[2,32,512]{2,1,0:T(8,128)S(1)}, f32[2,32,512]{2,1,0:T(8,128)}, u32[]{:S(2)}) copy-start(f32[2,32,512]{2,1,0:T(8,128)} %param.9) | copy-start | bytes 393220
  3.0 21.1 %collective-permute-start.3 = (bf16[64]{0:T(256)(128)(2,1)S(1)}, bf16[64]{0:T(256)(128)(2,1)S(1)}, u32[]{:S(2)}, u32[]{:S(2)}) collective-permute-start(bf16[64]{0:T(256)(128)(2,1)S(1)} %get-tuple-element.26), channel_id=1, source_target_pairs={{9,0},{10,1},{11,2},{12,3},{13,4},{14,5},{15,6},{17,8},{18,9},{19,... | collective-permute-start | bytes 392 | tf_op jit(solution)/shard_map/ppermute | solution.py:38
  4.3 25.6 %collective-permute-start.4 = (bf16[64]{0:T(256)(128)(2,1)S(1)}, bf16[64]{0:T(256)(128)(2,1)S(1)}, u32[]{:S(2)}, u32[]{:S(2)}) collective-permute-start(bf16[64]{0:T(256)(128)(2,1)S(1)} %get-tuple-element.27), channel_id=1, source_target_pairs={{1,8},{2,9},{3,10},{4,11},{5,12},{6,13},{7,14},{9,16},{10,17},{11,... | collective-permute-start | bytes 392 | tf_op jit(solution)/shard_map/ppermute | solution.py:38
  5.6 26.3 %collective-permute-start.6 = (bf16[64]{0:T(256)(128)(2,1)S(1)}, bf16[64]{0:T(256)(128)(2,1)S(1)}, u32[]{:S(2)}, u32[]{:S(2)}) collective-permute-start(bf16[64]{0:T(256)(128)(2,1)S(1)} %get-tuple-element.28), channel_id=1, source_target_pairs={{8,1},{9,2},{10,3},{11,4},{12,5},{13,6},{14,7},{16,9},{17,10},{18,... | collective-permute-start | bytes 392 | tf_op jit(solution)/shard_map/ppermute | solution.py:38
  12.7 23.1 %collective-permute-start.2 = (bf16[64,64]{1,0:T(8,128)(2,1)S(1)}, bf16[64,64]{1,0:T(8,128)(2,1)S(1)}, u32[]{:S(2)}, u32[]{:S(2)}) collective-permute-start(bf16[64,64]{1,0:T(8,128)(2,1)S(1)} %bitcast.110), channel_id=1, source_target_pairs={{1,0},{2,1},{3,2},{4,3},{5,4},{6,5},{7,6},{9,8},{10,9},{11,10},{12... | collective-permute-start | bytes 24584 | tf_op jit(solution)/shard_map/ppermute | solution.py:27
  14.5 21.4 %collective-permute-start.5 = (bf16[64,64]{1,0:T(8,128)(2,1)S(1)}, bf16[64,64]{1,0:T(8,128)(2,1)S(1)}, u32[]{:S(2)}, u32[]{:S(2)}) collective-permute-start(bf16[64,64]{1,0:T(8,128)(2,1)S(1)} %bitcast.111), channel_id=1, source_target_pairs={{0,1},{1,2},{2,3},{3,4},{4,5},{5,6},{6,7},{8,9},{9,10},{10,11},{11... | collective-permute-start | bytes 24584 | tf_op jit(solution)/shard_map/ppermute | solution.py:27
  24.1 11.6 %collective-permute-start.7 = (bf16[64]{0:T(256)(128)(2,1)S(1)}, bf16[64]{0:T(256)(128)(2,1)S(1)}, u32[]{:S(2)}, u32[]{:S(2)}) collective-permute-start(bf16[64]{0:T(256)(128)(2,1)S(1)} %get-tuple-element.29), channel_id=1, source_target_pairs={{0,9},{1,10},{2,11},{3,12},{4,13},{5,14},{6,15},{8,17},{9,18},{10,... | collective-permute-start | bytes 392 | tf_op jit(solution)/shard_map/ppermute | solution.py:38
  29.9 8.9 %collective-permute-start = (bf16[64,512]{1,0:T(8,128)(2,1)S(1)}, bf16[64,512]{1,0:T(8,128)(2,1)S(1)}, u32[]{:S(2)}, u32[]{:S(2)}) collective-permute-start(bf16[64,512]{1,0:T(8,128)(2,1)S(1)} %bitcast.108), channel_id=1, source_target_pairs={{8,0},{16,8},{24,16},{32,24},{40,32},{48,40},{56,48},{64,56},{72,6... | collective-permute-start | bytes 196616 | tf_op jit(solution)/shard_map/ppermute | solution.py:27
  32.0 7.0 %collective-permute-start.1 = (bf16[64,512]{1,0:T(8,128)(2,1)S(1)}, bf16[64,512]{1,0:T(8,128)(2,1)S(1)}, u32[]{:S(2)}, u32[]{:S(2)}) collective-permute-start(bf16[64,512]{1,0:T(8,128)(2,1)S(1)} %bitcast.107), channel_id=1, source_target_pairs={{0,8},{8,16},{16,24},{24,32},{32,40},{40,48},{48,56},{56,64},{64,7... | collective-permute-start | bytes 196616 | tf_op jit(solution)/shard_map/ppermute | solution.py:27
  93.2 6.2 %copy-start.2 = (f32[8,16,256]{2,1,0:T(8,128)S(1)}, f32[8,16,256]{2,1,0:T(8,128)}, u32[]{:S(2)}) copy-start(f32[8,16,256]{2,1,0:T(8,128)} %get-tuple-element.14) | copy-start | bytes 393220

commit v6 on v4

--- a/solution.py
+++ b/solution.py
@@ -27,19 +27,91 @@
     return lax.ppermute(part, axis, pairs)
 
 
+def halo_kernel(ny, nz, rows_ref, cols_ref, rows_out, cols_out, rows_got, cols_got,
+                send_sems, recv_sems):
+    my, mz = lax.axis_index("gy"), lax.axis_index("gz")
+    up, down = lax.rem(my + 1, ny), lax.rem(my + ny - 1, ny)
+    right, left = lax.rem(mz + 1, nz), lax.rem(mz + nz - 1, nz)
+    plan = [
+        (rows_ref.at[0], rows_got.at[0], (down, mz)),
+        (rows_ref.at[1], rows_got.at[1], (up, mz)),
+        (cols_ref.at[0], cols_got.at[0], (my, left)),
+        (cols_ref.at[1], cols_got.at[1], (my, right)),
+        (cols_ref.at[0], cols_got.at[2], (down, left)),
+        (cols_ref.at[0], cols_got.at[3], (up, left)),
+        (cols_ref.at[1], cols_got.at[4], (down, right)),
+        (cols_ref.at[1], cols_got.at[5], (up, right)),
+    ]
+    barrier = pltpu.get_barrier_semaphore()
+    for _, _, device in plan:
+        pl.semaphore_signal(barrier, inc=1, device_id=device,
+                            device_id_type=pl.DeviceIdType.MESH)
+    pl.semaphore_wait(barrier, len(plan))
+    copies = []
+    for k, (source, slot, device) in enumerate(plan):
+        copy = pltpu.make_async_remote_copy(
+            src_ref=source, dst_ref=slot, send_sem=send_sems.at[k], recv_sem=recv_sems.at[k],
+            device_id=device, device_id_type=pl.DeviceIdType.MESH)
+        copy.start()
+        copies.append(copy)
+    for copy in copies:
+        copy.wait()
+    rows_out[...] = rows_got[...]
+    cols_out[...] = cols_got[...]
+
+
+def swap_halos(rows_send, cols_send):
+    ny, nz = lax.axis_size("gy"), lax.axis_size("gz")
+    dma = pltpu.SemaphoreType.DMA
+    rows_shape = rows_send.shape
+    cols_shape = (6,) + cols_send.shape[1:]
+    return pl.pallas_call(
+        functools.partial(halo_kernel, ny, nz),
+        out_shape=[jax.ShapeDtypeStruct(rows_shape, rows_send.dtype),
+                   jax.ShapeDtypeStruct(cols_shape, cols_send.dtype)],
+        in_specs=[pl.BlockSpec(memory_space=pltpu.VMEM)] * 2,
+        out_specs=[pl.BlockSpec(memory_space=pltpu.VMEM)] * 2,
+        scratch_shapes=[
+            pltpu.VMEM(rows_shape, rows_send.dtype),
+            pltpu.VMEM(cols_shape, cols_send.dtype),
+            dma((8,)),
+            dma((8,)),
+        ],
+        compiler_params=pltpu.CompilerParams(collective_id=2, has_side_effects=True),
+    )(rows_send, cols_send)
+
+
 def halo_blocks(deformed):
     depth_x, width_y, width_z = deformed.shape
-    low_y = neighbours(deformed[:, width_y - 1 :, :], "gy", True)
-    high_y = neighbours(deformed[:, :1, :], "gy", False)
-    gap_y = jnp.zeros((depth_x, 6, width_z), deformed.dtype)
-    rows = jnp.concatenate([high_y, gap_y, low_y], axis=1)
-    first = jnp.concatenate([deformed[:, :, :1], rows[:, :, :1]], axis=1)
-    last = jnp.concatenate([deformed[:, :, width_z - 1 :], rows[:, :, width_z - 1 :]], axis=1)
-    low_z = neighbours(last, "gz", True)
-    high_z = neighbours(first, "gz", False)
-    gap_z = jnp.zeros((depth_x, first.shape[1], 126), deformed.dtype)
-    columns = jnp.concatenate([high_z, gap_z, low_z], axis=2)
-    return rows.astype(jnp.float32), columns.astype(jnp.float32)
+    f32 = jnp.float32
+    ny, nz = lax.axis_size("gy"), lax.axis_size("gz")
+    my, mz = lax.axis_index("gy"), lax.axis_index("gz")
+    rows_send = jnp.stack([deformed[:, 0, :], deformed[:, width_y - 1, :]])
+    cols_send = jnp.stack([deformed[:, :, 0], deformed[:, :, width_z - 1]])
+    rows_got, cols_got = swap_halos(rows_send, cols_send)
+    has_up = (my < ny - 1).astype(f32)
+    has_down = (my > 0).astype(f32)
+    has_right = (mz < nz - 1).astype(f32)
+    has_left = (mz > 0).astype(f32)
+    rows_got = rows_got.astype(f32)
+    cols_got = cols_got.astype(f32)
+    high_y = rows_got[0] * has_up
+    low_y = rows_got[1] * has_down
+    high_z = cols_got[0] * has_right
+    low_z = cols_got[1] * has_left
+    high_high = cols_got[2][:, 0] * (has_up * has_right)
+    low_high = cols_got[3][:, width_y - 1] * (has_down * has_right)
+    high_low = cols_got[4][:, 0] * (has_up * has_left)
+    low_low = cols_got[5][:, width_y - 1] * (has_down * has_left)
+    gap_y = jnp.zeros((depth_x, 6, width_z), f32)
+    rows = jnp.concatenate([high_y[:, None], gap_y, low_y[:, None]], axis=1)
+    gap = jnp.zeros((depth_x, 6), f32)
+    side_high = jnp.concatenate([high_z, high_high[:, None], gap, low_high[:, None]], axis=1)
+    side_low = jnp.concatenate([low_z, high_low[:, None], gap, low_low[:, None]], axis=1)
+    lanes = lax.broadcasted_iota(jnp.int32, (1, 1, 128), 2)
+    cols = jnp.where(lanes == 0, side_high[:, :, None],
+                     jnp.where(lanes == 127, side_low[:, :, None], 0.0))
+    return rows, cols
 
 
 def lerp(base, other, weight):

time: 121 us -> 120 us (level)
  starting transfers between devices: 11.7 us -> 0 us
  Pallas kernels: 79.4 us -> 86.6 us
  other arithmetic: 12.2 us -> 17.6 us
  local copies, waits for them, and re-layouts: 13.4 us -> 11.2 us
    pallas_call x0 -> x1, Pallas kernels: none -> 13.9 us  [swap_halos(): pl.pallas_call(functools.partial(halo_kernel, ny, nz), out_shape=[jax.Sha...]
    ppermute x4 -> x0, starting transfers between devices: 11.7 us -> none  [neighbours(): return lax.ppermute(part, axis, pairs)]
    pallas_call x1, Pallas kernels: 26.5 us -> 19.7 us  [both_sums(): pl.pallas_call(functools.partial(both_sums_kernel, nz, ny, plane_row, dep...]
    select_n x0 -> x1, other arithmetic: none -> 2.9 us  [halo_blocks(): jnp.where(lanes == 0, side_high[:, :, None], jnp.where(lanes == 127, side...]
    another operation x0 -> x2, other arithmetic: none -> 1.3 us  [the longest x1 0.67 us: halo_blocks(): rows_send = jnp.stack([deformed[:, 0, :], deformed[:, width_y - 1, :]])]
    slice x5 -> x2, local copies, waits for them, and re-layouts: 4.47 us -> 3.44 us  [the longest x1 2.02 us: halo_blocks(): cols_send = jnp.stack([deformed[:, :, 0], deformed[:, :, width_z - 1]])]
  transfers between devices with their start and end apart: 4 -> 0, of which waited for: 0 -> 0; matrix products, arithmetic and copies ran while one was open for 5% -> 0% of each run, Pallas kernels for 0% -> 0%
where the time goes in v6:
time: 120 us
  Pallas kernels  86.6 us (72%)
  other arithmetic  17.6 us (15%)
  local copies, waits for them, and re-layouts  11.2 us (9%)
  between operations  2.3 us (2%)
  matrix products  1.86 us (2%)
    pallas_call x1, Pallas kernels, strip_sums(): pl.pallas_call(strip_kernel, grid=(nodes,), in_specs=[pl.BlockSpec((1, wi...  53 us
    pallas_call x1, Pallas kernels, both_sums(): pl.pallas_call(functools.partial(both_sums_kernel, nz, ny, plane_row, dep...  19.7 us
    pallas_call x1, Pallas kernels, swap_halos(): pl.pallas_call(functools.partial(halo_kernel, ny, nz), out_shape=[jax.Sha...  13.9 us
    reduce_sum x3, other arithmetic, node_sums(): return field.reshape(nodes, width_y // KNOT, KNOT, width_z).sum(axis=2)  4.49 us
    select_n x1, other arithmetic, halo_blocks(): jnp.where(lanes == 0, side_high[:, :, None], jnp.where(lanes == 127, side...  2.9 us

profile of v6, /device:TPU:1, one launch (start us, length us, event | category | flops | bytes accessed | tf_op | source)
XLA Modules:
  0.0 119.7 jit_solution(8461372681105869511)
XLA Ops:
  0.6 1.4 %fusion.25 = (bf16[64,1,512]{2,1,0:T(2,128)(2,1)S(1)}, bf16[64,1,512]{2,1,0:T(2,128)(2,1)S(1)}) fusion(bf16[64,64,512]{2,1,0:T(8,128)(2,1)} %next_ref.1), kind=kLoop, calls=%fused_computation.81 | loop fusion | bytes 262144 | tf_op jit(solution)/shard_map/slice | solution.py:89
  2.1 0.7 pad_maximum_fusion.2.rows_ref
  2.7 2.0 %fusion.24 = (bf16[64,64,1]{2,1,0:T(8,128)(2,1)S(1)}, bf16[64,64,1]{2,1,0:T(8,128)(2,1)S(1)}) fusion(bf16[64,64,512]{2,1,0:T(8,128)(2,1)} %next_ref.1), kind=kLoop, calls=%fused_computation.80 | loop fusion | bytes 32768 | tf_op jit(solution)/shard_map/slice | solution.py:90
  4.8 0.5 copy.44
  5.3 0.5 copy.45
  5.7 0.6 pad_maximum_fusion.3.cols_ref
  6.4 13.9 %shard_map.76 = (bf16[2,64,512]{2,1,0:T(8,128)(2,1)}, bf16[6,64,64]{2,1,0:T(8,128)(2,1)}) custom-call(bf16[2,64,512]{2,1,0:T(8,128)(2,1)} %pad_maximum_fusion.2.rows_ref, bf16[2,64,64]{2,1,0:T(8,128)(2,1)} %pad_maximum_fusion.3.cols_ref), custom_call_target="tpu_custom_call" | custom-call | tf_op jit(solution)/shard_map/pallas_call | solution.py:68
  20.3 0.9 convert_element_type.24
  21.6 2.9 %select_select_fusion.cols_ref = f32[64,72,128]{2,1,0:T(8,128)} fusion(f32[64,72]{1,0:T(8,128)S(1)} %get-tuple-element.45, f32[64,72]{1,0:T(8,128)S(1)} %get-tuple-element.44, pred[128]{0:T(512)(128)(4,1)S(1)} %get-tuple-element.48, pred[128]{0:T(512)(128)(4,1)S(1)} %get-tuple-element.49), kind=kLoop, calls=%fused_computation | loop fusion | flops 1179648 | bytes 2396416 | tf_op jit(solution)/shard_map/jit(_where)/select_n | solution.py:112
  24.5 1.0 copy_convert_fusion
  25.8 1.2 %pad_maximum_fusion.rows_ref = f32[64,8,512]{2,1,0:T(8,128)} fusion(f32[64,1,512]{2,1,0:T(1,128)S(1)} %get-tuple-element.37, f32[64,1,512]{2,1,0:T(1,128)S(1)} %get-tuple-element.36, f32[8]{0:T(128)S(1)} %pad.40.clone), kind=kLoop, calls=%fused_computation.6 | loop fusion | flops 524288 | bytes 1310752 | tf_op jit(solution)/shard_map/concatenate | solution.py:107
  27.1 0.3 fusion.6
  27.5 1.6 %broadcast_bitcast_fusion = (f32[8,64,512]{2,1,0:T(8,128)}, f32[8,64,512]{2,1,0:T(8,128)}) fusion(f32[8,8,512]{2,1,0:T(8,128)S(1)} %get-tuple-element.34, f32[8,8,512]{2,1,0:T(8,128)S(1)} %get-tuple-element.35), kind=kLoop, calls=%fused_computation.10 | loop fusion | bytes 2359296 | tf_op jit(solution)/shard_map/broadcast_in_dim | solution.py:375
  29.1 53.0 %shard_map.77 = (bf16[64,64,512]{2,1,0:T(8,128)(2,1)}, f32[8,64,512]{2,1,0:T(8,128)}, f32[8,64,512]{2,1,0:T(8,128)}, f32[8,64,512]{2,1,0:T(8,128)}, f32[8,16,256]{2,1,0:T(8,128)}) custom-call(bf16[64,64,512]{2,1,0:T(8,128)(2,1)} %next_ref.1, bf16[64,64,512]{2,1,0:T(8,128)(2,1)} %next_ref.1, bf16[64,64,512]{2,1,0:T(8,128)(2,1)} %next_ref.1, ...), custom_call_target="tpu_custom_call" | custom-call | tf_op jit(solution)/shard_map/pallas_call | solution.py:219
  82.1 1.5 %bitcast_reduce_fusion.1 = f32[8,8,512]{2,1,0:T(8,128)S(1)} fusion(f32[8,64,512]{2,1,0:T(8,128)} %get-tuple-element.16), kind=kLoop, calls=%fused_computation.8 | loop fusion | flops 229376 | bytes 1179648 | tf_op jit(solution)/shard_map/reduce_sum | solution.py:259
  83.6 0.3 convolution_bitcast_fusion.1
  83.9 1.5 %bitcast_reduce_fusion.2 = f32[8,8,512]{2,1,0:T(8,128)S(1)} fusion(f32[8,64,512]{2,1,0:T(8,128)} %get-tuple-element.15), kind=kLoop, calls=%fused_computation.9 | loop fusion | flops 229376 | bytes 1179648 | tf_op jit(solution)/shard_map/reduce_sum | solution.py:259
  85.7 1.5 %bitcast_reduce_fusion = f32[8,8,512]{2,1,0:T(8,128)S(1)} fusion(f32[8,64,512]{2,1,0:T(8,128)} %get-tuple-element.17), kind=kLoop, calls=%fused_computation.7 | loop fusion | flops 229376 | bytes 1179648 | tf_op jit(solution)/shard_map/reduce_sum | solution.py:259
  87.2 0.3 convolution_bitcast_fusion
  87.5 0.6 reduce_sum.68
  88.1 0.7 select_maximum_fusion
  89.0 0.8 maximum_maximum_fusion.depth_ref
  90.6 0.3 fusion.8
  91.4 0.7 maximum_maximum_fusion.1.plane_ref
  92.1 19.7 %shard_map.78 = (f32[8,8,128]{2,1,0:T(8,128)}, f32[16,32,128]{2,1,0:T(8,128)}) custom-call(f32[8,8,128]{2,1,0:T(8,128)} %maximum_maximum_fusion.1.plane_ref, f32[16,32,128]{2,1,0:T(8,128)} %maximum_maximum_fusion.depth_ref), custom_call_target="tpu_custom_call" | custom-call | tf_op jit(solution)/shard_map/pallas_call | solution.py:352
  111.8 0.9 slice.143
  112.8 0.7 slice_bitcast_fusion.6
  113.6 1.4 %slice_reduce_fusion = f32[]{:T(128)} fusion(f32[8,8,128]{2,1,0:T(8,128)} %get-tuple-element.19), kind=kLoop, calls=%fused_computation.71 | loop fusion | flops 7 | bytes 36 | tf_op jit(solution)/shard_map/reduce_sum | solution.py:408
  115.7 0.7 fusion.2
  116.4 1.0 slice.138
  117.4 0.7 slice_bitcast_fusion.7
  118.9 0.8 copy.40
  (49 shorter events, 2.7 us)
Async XLA Ops:
  4.8 22.3 %copy-start = (f32[2,32,512]{2,1,0:T(8,128)S(1)}, f32[2,32,512]{2,1,0:T(8,128)}, u32[]{:S(2)}) copy-start(f32[2,32,512]{2,1,0:T(8,128)} %param.9) | copy-start | bytes 393220
  4.8 22.3 %copy-start.1 = (f32[2,32,8,8]{1,3,2,0:T(8,128)S(1)}, f32[2,32,8,8]{1,3,2,0:T(8,128)}, u32[]{:S(2)}) copy-start(f32[2,32,8,8]{1,3,2,0:T(8,128)} %param.8) | copy-start | bytes 49156
  82.1 5.4 %copy-start.2 = (f32[8,16,256]{2,1,0:T(8,128)S(1)}, f32[8,16,256]{2,1,0:T(8,128)}, u32[]{:S(2)}) copy-start(f32[8,16,256]{2,1,0:T(8,128)} %get-tuple-element.18) | copy-start | bytes 393220

commit v7 on v6

--- a/solution.py
+++ b/solution.py
@@ -103,36 +103,39 @@
     low_high = cols_got[3][:, width_y - 1] * (has_down * has_right)
     high_low = cols_got[4][:, 0] * (has_up * has_left)
     low_low = cols_got[5][:, width_y - 1] * (has_down * has_left)
-    gap_y = jnp.zeros((depth_x, 6, width_z), f32)
-    rows = jnp.concatenate([high_y[:, None], gap_y, low_y[:, None]], axis=1)
+    rows = jnp.stack([high_y, low_y])
     gap = jnp.zeros((depth_x, 6), f32)
     side_high = jnp.concatenate([high_z, high_high[:, None], gap, low_high[:, None]], axis=1)
     side_low = jnp.concatenate([low_z, high_low[:, None], gap, low_low[:, None]], axis=1)
-    lanes = lax.broadcasted_iota(jnp.int32, (1, 1, 128), 2)
-    cols = jnp.where(lanes == 0, side_high[:, :, None],
-                     jnp.where(lanes == 127, side_low[:, :, None], 0.0))
-    return rows, cols
+    sides = jnp.stack([side_high.T, side_low.T])
+    sides = jnp.pad(sides, ((0, 0), (0, 0), (0, 128 - depth_x)))
+    return rows, sides
 
 
 def lerp(base, other, weight):
     return base + weight * (other - base)
 
 
-def strip_kernel(prev_ref, main_ref, next_ref, rows_ref, cols_ref, disp_ref, image_ref,
-                 contrast_ref, bright_ref,
+def strip_kernel(prev_ref, main_ref, next_ref, rows_ref, sides_ref, disp_ref, image_ref,
+                 fields_ref,
                  res_ref, prod_ref, mis_ref, sq_ref, energy_ref, pad_ref, shifts_ref):
     block = pl.program_id(0)
-    depth_x = rows_ref.shape[0]
+    depth_x = rows_ref.shape[1]
     width_y, width_z = image_ref.shape[1], image_ref.shape[2]
     pad_y, pad_z = pad_ref.shape
+    pad_ref[width_y:, :width_z] = jnp.zeros((pad_y - width_y, width_z), jnp.float32)
+    lane = lax.broadcasted_iota(jnp.int32, (pad_y, pad_z - width_z), 1)
 
     def source_plane(p, plane):
         plane_x = block * KNOT - 1 + p
         valid = jnp.logical_and(plane_x >= 0, plane_x < depth_x)
         safe = jnp.clip(plane_x, 0, depth_x - 1)
         pad_ref[:width_y, :width_z] = plane.astype(jnp.float32)
-        pad_ref[width_y:, :width_z] = rows_ref[safe]
-        pad_ref[:, width_z:] = cols_ref[safe]
+        pad_ref[pl.ds(width_y, 1), :width_z] = rows_ref[0, pl.ds(safe, 1), :]
+        pad_ref[pl.ds(pad_y - 1, 1), :width_z] = rows_ref[1, pl.ds(safe, 1), :]
+        high = jnp.sum(jnp.where(lane == safe, sides_ref[0], 0.0), axis=1, keepdims=True)
+        low = jnp.sum(jnp.where(lane == safe, sides_ref[1], 0.0), axis=1, keepdims=True)
+        pad_ref[:, width_z:] = jnp.where(lane == 0, high, jnp.where(lane == pad_z - width_z - 1, low, 0.0))
         whole = jnp.where(valid, pad_ref[...], 0.0)
         by_y = (pltpu.roll(whole, 1, 0), whole, pltpu.roll(whole, pad_y - 1, 0))
         for b in range(3):
@@ -158,8 +161,15 @@
         c0 = pl.multiple_of((k % chunks_z) * LANES, LANES)
         rs = pl.ds(r0, ROWS)
         cs = pl.ds(c0, LANES)
-        contrast = contrast_ref[0, rs, cs]
-        bright = bright_ref[0, rs, cs]
+        j0 = r0 // KNOT
+        upper = lax.broadcasted_iota(jnp.int32, (ROWS, LANES), 0) < KNOT
+        node = lax.broadcasted_iota(jnp.int32, (KNOT, LANES), 0)
+
+        def node_row(k, j):
+            return jnp.sum(jnp.where(node == j, fields_ref[k, 0, :, cs], 0.0), axis=0, keepdims=True)
+
+        contrast = jnp.where(upper, node_row(0, j0), node_row(0, j0 + 1))
+        bright = jnp.where(upper, node_row(1, j0), node_row(1, j0 + 1))
 
         def plane(xl, acc):
             prod_acc, mis_acc, sq_acc, e_acc = acc
@@ -209,7 +219,7 @@
     energy_ref[0] = energy
 
 
-def strip_sums(deformed, rows, cols, displacement, image, contrast_y, bright_y):
+def strip_sums(deformed, rows, sides, displacement, image, fields):
     depth_x, width_y, width_z = image.shape
     nodes = depth_x // KNOT
     f32 = jnp.float32
@@ -228,8 +238,7 @@
             pl.BlockSpec(memory_space=pltpu.VMEM),
             pl.BlockSpec((3, KNOT, width_y, width_z), lambda i: (0, i, 0, 0)),
             plane_spec,
-            node_spec,
-            node_spec,
+            pl.BlockSpec((2, 1) + fields.shape[2:], lambda i: (0, i, 0, 0)),
         ],
         out_specs=[
             plane_spec,
@@ -246,12 +255,12 @@
             jax.ShapeDtypeStruct((nodes, ROWS, LANES), f32),
         ],
         scratch_shapes=[
-            pltpu.VMEM((width_y + rows.shape[1], width_z + cols.shape[2]), f32),
+            pltpu.VMEM((sides.shape[1], width_z + 128), f32),
             pltpu.VMEM((KNOT + 2, 9, width_y, width_z), f32),
         ],
         compiler_params=pltpu.CompilerParams(
             dimension_semantics=("arbitrary",), vmem_limit_bytes=60 * 1024 * 1024),
-    )(deformed, deformed, deformed, rows, cols, displacement, image, contrast_y, bright_y)
+    )(deformed, deformed, deformed, rows, sides, displacement, image, fields)
 
 
 def node_sums(field):
@@ -370,11 +379,10 @@
 
 
 def local(reference_image, deformed, displacement, plane_factors, depth_factors):
-    rows, cols = halo_blocks(deformed)
+    rows, sides = halo_blocks(deformed)
     fields = jnp.einsum("krij,krz->kijz", plane_factors, depth_factors, precision=highest)
-    fields = jnp.repeat(fields, KNOT, axis=2)
     residual, prod, mis, sq, energy_parts = strip_sums(
-        deformed, rows, cols, displacement, reference_image, fields[0], fields[1])
+        deformed, rows, sides, displacement, reference_image, fields)
     prod, mis, sq = node_sums(prod), node_sums(mis), node_sums(sq)
     local_energy = jnp.sum(energy_parts)
 

time: 120 us -> 120 us (level)
  Pallas kernels: 86.6 us -> 90.7 us
  other arithmetic: 17.6 us -> 13.5 us
    pallas_call x1, Pallas kernels: 53 us -> 57.1 us  [strip_sums(): pl.pallas_call(strip_kernel, grid=(nodes,), in_specs=[pl.BlockSpec((1, wi...]
    select_n x1 -> x0, other arithmetic: 2.9 us -> none  [halo_blocks(): jnp.where(lanes == 0, side_high[:, :, None], jnp.where(lanes == 127, side...]
    broadcast_in_dim x2 -> x1, local copies, waits for them, and re-layouts: 1.63 us -> 0.01 us  [halo_blocks(): gap = jnp.zeros((depth_x, 6), f32)]
    another operation x0 -> x3, other arithmetic: none -> 1.46 us  [the longest x1 0.74 us: halo_blocks(): rows = jnp.stack([high_y, low_y])]
    concatenate x2 -> x0, other arithmetic: 1.34 us -> none  [the longest x1 1.24 us: halo_blocks(): rows = jnp.concatenate([high_y[:, None], gap_y, low_y[:, None]], axis=1)]
where the time goes in v7:
time: 120 us
  Pallas kernels  90.7 us (76%)
  other arithmetic  13.5 us (11%)
  local copies, waits for them, and re-layouts  10.6 us (9%)
  matrix products  2.59 us (2%)
  between operations  2.3 us (2%)
    pallas_call x1, Pallas kernels, strip_sums(): pl.pallas_call(strip_kernel, grid=(nodes,), in_specs=[pl.BlockSpec((1, wi...  57.1 us
    pallas_call x1, Pallas kernels, both_sums(): pl.pallas_call(functools.partial(both_sums_kernel, nz, ny, plane_row, dep...  19.7 us
    pallas_call x1, Pallas kernels, swap_halos(): pl.pallas_call(functools.partial(halo_kernel, ny, nz), out_shape=[jax.Sha...  13.9 us
    reduce_sum x3, other arithmetic, node_sums(): return field.reshape(nodes, width_y // KNOT, KNOT, width_z).sum(axis=2)  4.49 us

profile of v7, /device:TPU:1, one launch (start us, length us, event | category | flops | bytes accessed | tf_op | source)
XLA Modules:
  0.0 119.7 jit_solution(10002242879525895324)
XLA Ops:
  0.6 1.4 %fusion.23 = (bf16[64,1,512]{2,1,0:T(2,128)(2,1)S(1)}, bf16[64,1,512]{2,1,0:T(2,128)(2,1)S(1)}) fusion(bf16[64,64,512]{2,1,0:T(8,128)(2,1)} %next_ref.1), kind=kLoop, calls=%fused_computation.73 | loop fusion | bytes 262144 | tf_op jit(solution)/shard_map/slice | solution.py:89
  2.1 0.7 pad_maximum_fusion.2.rows_ref
  2.7 2.1 %fusion.22 = (bf16[64,64,1]{2,1,0:T(8,128)(2,1)S(1)}, bf16[64,64,1]{2,1,0:T(8,128)(2,1)S(1)}) fusion(bf16[64,64,512]{2,1,0:T(8,128)(2,1)} %next_ref.1), kind=kLoop, calls=%fused_computation.72 | loop fusion | bytes 32768 | tf_op jit(solution)/shard_map/slice | solution.py:90
  4.8 0.5 copy.44
  5.3 0.5 copy.45
  5.8 0.6 pad_maximum_fusion.3.cols_ref
  6.4 13.9 %shard_map.76 = (bf16[2,64,512]{2,1,0:T(8,128)(2,1)}, bf16[6,64,64]{2,1,0:T(8,128)(2,1)}) custom-call(bf16[2,64,512]{2,1,0:T(8,128)(2,1)} %pad_maximum_fusion.2.rows_ref, bf16[2,64,64]{2,1,0:T(8,128)(2,1)} %pad_maximum_fusion.3.cols_ref), custom_call_target="tpu_custom_call" | custom-call | tf_op jit(solution)/shard_map/pallas_call | solution.py:68
  20.3 1.0 copy.37
  21.6 0.6 select_maximum_fusion.sides_ref
  22.3 0.9 convert_element_type.23
  23.2 0.7 pad_maximum_fusion.rows_ref
  24.0 1.1 fusion.4.fields_ref
  25.0 57.1 %shard_map.77 = (bf16[64,64,512]{2,1,0:T(8,128)(2,1)}, f32[8,64,512]{2,1,0:T(8,128)}, f32[8,64,512]{2,1,0:T(8,128)}, f32[8,64,512]{2,1,0:T(8,128)}, f32[8,16,256]{2,1,0:T(8,128)}) custom-call(bf16[64,64,512]{2,1,0:T(8,128)(2,1)} %next_ref.1, bf16[64,64,512]{2,1,0:T(8,128)(2,1)} %next_ref.1, bf16[64,64,512]{2,1,0:T(8,128)(2,1)} %next_ref.1, ...), custom_call_target="tpu_custom_call" | custom-call | tf_op jit(solution)/shard_map/pallas_call | solution.py:229
  82.1 1.5 %bitcast_reduce_fusion.1 = f32[8,8,512]{2,1,0:T(8,128)S(1)} fusion(f32[8,64,512]{2,1,0:T(8,128)} %get-tuple-element.16), kind=kLoop, calls=%fused_computation.6 | loop fusion | flops 229376 | bytes 1179648 | tf_op jit(solution)/shard_map/reduce_sum | solution.py:268
  83.6 0.3 convolution_bitcast_fusion.1
  83.9 1.5 %bitcast_reduce_fusion.2 = f32[8,8,512]{2,1,0:T(8,128)S(1)} fusion(f32[8,64,512]{2,1,0:T(8,128)} %get-tuple-element.15), kind=kLoop, calls=%fused_computation.7 | loop fusion | flops 229376 | bytes 1179648 | tf_op jit(solution)/shard_map/reduce_sum | solution.py:268
  85.4 0.3 convolution_bitcast_fusion.2
  85.7 1.5 %bitcast_reduce_fusion = f32[8,8,512]{2,1,0:T(8,128)S(1)} fusion(f32[8,64,512]{2,1,0:T(8,128)} %get-tuple-element.17), kind=kLoop, calls=%fused_computation.5 | loop fusion | flops 229376 | bytes 1179648 | tf_op jit(solution)/shard_map/reduce_sum | solution.py:268
  87.2 0.3 convolution_bitcast_fusion
  87.5 0.6 reduce_sum.68
  88.2 0.7 select_maximum_fusion.1
  89.0 0.8 maximum_maximum_fusion.depth_ref
  90.6 0.3 fusion.6
  91.4 0.7 maximum_maximum_fusion.1.plane_ref
  92.1 19.7 %shard_map.78 = (f32[8,8,128]{2,1,0:T(8,128)}, f32[16,32,128]{2,1,0:T(8,128)}) custom-call(f32[8,8,128]{2,1,0:T(8,128)} %maximum_maximum_fusion.1.plane_ref, f32[16,32,128]{2,1,0:T(8,128)} %maximum_maximum_fusion.depth_ref), custom_call_target="tpu_custom_call" | custom-call | tf_op jit(solution)/shard_map/pallas_call | solution.py:361
  111.9 0.9 slice.125
  112.9 0.7 slice_bitcast_fusion.4
  113.6 1.4 %slice_reduce_fusion = f32[]{:T(128)} fusion(f32[8,8,128]{2,1,0:T(8,128)} %get-tuple-element.19), kind=kLoop, calls=%fused_computation.61 | loop fusion | flops 7 | bytes 36 | tf_op jit(solution)/shard_map/reduce_sum | solution.py:416
  115.7 0.7 fusion.2
  116.4 1.0 slice.120
  117.4 0.7 slice_bitcast_fusion.5
  118.9 0.8 copy.40
  (46 shorter events, 2.1 us)
Async XLA Ops:
  2.7 21.2 %copy-start = (f32[2,32,512]{2,1,0:T(8,128)S(1)}, f32[2,32,512]{2,1,0:T(8,128)}, u32[]{:S(2)}) copy-start(f32[2,32,512]{2,1,0:T(8,128)} %param.9) | copy-start | bytes 393220
  2.7 21.2 %copy-start.1 = (f32[2,32,8,8]{1,3,2,0:T(8,128)S(1)}, f32[2,32,8,8]{1,3,2,0:T(8,128)}, u32[]{:S(2)}) copy-start(f32[2,32,8,8]{1,3,2,0:T(8,128)} %param.8) | copy-start | bytes 49156
  82.1 5.4 %copy-start.2 = (f32[8,16,256]{2,1,0:T(8,128)S(1)}, f32[8,16,256]{2,1,0:T(8,128)}, u32[]{:S(2)}) copy-start(f32[8,16,256]{2,1,0:T(8,128)} %get-tuple-element.18) | copy-start | bytes 393220

commit v8 on v7

--- a/solution.py
+++ b/solution.py
@@ -118,31 +118,60 @@
 
 def strip_kernel(prev_ref, main_ref, next_ref, rows_ref, sides_ref, disp_ref, image_ref,
                  fields_ref,
-                 res_ref, prod_ref, mis_ref, sq_ref, energy_ref, pad_ref, shifts_ref):
+                 res_ref, prod_ref, mis_ref, sq_ref, energy_ref, pad_ref, edge_ref, shifts_ref):
     block = pl.program_id(0)
     depth_x = rows_ref.shape[1]
     width_y, width_z = image_ref.shape[1], image_ref.shape[2]
-    pad_y, pad_z = pad_ref.shape
-    pad_ref[width_y:, :width_z] = jnp.zeros((pad_y - width_y, width_z), jnp.float32)
-    lane = lax.broadcasted_iota(jnp.int32, (pad_y, pad_z - width_z), 1)
+    pad_y, pad_z = pad_ref.shape[1], pad_ref.shape[2]
+    side = pad_z - width_z
+    blocks = pad_z // 128
+    half = width_y // 2
+    f32 = jnp.float32
+    pad_ref[:, width_y:, :width_z] = jnp.zeros((pad_ref.shape[0], pad_y - width_y, width_z), f32)
+    lane = lax.broadcasted_iota(jnp.int32, (pad_y, side), 1)
+    lane_block = lax.broadcasted_iota(jnp.int32, (half, 128), 1)
 
     def source_plane(p, plane):
         plane_x = block * KNOT - 1 + p
         valid = jnp.logical_and(plane_x >= 0, plane_x < depth_x)
         safe = jnp.clip(plane_x, 0, depth_x - 1)
-        pad_ref[:width_y, :width_z] = plane.astype(jnp.float32)
-        pad_ref[pl.ds(width_y, 1), :width_z] = rows_ref[0, pl.ds(safe, 1), :]
-        pad_ref[pl.ds(pad_y - 1, 1), :width_z] = rows_ref[1, pl.ds(safe, 1), :]
+        held = pad_ref.at[p]
+        held[:width_y, :width_z] = jnp.where(valid, plane.astype(f32), 0.0)
+        held[pl.ds(width_y, 1), :width_z] = jnp.where(valid, rows_ref[0, pl.ds(safe, 1), :], 0.0)
+        held[pl.ds(pad_y - 1, 1), :width_z] = jnp.where(valid, rows_ref[1, pl.ds(safe, 1), :], 0.0)
         high = jnp.sum(jnp.where(lane == safe, sides_ref[0], 0.0), axis=1, keepdims=True)
         low = jnp.sum(jnp.where(lane == safe, sides_ref[1], 0.0), axis=1, keepdims=True)
-        pad_ref[:, width_z:] = jnp.where(lane == 0, high, jnp.where(lane == pad_z - width_z - 1, low, 0.0))
-        whole = jnp.where(valid, pad_ref[...], 0.0)
-        by_y = (pltpu.roll(whole, 1, 0), whole, pltpu.roll(whole, pad_y - 1, 0))
+        column = jnp.where(lane == 0, high, jnp.where(lane == side - 1, low, 0.0))
+        held[:, width_z:] = jnp.where(valid, column, 0.0)
+        for k in range(blocks):
+            lanes = slice(128 * k, 128 * k + 128)
+            col = held[:, lanes]
+            for b, shift in ((0, 1), (2, pad_y - 1)):
+                moved = pltpu.roll(col, shift, 0)[:width_y]
+                if k < blocks - 1:
+                    shifts_ref[p, 3 * b + 1, :, lanes] = moved
+                else:
+                    edge_ref[b // 2] = moved
         for b in range(3):
-            part = by_y[b][:width_y]
-            by_z = (pltpu.roll(part, 1, 1), part, pltpu.roll(part, pad_z - 1, 1))
-            for c in range(3):
-                shifts_ref[p, 3 * b + c] = by_z[c][:, :width_z]
+            def piece(k, h):
+                rows = slice(half * h, half * h + half)
+                if b == 1:
+                    return held[rows, 128 * k : 128 * k + 128]
+                if k == blocks - 1:
+                    return edge_ref[b // 2, rows, :]
+                return shifts_ref[p, 3 * b + 1, rows, 128 * k : 128 * k + 128]
+
+            for k in range(blocks - 1):
+                for h in range(2):
+                    rows = slice(half * h, half * h + half)
+                    lanes = slice(128 * k, 128 * k + 128)
+                    centre = piece(k, h)
+                    before = piece(k - 1 if k > 0 else blocks - 1, h)
+                    after = piece(k + 1, h)
+                    shifts_ref[p, 3 * b, rows, lanes] = jnp.where(
+                        lane_block == 0, pltpu.roll(before, 1, 1), pltpu.roll(centre, 1, 1))
+                    shifts_ref[p, 3 * b + 2, rows, lanes] = jnp.where(
+                        lane_block == 127, pltpu.roll(after, 127, 1), pltpu.roll(centre, 127, 1))
 
     source_plane(0, prev_ref[0])
 
@@ -175,6 +204,8 @@
             prod_acc, mis_acc, sq_acc, e_acc = acc
 
             def src(a, b, c):
+                if b == 0 and c == 0:
+                    return pad_ref[xl + 1 + a, rs, cs]
                 return shifts_ref[xl + 1 + a, 3 * (b + 1) + (c + 1), rs, cs]
 
             sx = disp_ref[0, xl, rs, cs].astype(jnp.float32)
@@ -255,7 +286,8 @@
             jax.ShapeDtypeStruct((nodes, ROWS, LANES), f32),
         ],
         scratch_shapes=[
-            pltpu.VMEM((sides.shape[1], width_z + 128), f32),
+            pltpu.VMEM((KNOT + 2, sides.shape[1], width_z + 128), f32),
+            pltpu.VMEM((2, width_y, 128), f32),
             pltpu.VMEM((KNOT + 2, 9, width_y, width_z), f32),
         ],
         compiler_params=pltpu.CompilerParams(

time: 120 us -> 126 us (1.050)
  Pallas kernels: 90.7 us -> 96.2 us
    pallas_call x1, Pallas kernels: 57.1 us -> 62.6 us  [strip_sums(): pl.pallas_call(strip_kernel, grid=(nodes,), in_specs=[pl.BlockSpec((1, wi...]
where the time goes in v8:
time: 126 us; the launch traced here: 125 us
  Pallas kernels  96.2 us (76%)
  other arithmetic  13.5 us (11%)
  local copies, waits for them, and re-layouts  10.6 us (8%)
  matrix products  2.59 us (2%)
  between operations  2.3 us (2%)
    pallas_call x1, Pallas kernels, strip_sums(): pl.pallas_call(strip_kernel, grid=(nodes,), in_specs=[pl.BlockSpec((1, wi...  62.6 us
    pallas_call x1, Pallas kernels, both_sums(): pl.pallas_call(functools.partial(both_sums_kernel, nz, ny, plane_row, dep...  19.7 us
    pallas_call x1, Pallas kernels, swap_halos(): pl.pallas_call(functools.partial(halo_kernel, ny, nz), out_shape=[jax.Sha...  13.9 us
    reduce_sum x3, other arithmetic, node_sums(): return field.reshape(nodes, width_y // KNOT, KNOT, width_z).sum(axis=2)  4.49 us

profile of v8, /device:TPU:1, one launch (start us, length us, event | category | flops | bytes accessed | tf_op | source)
XLA Modules:
  0.0 125.2 jit_solution(7688042031950208)
XLA Ops:
  0.6 1.4 %fusion.23 = (bf16[64,1,512]{2,1,0:T(2,128)(2,1)S(1)}, bf16[64,1,512]{2,1,0:T(2,128)(2,1)S(1)}) fusion(bf16[64,64,512]{2,1,0:T(8,128)(2,1)} %next_ref.1), kind=kLoop, calls=%fused_computation.73 | loop fusion | bytes 262144 | tf_op jit(solution)/shard_map/slice | solution.py:89
  2.1 0.7 pad_maximum_fusion.2.rows_ref
  2.7 2.1 %fusion.22 = (bf16[64,64,1]{2,1,0:T(8,128)(2,1)S(1)}, bf16[64,64,1]{2,1,0:T(8,128)(2,1)S(1)}) fusion(bf16[64,64,512]{2,1,0:T(8,128)(2,1)} %next_ref.1), kind=kLoop, calls=%fused_computation.72 | loop fusion | bytes 32768 | tf_op jit(solution)/shard_map/slice | solution.py:90
  4.8 0.5 copy.44
  5.3 0.5 copy.45
  5.8 0.6 pad_maximum_fusion.3.cols_ref
  6.4 13.9 %shard_map.76 = (bf16[2,64,512]{2,1,0:T(8,128)(2,1)}, bf16[6,64,64]{2,1,0:T(8,128)(2,1)}) custom-call(bf16[2,64,512]{2,1,0:T(8,128)(2,1)} %pad_maximum_fusion.2.rows_ref, bf16[2,64,64]{2,1,0:T(8,128)(2,1)} %pad_maximum_fusion.3.cols_ref), custom_call_target="tpu_custom_call" | custom-call | tf_op jit(solution)/shard_map/pallas_call | solution.py:68
  20.3 1.0 copy.37
  21.6 0.6 select_maximum_fusion.sides_ref
  22.3 0.9 convert_element_type.23
  23.2 0.7 pad_maximum_fusion.rows_ref
  24.0 1.1 fusion.4.fields_ref
  25.0 62.6 %shard_map.77 = (bf16[64,64,512]{2,1,0:T(8,128)(2,1)}, f32[8,64,512]{2,1,0:T(8,128)}, f32[8,64,512]{2,1,0:T(8,128)}, f32[8,64,512]{2,1,0:T(8,128)}, f32[8,16,256]{2,1,0:T(8,128)}) custom-call(bf16[64,64,512]{2,1,0:T(8,128)(2,1)} %next_ref.1, bf16[64,64,512]{2,1,0:T(8,128)(2,1)} %next_ref.1, bf16[64,64,512]{2,1,0:T(8,128)(2,1)} %next_ref.1, ...), custom_call_target="tpu_custom_call" | custom-call | tf_op jit(solution)/shard_map/pallas_call | solution.py:260
  87.6 1.5 %bitcast_reduce_fusion.1 = f32[8,8,512]{2,1,0:T(8,128)S(1)} fusion(f32[8,64,512]{2,1,0:T(8,128)} %get-tuple-element.16), kind=kLoop, calls=%fused_computation.6 | loop fusion | flops 229376 | bytes 1179648 | tf_op jit(solution)/shard_map/reduce_sum | solution.py:300
  89.1 0.3 convolution_bitcast_fusion.1
  89.4 1.5 %bitcast_reduce_fusion.2 = f32[8,8,512]{2,1,0:T(8,128)S(1)} fusion(f32[8,64,512]{2,1,0:T(8,128)} %get-tuple-element.15), kind=kLoop, calls=%fused_computation.7 | loop fusion | flops 229376 | bytes 1179648 | tf_op jit(solution)/shard_map/reduce_sum | solution.py:300
  90.9 0.3 convolution_bitcast_fusion.2
  91.2 1.5 %bitcast_reduce_fusion = f32[8,8,512]{2,1,0:T(8,128)S(1)} fusion(f32[8,64,512]{2,1,0:T(8,128)} %get-tuple-element.17), kind=kLoop, calls=%fused_computation.5 | loop fusion | flops 229376 | bytes 1179648 | tf_op jit(solution)/shard_map/reduce_sum | solution.py:300
  92.7 0.3 convolution_bitcast_fusion
  93.0 0.6 reduce_sum.68
  93.7 0.7 select_maximum_fusion.1
  94.5 0.8 maximum_maximum_fusion.depth_ref
  96.1 0.3 fusion.6
  96.9 0.7 maximum_maximum_fusion.1.plane_ref
  97.6 19.7 %shard_map.78 = (f32[8,8,128]{2,1,0:T(8,128)}, f32[16,32,128]{2,1,0:T(8,128)}) custom-call(f32[8,8,128]{2,1,0:T(8,128)} %maximum_maximum_fusion.1.plane_ref, f32[16,32,128]{2,1,0:T(8,128)} %maximum_maximum_fusion.depth_ref), custom_call_target="tpu_custom_call" | custom-call | tf_op jit(solution)/shard_map/pallas_call | solution.py:393
  117.4 0.9 slice.125
  118.4 0.7 slice_bitcast_fusion.4
  119.1 1.4 %slice_reduce_fusion = f32[]{:T(128)} fusion(f32[8,8,128]{2,1,0:T(8,128)} %get-tuple-element.19), kind=kLoop, calls=%fused_computation.61 | loop fusion | flops 7 | bytes 36 | tf_op jit(solution)/shard_map/reduce_sum | solution.py:448
  121.2 0.7 fusion.2
  121.9 1.0 slice.120
  122.9 0.7 slice_bitcast_fusion.5
  124.4 0.8 copy.40
  (46 shorter events, 2.1 us)
Async XLA Ops:
  2.7 21.2 %copy-start = (f32[2,32,512]{2,1,0:T(8,128)S(1)}, f32[2,32,512]{2,1,0:T(8,128)}, u32[]{:S(2)}) copy-start(f32[2,32,512]{2,1,0:T(8,128)} %param.9) | copy-start | bytes 393220
  2.7 21.2 %copy-start.1 = (f32[2,32,8,8]{1,3,2,0:T(8,128)S(1)}, f32[2,32,8,8]{1,3,2,0:T(8,128)}, u32[]{:S(2)}) copy-start(f32[2,32,8,8]{1,3,2,0:T(8,128)} %param.8) | copy-start | bytes 49156
  87.6 5.4 %copy-start.2 = (f32[8,16,256]{2,1,0:T(8,128)S(1)}, f32[8,16,256]{2,1,0:T(8,128)}, u32[]{:S(2)}) copy-start(f32[8,16,256]{2,1,0:T(8,128)} %get-tuple-element.18) | copy-start | bytes 393220

commit v9 on v7

--- a/solution.py
+++ b/solution.py
@@ -209,9 +209,11 @@
         zero = jnp.zeros((ROWS, LANES), jnp.float32)
         prod_acc, mis_acc, sq_acc, e_acc = lax.fori_loop(
             0, KNOT, plane, (zero, zero, zero, energy))
-        prod_ref[0, rs, cs] = prod_acc
-        mis_ref[0, rs, cs] = mis_acc
-        sq_ref[0, rs, cs] = sq_acc
+        ky = k // chunks_z
+        for out_ref, acc in ((prod_ref, prod_acc), (mis_ref, mis_acc), (sq_ref, sq_acc)):
+            for n in range(ROWS // KNOT):
+                out_ref[0, ky, pl.ds(n, 1), cs] = jnp.sum(
+                    acc[n * KNOT : (n + 1) * KNOT], axis=0, keepdims=True)
         return e_acc
 
     energy = lax.fori_loop(0, chunks_y * chunks_z, chunk,
@@ -223,8 +225,9 @@
     depth_x, width_y, width_z = image.shape
     nodes = depth_x // KNOT
     f32 = jnp.float32
-    block_sum = jax.ShapeDtypeStruct((nodes, width_y, width_z), f32)
-    node_spec = pl.BlockSpec((1, width_y, width_z), lambda i: (i, 0, 0))
+    pairs = ROWS // KNOT
+    block_sum = jax.ShapeDtypeStruct((nodes, width_y // ROWS, pairs, width_z), f32)
+    node_spec = pl.BlockSpec((1, width_y // ROWS, pairs, width_z), lambda i: (i, 0, 0, 0))
     plane_spec = pl.BlockSpec((KNOT, width_y, width_z), lambda i: (i, 0, 0))
     return pl.pallas_call(
         strip_kernel,
@@ -264,8 +267,8 @@
 
 
 def node_sums(field):
-    nodes, width_y, width_z = field.shape
-    return field.reshape(nodes, width_y // KNOT, KNOT, width_z).sum(axis=2)
+    nodes, chunks, pairs, width_z = field.shape
+    return field.reshape(nodes, chunks * pairs, width_z)
 
 
 def exchange(axis, n, me, d, src, buffer, send_sem, recv_sem):

time: 120 us -> 121 us (level)
  other arithmetic: 13.5 us -> 9.95 us
  local copies, waits for them, and re-layouts: 10.6 us -> 13.5 us
  Pallas kernels: 90.7 us -> 92.3 us
    reduce_sum x3 -> x0, other arithmetic: 4.49 us -> none  [node_sums(): return field.reshape(nodes, width_y // KNOT, KNOT, width_z).sum(axis=2)]
    reshape x0 -> x3, local copies, waits for them, and re-layouts: none -> 2.99 us  [node_sums(): return field.reshape(nodes, chunks * pairs, width_z)]
    pallas_call x1, Pallas kernels: 57.1 us -> 58.7 us  [strip_sums(): pl.pallas_call(strip_kernel, grid=(nodes,), in_specs=[pl.BlockSpec((1, wi...]
where the time goes in v9:
time: 121 us
  Pallas kernels  92.3 us (76%)
  local copies, waits for them, and re-layouts  13.5 us (11%)
  other arithmetic  9.95 us (8%)
  matrix products  2.57 us (2%)
  between operations  2.28 us (2%)
    pallas_call x1, Pallas kernels, strip_sums(): pl.pallas_call(strip_kernel, grid=(nodes,), in_specs=[pl.BlockSpec((1, wi...  58.7 us
    pallas_call x1, Pallas kernels, both_sums(): pl.pallas_call(functools.partial(both_sums_kernel, nz, ny, plane_row, dep...  19.7 us
    pallas_call x1, Pallas kernels, swap_halos(): pl.pallas_call(functools.partial(halo_kernel, ny, nz), out_shape=[jax.Sha...  13.9 us
    reshape x3, local copies, waits for them, and re-layouts, node_sums(): return field.reshape(nodes, chunks * pairs, width_z)  2.99 us

profile of v9, /device:TPU:1, one launch (start us, length us, event | category | flops | bytes accessed | tf_op | source)
XLA Modules:
  0.0 120.7 jit_solution(14569936741095167422)
XLA Ops:
  0.6 1.4 %fusion.26 = (bf16[64,1,512]{2,1,0:T(2,128)(2,1)S(1)}, bf16[64,1,512]{2,1,0:T(2,128)(2,1)S(1)}) fusion(bf16[64,64,512]{2,1,0:T(8,128)(2,1)} %next_ref.1), kind=kLoop, calls=%fused_computation.71 | loop fusion | bytes 262144 | tf_op jit(solution)/shard_map/slice | solution.py:89
  2.1 0.7 pad_maximum_fusion.2.rows_ref
  2.7 2.1 %fusion.25 = (bf16[64,64,1]{2,1,0:T(8,128)(2,1)S(1)}, bf16[64,64,1]{2,1,0:T(8,128)(2,1)S(1)}) fusion(bf16[64,64,512]{2,1,0:T(8,128)(2,1)} %next_ref.1), kind=kLoop, calls=%fused_computation.70 | loop fusion | bytes 32768 | tf_op jit(solution)/shard_map/slice | solution.py:90
  4.8 0.5 copy.44
  5.3 0.5 copy.45
  5.8 0.6 pad_maximum_fusion.3.cols_ref
  6.4 13.9 %shard_map.76 = (bf16[2,64,512]{2,1,0:T(8,128)(2,1)}, bf16[6,64,64]{2,1,0:T(8,128)(2,1)}) custom-call(bf16[2,64,512]{2,1,0:T(8,128)(2,1)} %pad_maximum_fusion.2.rows_ref, bf16[2,64,64]{2,1,0:T(8,128)(2,1)} %pad_maximum_fusion.3.cols_ref), custom_call_target="tpu_custom_call" | custom-call | tf_op jit(solution)/shard_map/pallas_call | solution.py:68
  20.3 1.0 copy.37
  21.6 0.6 select_maximum_fusion.sides_ref
  22.3 0.9 convert_element_type.23
  23.2 0.7 pad_maximum_fusion.rows_ref
  23.9 1.1 fusion.4.fields_ref
  25.0 58.7 %shard_map.77 = (bf16[64,64,512]{2,1,0:T(8,128)(2,1)}, f32[8,4,2,512]{3,2,1,0:T(2,128)}, f32[8,4,2,512]{3,2,1,0:T(2,128)}, f32[8,4,2,512]{3,2,1,0:T(2,128)}, f32[8,16,256]{2,1,0:T(8,128)}) custom-call(bf16[64,64,512]{2,1,0:T(8,128)(2,1)} %next_ref.1, bf16[64,64,512]{2,1,0:T(8,128)(2,1)} %next_ref.1, bf16[64,64,512]{2,1,0:T(8,128)(2,1)} %next_ref.1, ...), custom_call_target="tpu_custom_call" | custom-call | tf_op jit(solution)/shard_map/pallas_call | solution.py:232
  83.7 1.0 reshape.62
  84.7 0.3 convolution_bitcast_fusion.1
  85.0 1.0 reshape.61
  86.0 0.3 convolution_bitcast_fusion.2
  86.3 1.0 reshape.63
  87.3 0.3 convolution_bitcast_fusion
  87.6 1.5 %reduce_sum.38 = f32[]{:T(128)} reduce(f32[8,16,256]{2,1,0:T(8,128)} %get-tuple-element.18, f32[]{:T(128)} %constant.36.clone.1), dimensions={0,1,2}, to_apply=%region_2.3 | reduce | flops 32767 | bytes 131080 | tf_op jit(solution)/shard_map/reduce_sum | solution.py:390
  89.2 0.7 select_maximum_fusion.1
  90.0 0.8 maximum_maximum_fusion.depth_ref
  91.6 0.3 fusion.6
  92.4 0.7 maximum_maximum_fusion.1.plane_ref
  93.1 19.7 %shard_map.78 = (f32[8,8,128]{2,1,0:T(8,128)}, f32[16,32,128]{2,1,0:T(8,128)}) custom-call(f32[8,8,128]{2,1,0:T(8,128)} %maximum_maximum_fusion.1.plane_ref, f32[16,32,128]{2,1,0:T(8,128)} %maximum_maximum_fusion.depth_ref), custom_call_target="tpu_custom_call" | custom-call | tf_op jit(solution)/shard_map/pallas_call | solution.py:364
  112.8 0.9 slice.125
  113.9 0.7 slice_bitcast_fusion.4
  114.6 1.4 %slice_reduce_fusion = f32[]{:T(128)} fusion(f32[8,8,128]{2,1,0:T(8,128)} %get-tuple-element.19), kind=kLoop, calls=%fused_computation.59 | loop fusion | flops 7 | bytes 36 | tf_op jit(solution)/shard_map/reduce_sum | solution.py:419
  116.7 0.7 fusion.2
  117.4 1.0 slice.120
  118.4 0.7 slice_bitcast_fusion.5
  119.9 0.8 copy.40
  (44 shorter events, 2.0 us)
Async XLA Ops:
  2.7 21.2 %copy-start = (f32[2,32,512]{2,1,0:T(8,128)S(1)}, f32[2,32,512]{2,1,0:T(8,128)}, u32[]{:S(2)}) copy-start(f32[2,32,512]{2,1,0:T(8,128)} %param.9) | copy-start | bytes 393220
  2.7 21.2 %copy-start.1 = (f32[2,32,8,8]{1,3,2,0:T(8,128)S(1)}, f32[2,32,8,8]{1,3,2,0:T(8,128)}, u32[]{:S(2)}) copy-start(f32[2,32,8,8]{1,3,2,0:T(8,128)} %param.8) | copy-start | bytes 49156

commit v10 on v6

--- a/solution.py
+++ b/solution.py
@@ -198,7 +198,7 @@
 
         zero = jnp.zeros((ROWS, LANES), jnp.float32)
         prod_acc, mis_acc, sq_acc, e_acc = lax.fori_loop(
-            0, KNOT, plane, (zero, zero, zero, energy))
+            0, KNOT, plane, (zero, zero, zero, energy), unroll=2)
         prod_ref[0, rs, cs] = prod_acc
         mis_ref[0, rs, cs] = mis_acc
         sq_ref[0, rs, cs] = sq_acc

time: 120 us -> 116 us (0.967)
  Pallas kernels: 86.6 us -> 82 us
    pallas_call x1, Pallas kernels: 53 us -> 48.4 us  [strip_sums(): pl.pallas_call(strip_kernel, grid=(nodes,), in_specs=[pl.BlockSpec((1, wi...]
where the time goes in v10:
time: 116 us; the launch traced here: 115 us
  Pallas kernels  82 us (71%)
  other arithmetic  17.6 us (15%)
  local copies, waits for them, and re-layouts  11.2 us (10%)
  between operations  2.3 us (2%)
  matrix products  1.87 us (2%)
    pallas_call x1, Pallas kernels, strip_sums(): pl.pallas_call(strip_kernel, grid=(nodes,), in_specs=[pl.BlockSpec((1, wi...  48.4 us
    pallas_call x1, Pallas kernels, both_sums(): pl.pallas_call(functools.partial(both_sums_kernel, nz, ny, plane_row, dep...  19.7 us
    pallas_call x1, Pallas kernels, swap_halos(): pl.pallas_call(functools.partial(halo_kernel, ny, nz), out_shape=[jax.Sha...  13.9 us
    reduce_sum x3, other arithmetic, node_sums(): return field.reshape(nodes, width_y // KNOT, KNOT, width_z).sum(axis=2)  4.49 us
    select_n x1, other arithmetic, halo_blocks(): jnp.where(lanes == 0, side_high[:, :, None], jnp.where(lanes == 127, side...  2.9 us

profile of v10, /device:TPU:1, one launch (start us, length us, event | category | flops | bytes accessed | tf_op | source)
XLA Modules:
  0.0 115.1 jit_solution(17172254660116944838)
XLA Ops:
  0.6 1.4 %fusion.25 = (bf16[64,1,512]{2,1,0:T(2,128)(2,1)S(1)}, bf16[64,1,512]{2,1,0:T(2,128)(2,1)S(1)}) fusion(bf16[64,64,512]{2,1,0:T(8,128)(2,1)} %next_ref.1), kind=kLoop, calls=%fused_computation.81 | loop fusion | bytes 262144 | tf_op jit(solution)/shard_map/slice | solution.py:89
  2.1 0.7 pad_maximum_fusion.2.rows_ref
  2.7 2.0 %fusion.24 = (bf16[64,64,1]{2,1,0:T(8,128)(2,1)S(1)}, bf16[64,64,1]{2,1,0:T(8,128)(2,1)S(1)}) fusion(bf16[64,64,512]{2,1,0:T(8,128)(2,1)} %next_ref.1), kind=kLoop, calls=%fused_computation.80 | loop fusion | bytes 32768 | tf_op jit(solution)/shard_map/slice | solution.py:90
  4.8 0.5 copy.44
  5.3 0.5 copy.45
  5.7 0.6 pad_maximum_fusion.3.cols_ref
  6.4 13.9 %shard_map.76 = (bf16[2,64,512]{2,1,0:T(8,128)(2,1)}, bf16[6,64,64]{2,1,0:T(8,128)(2,1)}) custom-call(bf16[2,64,512]{2,1,0:T(8,128)(2,1)} %pad_maximum_fusion.2.rows_ref, bf16[2,64,64]{2,1,0:T(8,128)(2,1)} %pad_maximum_fusion.3.cols_ref), custom_call_target="tpu_custom_call" | custom-call | tf_op jit(solution)/shard_map/pallas_call | solution.py:68
  20.3 0.9 convert_element_type.24
  21.6 2.9 %select_select_fusion.cols_ref = f32[64,72,128]{2,1,0:T(8,128)} fusion(f32[64,72]{1,0:T(8,128)S(1)} %get-tuple-element.45, f32[64,72]{1,0:T(8,128)S(1)} %get-tuple-element.44, pred[128]{0:T(512)(128)(4,1)S(1)} %get-tuple-element.48, pred[128]{0:T(512)(128)(4,1)S(1)} %get-tuple-element.49), kind=kLoop, calls=%fused_computation | loop fusion | flops 1179648 | bytes 2396416 | tf_op jit(solution)/shard_map/jit(_where)/select_n | solution.py:112
  24.5 1.0 copy_convert_fusion
  25.8 1.2 %pad_maximum_fusion.rows_ref = f32[64,8,512]{2,1,0:T(8,128)} fusion(f32[64,1,512]{2,1,0:T(1,128)S(1)} %get-tuple-element.37, f32[64,1,512]{2,1,0:T(1,128)S(1)} %get-tuple-element.36, f32[8]{0:T(128)S(1)} %pad.40.clone), kind=kLoop, calls=%fused_computation.6 | loop fusion | flops 524288 | bytes 1310752 | tf_op jit(solution)/shard_map/concatenate | solution.py:107
  27.1 0.3 fusion.6
  27.5 1.6 %broadcast_bitcast_fusion = (f32[8,64,512]{2,1,0:T(8,128)}, f32[8,64,512]{2,1,0:T(8,128)}) fusion(f32[8,8,512]{2,1,0:T(8,128)S(1)} %get-tuple-element.34, f32[8,8,512]{2,1,0:T(8,128)S(1)} %get-tuple-element.35), kind=kLoop, calls=%fused_computation.10 | loop fusion | bytes 2359296 | tf_op jit(solution)/shard_map/broadcast_in_dim | solution.py:375
  29.1 48.4 %shard_map.77 = (bf16[64,64,512]{2,1,0:T(8,128)(2,1)}, f32[8,64,512]{2,1,0:T(8,128)}, f32[8,64,512]{2,1,0:T(8,128)}, f32[8,64,512]{2,1,0:T(8,128)}, f32[8,16,256]{2,1,0:T(8,128)}) custom-call(bf16[64,64,512]{2,1,0:T(8,128)(2,1)} %next_ref.1, bf16[64,64,512]{2,1,0:T(8,128)(2,1)} %next_ref.1, bf16[64,64,512]{2,1,0:T(8,128)(2,1)} %next_ref.1, ...), custom_call_target="tpu_custom_call" | custom-call | tf_op jit(solution)/shard_map/pallas_call | solution.py:219
  77.5 1.5 %bitcast_reduce_fusion.1 = f32[8,8,512]{2,1,0:T(8,128)S(1)} fusion(f32[8,64,512]{2,1,0:T(8,128)} %get-tuple-element.16), kind=kLoop, calls=%fused_computation.8 | loop fusion | flops 229376 | bytes 1179648 | tf_op jit(solution)/shard_map/reduce_sum | solution.py:259
  79.3 1.5 %bitcast_reduce_fusion.2 = f32[8,8,512]{2,1,0:T(8,128)S(1)} fusion(f32[8,64,512]{2,1,0:T(8,128)} %get-tuple-element.15), kind=kLoop, calls=%fused_computation.9 | loop fusion | flops 229376 | bytes 1179648 | tf_op jit(solution)/shard_map/reduce_sum | solution.py:259
  80.8 0.3 convolution_bitcast_fusion.2
  81.1 1.5 %bitcast_reduce_fusion = f32[8,8,512]{2,1,0:T(8,128)S(1)} fusion(f32[8,64,512]{2,1,0:T(8,128)} %get-tuple-element.17), kind=kLoop, calls=%fused_computation.7 | loop fusion | flops 229376 | bytes 1179648 | tf_op jit(solution)/shard_map/reduce_sum | solution.py:259
  82.6 0.3 convolution_bitcast_fusion
  82.9 0.6 reduce_sum.68
  83.6 0.7 select_maximum_fusion
  84.4 0.8 maximum_maximum_fusion.depth_ref
  86.0 0.3 fusion.8
  86.8 0.7 maximum_maximum_fusion.1.plane_ref
  87.5 19.7 %shard_map.78 = (f32[8,8,128]{2,1,0:T(8,128)}, f32[16,32,128]{2,1,0:T(8,128)}) custom-call(f32[8,8,128]{2,1,0:T(8,128)} %maximum_maximum_fusion.1.plane_ref, f32[16,32,128]{2,1,0:T(8,128)} %maximum_maximum_fusion.depth_ref), custom_call_target="tpu_custom_call" | custom-call | tf_op jit(solution)/shard_map/pallas_call | solution.py:352
  107.3 0.9 slice.143
  108.3 0.7 slice_bitcast_fusion.6
  109.0 1.4 %slice_reduce_fusion = f32[]{:T(128)} fusion(f32[8,8,128]{2,1,0:T(8,128)} %get-tuple-element.19), kind=kLoop, calls=%fused_computation.71 | loop fusion | flops 7 | bytes 36 | tf_op jit(solution)/shard_map/reduce_sum | solution.py:408
  111.1 0.7 fusion.2
  111.8 1.0 slice.138
  112.8 0.7 slice_bitcast_fusion.7
  114.3 0.8 copy.40
  (49 shorter events, 2.7 us)
Async XLA Ops:
  4.8 22.3 %copy-start = (f32[2,32,512]{2,1,0:T(8,128)S(1)}, f32[2,32,512]{2,1,0:T(8,128)}, u32[]{:S(2)}) copy-start(f32[2,32,512]{2,1,0:T(8,128)} %param.9) | copy-start | bytes 393220
  4.8 22.3 %copy-start.1 = (f32[2,32,8,8]{1,3,2,0:T(8,128)S(1)}, f32[2,32,8,8]{1,3,2,0:T(8,128)}, u32[]{:S(2)}) copy-start(f32[2,32,8,8]{1,3,2,0:T(8,128)} %param.8) | copy-start | bytes 49156
  77.5 5.4 %copy-start.2 = (f32[8,16,256]{2,1,0:T(8,128)S(1)}, f32[8,16,256]{2,1,0:T(8,128)}, u32[]{:S(2)}) copy-start(f32[8,16,256]{2,1,0:T(8,128)} %get-tuple-element.18) | copy-start | bytes 393220

commit v11 on v10

--- a/solution.py
+++ b/solution.py
@@ -198,7 +198,7 @@
 
         zero = jnp.zeros((ROWS, LANES), jnp.float32)
         prod_acc, mis_acc, sq_acc, e_acc = lax.fori_loop(
-            0, KNOT, plane, (zero, zero, zero, energy), unroll=2)
+            0, KNOT, plane, (zero, zero, zero, energy), unroll=4)
         prod_ref[0, rs, cs] = prod_acc
         mis_ref[0, rs, cs] = mis_acc
         sq_ref[0, rs, cs] = sq_acc

time: 116 us -> 114 us (0.983)
  Pallas kernels: 82 us -> 80 us
    pallas_call x1, Pallas kernels: 48.4 us -> 46.4 us  [strip_sums(): pl.pallas_call(strip_kernel, grid=(nodes,), in_specs=[pl.BlockSpec((1, wi...]
where the time goes in v11:
time: 114 us; the launch traced here: 113 us
  Pallas kernels  80 us (70%)
  other arithmetic  17.6 us (15%)
  local copies, waits for them, and re-layouts  11.2 us (10%)
  between operations  2.3 us (2%)
  matrix products  1.87 us (2%)
    pallas_call x1, Pallas kernels, strip_sums(): pl.pallas_call(strip_kernel, grid=(nodes,), in_specs=[pl.BlockSpec((1, wi...  46.4 us
    pallas_call x1, Pallas kernels, both_sums(): pl.pallas_call(functools.partial(both_sums_kernel, nz, ny, plane_row, dep...  19.7 us
    pallas_call x1, Pallas kernels, swap_halos(): pl.pallas_call(functools.partial(halo_kernel, ny, nz), out_shape=[jax.Sha...  13.9 us
    reduce_sum x3, other arithmetic, node_sums(): return field.reshape(nodes, width_y // KNOT, KNOT, width_z).sum(axis=2)  4.49 us
    select_n x1, other arithmetic, halo_blocks(): jnp.where(lanes == 0, side_high[:, :, None], jnp.where(lanes == 127, side...  2.9 us

profile of v11, /device:TPU:1, one launch (start us, length us, event | category | flops | bytes accessed | tf_op | source)
XLA Modules:
  0.0 113.1 jit_solution(10690620204069924101)
XLA Ops:
  0.6 1.4 %fusion.25 = (bf16[64,1,512]{2,1,0:T(2,128)(2,1)S(1)}, bf16[64,1,512]{2,1,0:T(2,128)(2,1)S(1)}) fusion(bf16[64,64,512]{2,1,0:T(8,128)(2,1)} %next_ref.1), kind=kLoop, calls=%fused_computation.81 | loop fusion | bytes 262144 | tf_op jit(solution)/shard_map/slice | solution.py:89
  2.1 0.7 pad_maximum_fusion.2.rows_ref
  2.7 2.0 %fusion.24 = (bf16[64,64,1]{2,1,0:T(8,128)(2,1)S(1)}, bf16[64,64,1]{2,1,0:T(8,128)(2,1)S(1)}) fusion(bf16[64,64,512]{2,1,0:T(8,128)(2,1)} %next_ref.1), kind=kLoop, calls=%fused_computation.80 | loop fusion | bytes 32768 | tf_op jit(solution)/shard_map/slice | solution.py:90
  4.8 0.5 copy.44
  5.3 0.5 copy.45
  5.7 0.6 pad_maximum_fusion.3.cols_ref
  6.4 13.9 %shard_map.76 = (bf16[2,64,512]{2,1,0:T(8,128)(2,1)}, bf16[6,64,64]{2,1,0:T(8,128)(2,1)}) custom-call(bf16[2,64,512]{2,1,0:T(8,128)(2,1)} %pad_maximum_fusion.2.rows_ref, bf16[2,64,64]{2,1,0:T(8,128)(2,1)} %pad_maximum_fusion.3.cols_ref), custom_call_target="tpu_custom_call" | custom-call | tf_op jit(solution)/shard_map/pallas_call | solution.py:68
  20.3 0.9 convert_element_type.24
  21.6 2.9 %select_select_fusion.cols_ref = f32[64,72,128]{2,1,0:T(8,128)} fusion(f32[64,72]{1,0:T(8,128)S(1)} %get-tuple-element.45, f32[64,72]{1,0:T(8,128)S(1)} %get-tuple-element.44, pred[128]{0:T(512)(128)(4,1)S(1)} %get-tuple-element.48, pred[128]{0:T(512)(128)(4,1)S(1)} %get-tuple-element.49), kind=kLoop, calls=%fused_computation | loop fusion | flops 1179648 | bytes 2396416 | tf_op jit(solution)/shard_map/jit(_where)/select_n | solution.py:112
  24.5 1.0 copy_convert_fusion
  25.8 1.2 %pad_maximum_fusion.rows_ref = f32[64,8,512]{2,1,0:T(8,128)} fusion(f32[64,1,512]{2,1,0:T(1,128)S(1)} %get-tuple-element.37, f32[64,1,512]{2,1,0:T(1,128)S(1)} %get-tuple-element.36, f32[8]{0:T(128)S(1)} %pad.40.clone), kind=kLoop, calls=%fused_computation.6 | loop fusion | flops 524288 | bytes 1310752 | tf_op jit(solution)/shard_map/concatenate | solution.py:107
  27.1 0.3 fusion.6
  27.5 1.6 %broadcast_bitcast_fusion = (f32[8,64,512]{2,1,0:T(8,128)}, f32[8,64,512]{2,1,0:T(8,128)}) fusion(f32[8,8,512]{2,1,0:T(8,128)S(1)} %get-tuple-element.34, f32[8,8,512]{2,1,0:T(8,128)S(1)} %get-tuple-element.35), kind=kLoop, calls=%fused_computation.10 | loop fusion | bytes 2359296 | tf_op jit(solution)/shard_map/broadcast_in_dim | solution.py:375
  29.1 46.4 %shard_map.77 = (bf16[64,64,512]{2,1,0:T(8,128)(2,1)}, f32[8,64,512]{2,1,0:T(8,128)}, f32[8,64,512]{2,1,0:T(8,128)}, f32[8,64,512]{2,1,0:T(8,128)}, f32[8,16,256]{2,1,0:T(8,128)}) custom-call(bf16[64,64,512]{2,1,0:T(8,128)(2,1)} %next_ref.1, bf16[64,64,512]{2,1,0:T(8,128)(2,1)} %next_ref.1, bf16[64,64,512]{2,1,0:T(8,128)(2,1)} %next_ref.1, ...), custom_call_target="tpu_custom_call" | custom-call | tf_op jit(solution)/shard_map/pallas_call | solution.py:219
  75.5 1.5 %bitcast_reduce_fusion.1 = f32[8,8,512]{2,1,0:T(8,128)S(1)} fusion(f32[8,64,512]{2,1,0:T(8,128)} %get-tuple-element.16), kind=kLoop, calls=%fused_computation.8 | loop fusion | flops 229376 | bytes 1179648 | tf_op jit(solution)/shard_map/reduce_sum | solution.py:259
  77.3 1.5 %bitcast_reduce_fusion.2 = f32[8,8,512]{2,1,0:T(8,128)S(1)} fusion(f32[8,64,512]{2,1,0:T(8,128)} %get-tuple-element.15), kind=kLoop, calls=%fused_computation.9 | loop fusion | flops 229376 | bytes 1179648 | tf_op jit(solution)/shard_map/reduce_sum | solution.py:259
  78.8 0.3 convolution_bitcast_fusion.2
  79.1 1.5 %bitcast_reduce_fusion = f32[8,8,512]{2,1,0:T(8,128)S(1)} fusion(f32[8,64,512]{2,1,0:T(8,128)} %get-tuple-element.17), kind=kLoop, calls=%fused_computation.7 | loop fusion | flops 229376 | bytes 1179648 | tf_op jit(solution)/shard_map/reduce_sum | solution.py:259
  80.6 0.3 convolution_bitcast_fusion
  80.9 0.6 reduce_sum.68
  81.6 0.7 select_maximum_fusion
  82.4 0.8 maximum_maximum_fusion.depth_ref
  84.0 0.3 fusion.8
  84.8 0.7 maximum_maximum_fusion.1.plane_ref
  85.5 19.7 %shard_map.78 = (f32[8,8,128]{2,1,0:T(8,128)}, f32[16,32,128]{2,1,0:T(8,128)}) custom-call(f32[8,8,128]{2,1,0:T(8,128)} %maximum_maximum_fusion.1.plane_ref, f32[16,32,128]{2,1,0:T(8,128)} %maximum_maximum_fusion.depth_ref), custom_call_target="tpu_custom_call" | custom-call | tf_op jit(solution)/shard_map/pallas_call | solution.py:352
  105.2 0.9 slice.143
  106.2 0.7 slice_bitcast_fusion.6
  107.0 1.4 %slice_reduce_fusion = f32[]{:T(128)} fusion(f32[8,8,128]{2,1,0:T(8,128)} %get-tuple-element.19), kind=kLoop, calls=%fused_computation.71 | loop fusion | flops 7 | bytes 36 | tf_op jit(solution)/shard_map/reduce_sum | solution.py:408
  109.1 0.7 fusion.2
  109.8 1.0 slice.138
  110.8 0.7 slice_bitcast_fusion.7
  112.3 0.8 copy.40
  (49 shorter events, 2.7 us)
Async XLA Ops:
  4.8 22.3 %copy-start = (f32[2,32,512]{2,1,0:T(8,128)S(1)}, f32[2,32,512]{2,1,0:T(8,128)}, u32[]{:S(2)}) copy-start(f32[2,32,512]{2,1,0:T(8,128)} %param.9) | copy-start | bytes 393220
  4.8 22.3 %copy-start.1 = (f32[2,32,8,8]{1,3,2,0:T(8,128)S(1)}, f32[2,32,8,8]{1,3,2,0:T(8,128)}, u32[]{:S(2)}) copy-start(f32[2,32,8,8]{1,3,2,0:T(8,128)} %param.8) | copy-start | bytes 49156
  75.5 5.4 %copy-start.2 = (f32[8,16,256]{2,1,0:T(8,128)S(1)}, f32[8,16,256]{2,1,0:T(8,128)}, u32[]{:S(2)}) copy-start(f32[8,16,256]{2,1,0:T(8,128)} %get-tuple-element.18) | copy-start | bytes 393220

commit v12 on v11

--- a/solution.py
+++ b/solution.py
@@ -147,7 +147,7 @@
         source_plane(p, main_ref[p - 1])
         return carry
 
-    lax.fori_loop(1, KNOT + 1, inner_plane, 0)
+    lax.fori_loop(1, KNOT + 1, inner_plane, 0, unroll=2)
     source_plane(KNOT + 1, next_ref[0])
 
     chunks_y = width_y // ROWS

time: 114 us -> 112 us (0.982)
  Pallas kernels: 80 us -> 78.3 us
    pallas_call x1, Pallas kernels: 46.4 us -> 44.6 us  [strip_sums(): pl.pallas_call(strip_kernel, grid=(nodes,), in_specs=[pl.BlockSpec((1, wi...]
where the time goes in v12:
time: 112 us; the launch traced here: 111 us
  Pallas kernels  78.3 us (70%)
  other arithmetic  17.6 us (16%)
  local copies, waits for them, and re-layouts  11.2 us (10%)
  between operations  2.3 us (2%)
  matrix products  1.86 us (2%)
    pallas_call x1, Pallas kernels, strip_sums(): pl.pallas_call(strip_kernel, grid=(nodes,), in_specs=[pl.BlockSpec((1, wi...  44.6 us
    pallas_call x1, Pallas kernels, both_sums(): pl.pallas_call(functools.partial(both_sums_kernel, nz, ny, plane_row, dep...  19.7 us
    pallas_call x1, Pallas kernels, swap_halos(): pl.pallas_call(functools.partial(halo_kernel, ny, nz), out_shape=[jax.Sha...  13.9 us
    reduce_sum x3, other arithmetic, node_sums(): return field.reshape(nodes, width_y // KNOT, KNOT, width_z).sum(axis=2)  4.49 us
    select_n x1, other arithmetic, halo_blocks(): jnp.where(lanes == 0, side_high[:, :, None], jnp.where(lanes == 127, side...  2.9 us

profile of v12, /device:TPU:1, one launch (start us, length us, event | category | flops | bytes accessed | tf_op | source)
XLA Modules:
  0.0 111.3 jit_solution(10445924525900031123)
XLA Ops:
  0.6 1.4 %fusion.25 = (bf16[64,1,512]{2,1,0:T(2,128)(2,1)S(1)}, bf16[64,1,512]{2,1,0:T(2,128)(2,1)S(1)}) fusion(bf16[64,64,512]{2,1,0:T(8,128)(2,1)} %next_ref.1), kind=kLoop, calls=%fused_computation.81 | loop fusion | bytes 262144 | tf_op jit(solution)/shard_map/slice | solution.py:89
  2.1 0.7 pad_maximum_fusion.2.rows_ref
  2.7 2.0 %fusion.24 = (bf16[64,64,1]{2,1,0:T(8,128)(2,1)S(1)}, bf16[64,64,1]{2,1,0:T(8,128)(2,1)S(1)}) fusion(bf16[64,64,512]{2,1,0:T(8,128)(2,1)} %next_ref.1), kind=kLoop, calls=%fused_computation.80 | loop fusion | bytes 32768 | tf_op jit(solution)/shard_map/slice | solution.py:90
  4.8 0.5 copy.44
  5.3 0.5 copy.45
  5.7 0.6 pad_maximum_fusion.3.cols_ref
  6.4 13.9 %shard_map.76 = (bf16[2,64,512]{2,1,0:T(8,128)(2,1)}, bf16[6,64,64]{2,1,0:T(8,128)(2,1)}) custom-call(bf16[2,64,512]{2,1,0:T(8,128)(2,1)} %pad_maximum_fusion.2.rows_ref, bf16[2,64,64]{2,1,0:T(8,128)(2,1)} %pad_maximum_fusion.3.cols_ref), custom_call_target="tpu_custom_call" | custom-call | tf_op jit(solution)/shard_map/pallas_call | solution.py:68
  20.3 0.9 convert_element_type.24
  21.6 2.9 %select_select_fusion.cols_ref = f32[64,72,128]{2,1,0:T(8,128)} fusion(f32[64,72]{1,0:T(8,128)S(1)} %get-tuple-element.45, f32[64,72]{1,0:T(8,128)S(1)} %get-tuple-element.44, pred[128]{0:T(512)(128)(4,1)S(1)} %get-tuple-element.48, pred[128]{0:T(512)(128)(4,1)S(1)} %get-tuple-element.49), kind=kLoop, calls=%fused_computation | loop fusion | flops 1179648 | bytes 2396416 | tf_op jit(solution)/shard_map/jit(_where)/select_n | solution.py:112
  24.5 1.0 copy_convert_fusion
  25.8 1.2 %pad_maximum_fusion.rows_ref = f32[64,8,512]{2,1,0:T(8,128)} fusion(f32[64,1,512]{2,1,0:T(1,128)S(1)} %get-tuple-element.37, f32[64,1,512]{2,1,0:T(1,128)S(1)} %get-tuple-element.36, f32[8]{0:T(128)S(1)} %pad.40.clone), kind=kLoop, calls=%fused_computation.6 | loop fusion | flops 524288 | bytes 1310752 | tf_op jit(solution)/shard_map/concatenate | solution.py:107
  27.1 0.3 fusion.6
  27.5 1.6 %broadcast_bitcast_fusion = (f32[8,64,512]{2,1,0:T(8,128)}, f32[8,64,512]{2,1,0:T(8,128)}) fusion(f32[8,8,512]{2,1,0:T(8,128)S(1)} %get-tuple-element.34, f32[8,8,512]{2,1,0:T(8,128)S(1)} %get-tuple-element.35), kind=kLoop, calls=%fused_computation.10 | loop fusion | bytes 2359296 | tf_op jit(solution)/shard_map/broadcast_in_dim | solution.py:375
  29.1 44.6 %shard_map.77 = (bf16[64,64,512]{2,1,0:T(8,128)(2,1)}, f32[8,64,512]{2,1,0:T(8,128)}, f32[8,64,512]{2,1,0:T(8,128)}, f32[8,64,512]{2,1,0:T(8,128)}, f32[8,16,256]{2,1,0:T(8,128)}) custom-call(bf16[64,64,512]{2,1,0:T(8,128)(2,1)} %next_ref.1, bf16[64,64,512]{2,1,0:T(8,128)(2,1)} %next_ref.1, bf16[64,64,512]{2,1,0:T(8,128)(2,1)} %next_ref.1, ...), custom_call_target="tpu_custom_call" | custom-call | tf_op jit(solution)/shard_map/pallas_call | solution.py:219
  73.7 1.5 %bitcast_reduce_fusion.1 = f32[8,8,512]{2,1,0:T(8,128)S(1)} fusion(f32[8,64,512]{2,1,0:T(8,128)} %get-tuple-element.16), kind=kLoop, calls=%fused_computation.8 | loop fusion | flops 229376 | bytes 1179648 | tf_op jit(solution)/shard_map/reduce_sum | solution.py:259
  75.2 0.3 convolution_bitcast_fusion.1
  75.5 1.5 %bitcast_reduce_fusion.2 = f32[8,8,512]{2,1,0:T(8,128)S(1)} fusion(f32[8,64,512]{2,1,0:T(8,128)} %get-tuple-element.15), kind=kLoop, calls=%fused_computation.9 | loop fusion | flops 229376 | bytes 1179648 | tf_op jit(solution)/shard_map/reduce_sum | solution.py:259
  77.3 1.5 %bitcast_reduce_fusion = f32[8,8,512]{2,1,0:T(8,128)S(1)} fusion(f32[8,64,512]{2,1,0:T(8,128)} %get-tuple-element.17), kind=kLoop, calls=%fused_computation.7 | loop fusion | flops 229376 | bytes 1179648 | tf_op jit(solution)/shard_map/reduce_sum | solution.py:259
  78.8 0.3 convolution_bitcast_fusion
  79.1 0.6 reduce_sum.68
  79.8 0.7 select_maximum_fusion
  80.6 0.8 maximum_maximum_fusion.depth_ref
  82.2 0.3 fusion.8
  83.0 0.7 maximum_maximum_fusion.1.plane_ref
  83.7 19.7 %shard_map.78 = (f32[8,8,128]{2,1,0:T(8,128)}, f32[16,32,128]{2,1,0:T(8,128)}) custom-call(f32[8,8,128]{2,1,0:T(8,128)} %maximum_maximum_fusion.1.plane_ref, f32[16,32,128]{2,1,0:T(8,128)} %maximum_maximum_fusion.depth_ref), custom_call_target="tpu_custom_call" | custom-call | tf_op jit(solution)/shard_map/pallas_call | solution.py:352
  103.5 0.9 slice.143
  104.5 0.7 slice_bitcast_fusion.6
  105.2 1.4 %slice_reduce_fusion = f32[]{:T(128)} fusion(f32[8,8,128]{2,1,0:T(8,128)} %get-tuple-element.19), kind=kLoop, calls=%fused_computation.71 | loop fusion | flops 7 | bytes 36 | tf_op jit(solution)/shard_map/reduce_sum | solution.py:408
  107.3 0.7 fusion.2
  108.0 1.0 slice.138
  109.0 0.7 slice_bitcast_fusion.7
  110.5 0.8 copy.40
  (49 shorter events, 2.7 us)
Async XLA Ops:
  4.8 22.3 %copy-start = (f32[2,32,512]{2,1,0:T(8,128)S(1)}, f32[2,32,512]{2,1,0:T(8,128)}, u32[]{:S(2)}) copy-start(f32[2,32,512]{2,1,0:T(8,128)} %param.9) | copy-start | bytes 393220
  4.8 22.3 %copy-start.1 = (f32[2,32,8,8]{1,3,2,0:T(8,128)S(1)}, f32[2,32,8,8]{1,3,2,0:T(8,128)}, u32[]{:S(2)}) copy-start(f32[2,32,8,8]{1,3,2,0:T(8,128)} %param.8) | copy-start | bytes 49156
  73.7 5.4 %copy-start.2 = (f32[8,16,256]{2,1,0:T(8,128)S(1)}, f32[8,16,256]{2,1,0:T(8,128)}, u32[]{:S(2)}) copy-start(f32[8,16,256]{2,1,0:T(8,128)} %get-tuple-element.18) | copy-start | bytes 393220

commit v13 on v12

--- a/solution.py
+++ b/solution.py
@@ -89,12 +89,11 @@
     rows_send = jnp.stack([deformed[:, 0, :], deformed[:, width_y - 1, :]])
     cols_send = jnp.stack([deformed[:, :, 0], deformed[:, :, width_z - 1]])
     rows_got, cols_got = swap_halos(rows_send, cols_send)
-    has_up = (my < ny - 1).astype(f32)
-    has_down = (my > 0).astype(f32)
-    has_right = (mz < nz - 1).astype(f32)
-    has_left = (mz > 0).astype(f32)
-    rows_got = rows_got.astype(f32)
-    cols_got = cols_got.astype(f32)
+    held = deformed.dtype
+    has_up = (my < ny - 1).astype(held)
+    has_down = (my > 0).astype(held)
+    has_right = (mz < nz - 1).astype(held)
+    has_left = (mz > 0).astype(held)
     high_y = rows_got[0] * has_up
     low_y = rows_got[1] * has_down
     high_z = cols_got[0] * has_right
@@ -103,14 +102,14 @@
     low_high = cols_got[3][:, width_y - 1] * (has_down * has_right)
     high_low = cols_got[4][:, 0] * (has_up * has_left)
     low_low = cols_got[5][:, width_y - 1] * (has_down * has_left)
-    gap_y = jnp.zeros((depth_x, 6, width_z), f32)
+    gap_y = jnp.zeros((depth_x, 6, width_z), held)
     rows = jnp.concatenate([high_y[:, None], gap_y, low_y[:, None]], axis=1)
-    gap = jnp.zeros((depth_x, 6), f32)
+    gap = jnp.zeros((depth_x, 6), held)
     side_high = jnp.concatenate([high_z, high_high[:, None], gap, low_high[:, None]], axis=1)
     side_low = jnp.concatenate([low_z, high_low[:, None], gap, low_low[:, None]], axis=1)
     lanes = lax.broadcasted_iota(jnp.int32, (1, 1, 128), 2)
     cols = jnp.where(lanes == 0, side_high[:, :, None],
-                     jnp.where(lanes == 127, side_low[:, :, None], 0.0))
+                     jnp.where(lanes == 127, side_low[:, :, None], jnp.zeros((), held)))
     return rows, cols
 
 
@@ -131,8 +130,8 @@
         valid = jnp.logical_and(plane_x >= 0, plane_x < depth_x)
         safe = jnp.clip(plane_x, 0, depth_x - 1)
         pad_ref[:width_y, :width_z] = plane.astype(jnp.float32)
-        pad_ref[width_y:, :width_z] = rows_ref[safe]
-        pad_ref[:, width_z:] = cols_ref[safe]
+        pad_ref[width_y:, :width_z] = rows_ref[safe].astype(jnp.float32)
+        pad_ref[:, width_z:] = cols_ref[safe].astype(jnp.float32)
         whole = jnp.where(valid, pad_ref[...], 0.0)
         by_y = (pltpu.roll(whole, 1, 0), whole, pltpu.roll(whole, pad_y - 1, 0))
         for b in range(3):

time: 112 us -> 108 us (0.964)
  Pallas kernels: 78.3 us -> 75.4 us
    pallas_call x1, Pallas kernels: 44.6 us -> 41.7 us  [strip_sums(): pl.pallas_call(strip_kernel, grid=(nodes,), in_specs=[pl.BlockSpec((1, wi...]
    convert_element_type x2 -> x0, other arithmetic: 1.95 us -> none  [the longest x1 1.04 us: halo_blocks(): rows_got = rows_got.astype(f32)]
where the time goes in v13:
time: 108 us
  Pallas kernels  75.4 us (70%)
  other arithmetic  16.8 us (16%)
  local copies, waits for them, and re-layouts  11.4 us (11%)
  between operations  2.3 us (2%)
  matrix products  1.87 us (2%)
    pallas_call x1, Pallas kernels, strip_sums(): pl.pallas_call(strip_kernel, grid=(nodes,), in_specs=[pl.BlockSpec((1, wi...  41.7 us
    pallas_call x1, Pallas kernels, both_sums(): pl.pallas_call(functools.partial(both_sums_kernel, nz, ny, plane_row, dep...  19.7 us
    pallas_call x1, Pallas kernels, swap_halos(): pl.pallas_call(functools.partial(halo_kernel, ny, nz), out_shape=[jax.Sha...  13.9 us
    reduce_sum x3, other arithmetic, node_sums(): return field.reshape(nodes, width_y // KNOT, KNOT, width_z).sum(axis=2)  4.49 us
    select_n x1, other arithmetic, halo_blocks(): jnp.where(lanes == 0, side_high[:, :, None], jnp.where(lanes == 127, side...  2.58 us

profile of v13, /device:TPU:1, one launch (start us, length us, event | category | flops | bytes accessed | tf_op | source)
XLA Modules:
  0.0 107.8 jit_solution(16355551868057356196)
XLA Ops:
  0.6 1.4 %fusion.21 = (bf16[64,1,512]{2,1,0:T(2,128)(2,1)S(1)}, bf16[64,1,512]{2,1,0:T(2,128)(2,1)S(1)}) fusion(bf16[64,64,512]{2,1,0:T(8,128)(2,1)} %next_ref.1), kind=kLoop, calls=%fused_computation.76 | loop fusion | bytes 262144 | tf_op jit(solution)/shard_map/slice | solution.py:89
  2.1 0.7 pad_maximum_fusion.2.rows_ref
  2.7 2.1 %fusion.20 = (bf16[64,64,1]{2,1,0:T(8,128)(2,1)S(1)}, bf16[64,64,1]{2,1,0:T(8,128)(2,1)S(1)}) fusion(bf16[64,64,512]{2,1,0:T(8,128)(2,1)} %next_ref.1), kind=kLoop, calls=%fused_computation.75 | loop fusion | bytes 32768 | tf_op jit(solution)/shard_map/slice | solution.py:90
  4.8 0.5 copy.46
  5.3 0.5 copy.47
  5.8 0.6 pad_maximum_fusion.3.cols_ref
  6.4 13.9 %shard_map.76 = (bf16[2,64,512]{2,1,0:T(8,128)(2,1)}, bf16[6,64,64]{2,1,0:T(8,128)(2,1)}) custom-call(bf16[2,64,512]{2,1,0:T(8,128)(2,1)} %pad_maximum_fusion.2.rows_ref, bf16[2,64,64]{2,1,0:T(8,128)(2,1)} %pad_maximum_fusion.3.cols_ref), custom_call_target="tpu_custom_call" | custom-call | tf_op jit(solution)/shard_map/pallas_call | solution.py:68
  20.3 0.8 multiply_bitcast_fusion.3
  21.6 2.6 %select_select_fusion.cols_ref = bf16[64,72,128]{2,1,0:T(8,128)(2,1)} fusion(pred[128]{0:T(512)(128)(4,1)S(1)} %get-tuple-element.48, pred[128]{0:T(512)(128)(4,1)S(1)} %get-tuple-element.49, bf16[64,72]{1,0:T(8,128)(2,1)S(1)} %get-tuple-element.45, bf16[64,72]{1,0:T(8,128)(2,1)S(1)} %get-tuple-element.44), kind=kLoop, calls=%fused_computation | loop fusion | flops 1179648 | bytes 1198336 | tf_op jit(solution)/shard_map/jit(_where)/select_n | solution.py:111
  24.1 0.9 multiply_bitcast_fusion.1
  25.3 1.2 %pad_maximum_fusion.rows_ref = bf16[64,8,512]{2,1,0:T(8,128)(2,1)} fusion(bf16[64,1,512]{2,1,0:T(2,128)(2,1)S(1)} %copy.39, bf16[64,1,512]{2,1,0:T(2,128)(2,1)S(1)} %copy.38, bf16[8]{0:T(256)(128)(2,1)S(1)} %pad.40.clone), kind=kLoop, calls=%fused_computation.9 | loop fusion | flops 1572864 | bytes 655376 | tf_op jit(solution)/shard_map/concatenate | solution.py:106
  26.5 0.3 fusion.4
  26.9 1.6 %broadcast_bitcast_fusion = (f32[8,64,512]{2,1,0:T(8,128)}, f32[8,64,512]{2,1,0:T(8,128)}) fusion(f32[8,8,512]{2,1,0:T(8,128)S(1)} %get-tuple-element.34, f32[8,8,512]{2,1,0:T(8,128)S(1)} %get-tuple-element.35), kind=kLoop, calls=%fused_computation.10 | loop fusion | bytes 2359296 | tf_op jit(solution)/shard_map/broadcast_in_dim | solution.py:374
  28.5 41.7 %shard_map.77 = (bf16[64,64,512]{2,1,0:T(8,128)(2,1)}, f32[8,64,512]{2,1,0:T(8,128)}, f32[8,64,512]{2,1,0:T(8,128)}, f32[8,64,512]{2,1,0:T(8,128)}, f32[8,16,256]{2,1,0:T(8,128)}) custom-call(bf16[64,64,512]{2,1,0:T(8,128)(2,1)} %next_ref.1, bf16[64,64,512]{2,1,0:T(8,128)(2,1)} %next_ref.1, bf16[64,64,512]{2,1,0:T(8,128)(2,1)} %next_ref.1, ...), custom_call_target="tpu_custom_call" | custom-call | tf_op jit(solution)/shard_map/pallas_call | solution.py:218
  70.2 1.5 %bitcast_reduce_fusion.1 = f32[8,8,512]{2,1,0:T(8,128)S(1)} fusion(f32[8,64,512]{2,1,0:T(8,128)} %get-tuple-element.16), kind=kLoop, calls=%fused_computation.7 | loop fusion | flops 229376 | bytes 1179648 | tf_op jit(solution)/shard_map/reduce_sum | solution.py:258
  71.7 0.3 convolution_bitcast_fusion.1
  72.0 1.5 %bitcast_reduce_fusion.2 = f32[8,8,512]{2,1,0:T(8,128)S(1)} fusion(f32[8,64,512]{2,1,0:T(8,128)} %get-tuple-element.15), kind=kLoop, calls=%fused_computation.8 | loop fusion | flops 229376 | bytes 1179648 | tf_op jit(solution)/shard_map/reduce_sum | solution.py:258
  73.8 1.5 %bitcast_reduce_fusion = f32[8,8,512]{2,1,0:T(8,128)S(1)} fusion(f32[8,64,512]{2,1,0:T(8,128)} %get-tuple-element.17), kind=kLoop, calls=%fused_computation.6 | loop fusion | flops 229376 | bytes 1179648 | tf_op jit(solution)/shard_map/reduce_sum | solution.py:258
  75.3 0.3 convolution_bitcast_fusion
  75.6 0.6 reduce_sum.68
  76.3 0.7 select_maximum_fusion
  77.1 0.8 maximum_maximum_fusion.depth_ref
  78.7 0.3 fusion.6
  79.5 0.7 maximum_maximum_fusion.1.plane_ref
  80.2 19.7 %shard_map.78 = (f32[8,8,128]{2,1,0:T(8,128)}, f32[16,32,128]{2,1,0:T(8,128)}) custom-call(f32[8,8,128]{2,1,0:T(8,128)} %maximum_maximum_fusion.1.plane_ref, f32[16,32,128]{2,1,0:T(8,128)} %maximum_maximum_fusion.depth_ref), custom_call_target="tpu_custom_call" | custom-call | tf_op jit(solution)/shard_map/pallas_call | solution.py:351
  99.9 0.9 slice.143
  100.9 0.7 slice_bitcast_fusion.6
  101.7 1.4 %slice_reduce_fusion = f32[]{:T(128)} fusion(f32[8,8,128]{2,1,0:T(8,128)} %get-tuple-element.19), kind=kLoop, calls=%fused_computation.66 | loop fusion | flops 7 | bytes 36 | tf_op jit(solution)/shard_map/reduce_sum | solution.py:407
  103.8 0.7 fusion.2
  104.5 1.0 slice.138
  105.5 0.7 slice_bitcast_fusion.7
  107.0 0.8 copy.42
  (49 shorter events, 2.7 us)
Async XLA Ops:
  2.7 23.7 %copy-start = (f32[2,32,512]{2,1,0:T(8,128)S(1)}, f32[2,32,512]{2,1,0:T(8,128)}, u32[]{:S(2)}) copy-start(f32[2,32,512]{2,1,0:T(8,128)} %param.9) | copy-start | bytes 393220
  2.7 23.7 %copy-start.1 = (f32[2,32,8,8]{1,3,2,0:T(8,128)S(1)}, f32[2,32,8,8]{1,3,2,0:T(8,128)}, u32[]{:S(2)}) copy-start(f32[2,32,8,8]{1,3,2,0:T(8,128)} %param.8) | copy-start | bytes 49156
  70.2 5.4 %copy-start.2 = (f32[8,16,256]{2,1,0:T(8,128)S(1)}, f32[8,16,256]{2,1,0:T(8,128)}, u32[]{:S(2)}) copy-start(f32[8,16,256]{2,1,0:T(8,128)} %get-tuple-element.18) | copy-start | bytes 393220

commit v14 on v13

--- a/solution.py
+++ b/solution.py
@@ -152,9 +152,9 @@
     chunks_y = width_y // ROWS
     chunks_z = width_z // LANES
 
-    def chunk(k, energy):
-        r0 = pl.multiple_of((k // chunks_z) * ROWS, ROWS)
-        c0 = pl.multiple_of((k % chunks_z) * LANES, LANES)
+    def chunk(ky, kz, energy):
+        r0 = ky * ROWS
+        c0 = pl.multiple_of(kz * LANES, LANES)
         rs = pl.ds(r0, ROWS)
         cs = pl.ds(c0, LANES)
         contrast = contrast_ref[0, rs, cs]
@@ -198,13 +198,15 @@
         zero = jnp.zeros((ROWS, LANES), jnp.float32)
         prod_acc, mis_acc, sq_acc, e_acc = lax.fori_loop(
             0, KNOT, plane, (zero, zero, zero, energy), unroll=4)
-        prod_ref[0, rs, cs] = prod_acc
-        mis_ref[0, rs, cs] = mis_acc
-        sq_ref[0, rs, cs] = sq_acc
+        for out_ref, acc in ((prod_ref, prod_acc), (mis_ref, mis_acc), (sq_ref, sq_acc)):
+            for n in range(ROWS // KNOT):
+                out_ref[0, pl.ds(r0 // KNOT + n, 1), cs] = jnp.sum(
+                    acc[n * KNOT : (n + 1) * KNOT], axis=0, keepdims=True)
         return e_acc
 
-    energy = lax.fori_loop(0, chunks_y * chunks_z, chunk,
-                           jnp.zeros((ROWS, LANES), jnp.float32))
+    energy = jnp.zeros((ROWS, LANES), jnp.float32)
+    for ky in range(chunks_y):
+        energy = lax.fori_loop(0, chunks_z, functools.partial(chunk, ky), energy)
     energy_ref[0] = energy
 
 
@@ -212,8 +214,9 @@
     depth_x, width_y, width_z = image.shape
     nodes = depth_x // KNOT
     f32 = jnp.float32
-    block_sum = jax.ShapeDtypeStruct((nodes, width_y, width_z), f32)
-    node_spec = pl.BlockSpec((1, width_y, width_z), lambda i: (i, 0, 0))
+    block_sum = jax.ShapeDtypeStruct((nodes, width_y // KNOT, width_z), f32)
+    node_spec = pl.BlockSpec((1, width_y // KNOT, width_z), lambda i: (i, 0, 0))
+    field_spec = pl.BlockSpec((1, width_y, width_z), lambda i: (i, 0, 0))
     plane_spec = pl.BlockSpec((KNOT, width_y, width_z), lambda i: (i, 0, 0))
     return pl.pallas_call(
         strip_kernel,
@@ -227,8 +230,8 @@
             pl.BlockSpec(memory_space=pltpu.VMEM),
             pl.BlockSpec((3, KNOT, width_y, width_z), lambda i: (0, i, 0, 0)),
             plane_spec,
-            node_spec,
-            node_spec,
+            field_spec,
+            field_spec,
         ],
         out_specs=[
             plane_spec,
@@ -254,8 +257,7 @@
 
 
 def node_sums(field):
-    nodes, width_y, width_z = field.shape
-    return field.reshape(nodes, width_y // KNOT, KNOT, width_z).sum(axis=2)
+    return field
 
 
 def exchange(axis, n, me, d, src, buffer, send_sem, recv_sem):

time: 108 us -> 111 us (1.028)
  matrix products: 1.87 us -> 7.28 us
  other arithmetic: 16.8 us -> 13.2 us
    reduce_sum x3 -> x0, other arithmetic: 4.49 us -> none  [node_sums(): return field.reshape(nodes, width_y // KNOT, KNOT, width_z).sum(axis=2)]
where the time goes in v14:
time: 111 us; the launch traced here: 110 us
  Pallas kernels  76 us (68%)
  other arithmetic  13.2 us (12%)
  local copies, waits for them, and re-layouts  11.4 us (10%)
  matrix products  7.28 us (7%)
  between operations  2.28 us (2%)
    pallas_call x1, Pallas kernels, strip_sums(): pl.pallas_call(strip_kernel, grid=(nodes,), in_specs=[pl.BlockSpec((1, wi...  42.3 us
    pallas_call x1, Pallas kernels, both_sums(): pl.pallas_call(functools.partial(both_sums_kernel, nz, ny, plane_row, dep...  19.8 us
    pallas_call x1, Pallas kernels, swap_halos(): pl.pallas_call(functools.partial(halo_kernel, ny, nz), out_shape=[jax.Sha...  13.9 us
    select_n x1, other arithmetic, halo_blocks(): jnp.where(lanes == 0, side_high[:, :, None], jnp.where(lanes == 127, side...  2.54 us

profile of v14, /device:TPU:1, one launch (start us, length us, event | category | flops | bytes accessed | tf_op | source)
XLA Modules:
  0.0 110.1 jit_solution(11061905670669995295)
XLA Ops:
  0.6 1.4 %fusion.21 = (bf16[64,1,512]{2,1,0:T(2,128)(2,1)S(1)}, bf16[64,1,512]{2,1,0:T(2,128)(2,1)S(1)}) fusion(bf16[64,64,512]{2,1,0:T(8,128)(2,1)} %next_ref.1), kind=kLoop, calls=%fused_computation.73 | loop fusion | bytes 262144 | tf_op jit(solution)/shard_map/slice | solution.py:89
  2.1 0.7 pad_maximum_fusion.2.rows_ref
  2.7 2.1 %fusion.20 = (bf16[64,64,1]{2,1,0:T(8,128)(2,1)S(1)}, bf16[64,64,1]{2,1,0:T(8,128)(2,1)S(1)}) fusion(bf16[64,64,512]{2,1,0:T(8,128)(2,1)} %next_ref.1), kind=kLoop, calls=%fused_computation.72 | loop fusion | bytes 32768 | tf_op jit(solution)/shard_map/slice | solution.py:90
  4.8 0.5 copy.46
  5.3 0.5 copy.47
  5.8 0.6 pad_maximum_fusion.3.cols_ref
  6.4 13.9 %shard_map.76 = (bf16[2,64,512]{2,1,0:T(8,128)(2,1)}, bf16[6,64,64]{2,1,0:T(8,128)(2,1)}) custom-call(bf16[2,64,512]{2,1,0:T(8,128)(2,1)} %pad_maximum_fusion.2.rows_ref, bf16[2,64,64]{2,1,0:T(8,128)(2,1)} %pad_maximum_fusion.3.cols_ref), custom_call_target="tpu_custom_call" | custom-call | tf_op jit(solution)/shard_map/pallas_call | solution.py:68
  20.3 0.8 multiply_bitcast_fusion.3
  21.6 2.5 %select_select_fusion.cols_ref = bf16[64,72,128]{2,1,0:T(8,128)(2,1)} fusion(pred[128]{0:T(512)(128)(4,1)S(1)} %get-tuple-element.48, pred[128]{0:T(512)(128)(4,1)S(1)} %get-tuple-element.49, bf16[64,72]{1,0:T(8,128)(2,1)S(1)} %get-tuple-element.45, bf16[64,72]{1,0:T(8,128)(2,1)S(1)} %get-tuple-element.44), kind=kLoop, calls=%fused_computation | loop fusion | flops 1179648 | bytes 1198336 | tf_op jit(solution)/shard_map/jit(_where)/select_n | solution.py:111
  24.1 0.9 multiply_bitcast_fusion.1
  25.3 1.2 %pad_maximum_fusion.rows_ref = bf16[64,8,512]{2,1,0:T(8,128)(2,1)} fusion(bf16[64,1,512]{2,1,0:T(2,128)(2,1)S(1)} %copy.39, bf16[64,1,512]{2,1,0:T(2,128)(2,1)S(1)} %copy.38, bf16[8]{0:T(256)(128)(2,1)S(1)} %pad.40.clone), kind=kLoop, calls=%fused_computation.6 | loop fusion | flops 1572864 | bytes 655376 | tf_op jit(solution)/shard_map/concatenate | solution.py:106
  26.4 0.3 fusion.4
  26.8 1.6 %broadcast_bitcast_fusion = (f32[8,64,512]{2,1,0:T(8,128)}, f32[8,64,512]{2,1,0:T(8,128)}) fusion(f32[8,8,512]{2,1,0:T(8,128)S(1)} %get-tuple-element.34, f32[8,8,512]{2,1,0:T(8,128)S(1)} %get-tuple-element.35), kind=kLoop, calls=%fused_computation.7 | loop fusion | bytes 2359296 | tf_op jit(solution)/shard_map/broadcast_in_dim | solution.py:376
  28.4 42.3 %shard_map.77 = (bf16[64,64,512]{2,1,0:T(8,128)(2,1)}, f32[8,8,512]{2,1,0:T(8,128)}, f32[8,8,512]{2,1,0:T(8,128)}, f32[8,8,512]{2,1,0:T(8,128)}, f32[8,16,256]{2,1,0:T(8,128)}) custom-call(bf16[64,64,512]{2,1,0:T(8,128)(2,1)} %next_ref.1, bf16[64,64,512]{2,1,0:T(8,128)(2,1)} %next_ref.1, bf16[64,64,512]{2,1,0:T(8,128)(2,1)} %next_ref.1, ...), custom_call_target="tpu_custom_call" | custom-call | tf_op jit(solution)/shard_map/pallas_call | solution.py:221
  70.7 1.2 %convolution_bitcast_fusion.1 = f32[1,32,512]{2,1,0:T(8,128)S(1)} fusion(f32[8,8,512]{2,1,0:T(8,128)} %get-tuple-element.16, f32[2,32,8,8]{1,3,2,0:T(8,128)S(1)} %copy-done.1), kind=kOutput, calls=%fused_computation.2 | convolution fusion | flops 12582912 | bytes 229376 | tf_op jit(solution)/shard_map/rij,ijz->rz/dot_general | solution.py:385
  71.9 1.2 %convolution_bitcast_fusion.2 = f32[1,32,512]{2,1,0:T(8,128)S(1)} fusion(f32[8,8,512]{2,1,0:T(8,128)} %get-tuple-element.15, f32[2,32,8,8]{1,3,2,0:T(8,128)S(1)} %copy-done.1), kind=kOutput, calls=%fused_computation.3 | convolution fusion | flops 12582912 | bytes 229376 | tf_op jit(solution)/shard_map/rij,ijz->rz/dot_general | solution.py:384
  73.1 1.2 %convolution_bitcast_fusion = f32[4,4,8,128]{3,2,1,0:T(8,128)S(1)} fusion(f32[8,8,512]{2,1,0:T(8,128)} %get-tuple-element.17, f32[2,32,8,8]{1,3,2,0:T(8,128)S(1)} %copy-done.1), kind=kOutput, calls=%fused_computation.1 | convolution fusion | flops 12584960 | bytes 229376 | tf_op jit(solution)/shard_map/rij,ijz->rz/dot_general | solution.py:386
  74.3 1.5 %reduce_sum.38 = f32[]{:T(128)} reduce(f32[8,16,256]{2,1,0:T(8,128)} %get-tuple-element.18, f32[]{:T(128)} %constant.12.clone.1), dimensions={0,1,2}, to_apply=%region_2.3 | reduce | flops 32767 | bytes 131080 | tf_op jit(solution)/shard_map/reduce_sum | solution.py:380
  75.9 0.7 select_maximum_fusion
  76.7 0.8 maximum_maximum_fusion.depth_ref
  77.5 1.1 %convolution_bitcast_fusion.3 = f32[1,32,8,8]{1,3,2,0:T(8,128)S(1)} fusion(f32[8,8,512]{2,1,0:T(8,128)} %get-tuple-element.16, f32[2,32,512]{2,1,0:T(8,128)S(1)} %copy-done), kind=kOutput, calls=%fused_computation.4 | convolution fusion | flops 12582912 | bytes 204800 | tf_op jit(solution)/shard_map/rz,ijz->rij/dot_general | solution.py:390
  78.6 1.2 %convolution_bitcast_fusion.4 = f32[1,32,8,8]{1,3,2,0:T(8,128)S(1)} fusion(f32[8,8,512]{2,1,0:T(8,128)} %get-tuple-element.15, f32[2,32,512]{2,1,0:T(8,128)S(1)} %copy-done), kind=kOutput, calls=%fused_computation.5 | convolution fusion | flops 12582912 | bytes 204800 | tf_op jit(solution)/shard_map/rz,ijz->rij/dot_general | solution.py:389
  80.1 1.2 %fusion.6 = f32[32,8,8]{0,2,1:T(8,128)S(1)} fusion(f32[8,8,512]{2,1,0:T(8,128)} %get-tuple-element.17, f32[2,32,512]{2,1,0:T(8,128)S(1)} %copy-done), kind=kOutput, calls=%fused_computation.28 | convolution fusion | flops 12599296 | bytes 204800 | tf_op jit(solution)/shard_map/rz,ijz->rij/dot_general | solution.py:391
  81.8 0.7 maximum_maximum_fusion.1.plane_ref
  82.5 19.8 %shard_map.78 = (f32[8,8,128]{2,1,0:T(8,128)}, f32[16,32,128]{2,1,0:T(8,128)}) custom-call(f32[8,8,128]{2,1,0:T(8,128)} %maximum_maximum_fusion.1.plane_ref, f32[16,32,128]{2,1,0:T(8,128)} %maximum_maximum_fusion.depth_ref), custom_call_target="tpu_custom_call" | custom-call | tf_op jit(solution)/shard_map/pallas_call | solution.py:353
  102.3 0.9 slice.143
  103.3 0.7 slice_bitcast_fusion.6
  104.0 1.4 %slice_reduce_fusion = f32[]{:T(128)} fusion(f32[8,8,128]{2,1,0:T(8,128)} %get-tuple-element.19), kind=kLoop, calls=%fused_computation.63 | loop fusion | flops 7 | bytes 36 | tf_op jit(solution)/shard_map/reduce_sum | solution.py:409
  106.1 0.7 fusion.2
  106.8 1.0 slice.138
  107.8 0.7 slice_bitcast_fusion.7
  109.3 0.8 copy.42
  (44 shorter events, 2.0 us)
Async XLA Ops:
  2.7 23.7 %copy-start = (f32[2,32,512]{2,1,0:T(8,128)S(1)}, f32[2,32,512]{2,1,0:T(8,128)}, u32[]{:S(2)}) copy-start(f32[2,32,512]{2,1,0:T(8,128)} %param.9) | copy-start | bytes 393220
  2.7 23.7 %copy-start.1 = (f32[2,32,8,8]{1,3,2,0:T(8,128)S(1)}, f32[2,32,8,8]{1,3,2,0:T(8,128)}, u32[]{:S(2)}) copy-start(f32[2,32,8,8]{1,3,2,0:T(8,128)} %param.8) | copy-start | bytes 49156

commit v15 on v13

--- a/solution.py
+++ b/solution.py
@@ -16,6 +16,7 @@
 
 ROWS = 16
 LANES = 256
+SPAN = 16
 
 
 def neighbours(part, axis, forward):
@@ -126,7 +127,7 @@
     pad_y, pad_z = pad_ref.shape
 
     def source_plane(p, plane):
-        plane_x = block * KNOT - 1 + p
+        plane_x = block * SPAN - 1 + p
         valid = jnp.logical_and(plane_x >= 0, plane_x < depth_x)
         safe = jnp.clip(plane_x, 0, depth_x - 1)
         pad_ref[:width_y, :width_z] = plane.astype(jnp.float32)
@@ -146,21 +147,22 @@
         source_plane(p, main_ref[p - 1])
         return carry
 
-    lax.fori_loop(1, KNOT + 1, inner_plane, 0, unroll=2)
-    source_plane(KNOT + 1, next_ref[0])
+    lax.fori_loop(1, SPAN + 1, inner_plane, 0, unroll=2)
+    source_plane(SPAN + 1, next_ref[0])
 
     chunks_y = width_y // ROWS
     chunks_z = width_z // LANES
 
-    def chunk(k, energy):
+    def chunk(n, k, energy):
         r0 = pl.multiple_of((k // chunks_z) * ROWS, ROWS)
         c0 = pl.multiple_of((k % chunks_z) * LANES, LANES)
         rs = pl.ds(r0, ROWS)
         cs = pl.ds(c0, LANES)
-        contrast = contrast_ref[0, rs, cs]
-        bright = bright_ref[0, rs, cs]
-
-        def plane(xl, acc):
+        contrast = contrast_ref[n, rs, cs]
+        bright = bright_ref[n, rs, cs]
+
+        def plane(step, acc):
+            xl = n * KNOT + step
             prod_acc, mis_acc, sq_acc, e_acc = acc
 
             def src(a, b, c):
@@ -198,34 +200,37 @@
         zero = jnp.zeros((ROWS, LANES), jnp.float32)
         prod_acc, mis_acc, sq_acc, e_acc = lax.fori_loop(
             0, KNOT, plane, (zero, zero, zero, energy), unroll=4)
-        prod_ref[0, rs, cs] = prod_acc
-        mis_ref[0, rs, cs] = mis_acc
-        sq_ref[0, rs, cs] = sq_acc
+        prod_ref[n, rs, cs] = prod_acc
+        mis_ref[n, rs, cs] = mis_acc
+        sq_ref[n, rs, cs] = sq_acc
         return e_acc
 
-    energy = lax.fori_loop(0, chunks_y * chunks_z, chunk,
-                           jnp.zeros((ROWS, LANES), jnp.float32))
+    energy = jnp.zeros((ROWS, LANES), jnp.float32)
+    for n in range(SPAN // KNOT):
+        energy = lax.fori_loop(0, chunks_y * chunks_z, functools.partial(chunk, n), energy)
     energy_ref[0] = energy
 
 
 def strip_sums(deformed, rows, cols, displacement, image, contrast_y, bright_y):
     depth_x, width_y, width_z = image.shape
     nodes = depth_x // KNOT
+    steps = depth_x // SPAN
+    per = SPAN // KNOT
     f32 = jnp.float32
     block_sum = jax.ShapeDtypeStruct((nodes, width_y, width_z), f32)
-    node_spec = pl.BlockSpec((1, width_y, width_z), lambda i: (i, 0, 0))
-    plane_spec = pl.BlockSpec((KNOT, width_y, width_z), lambda i: (i, 0, 0))
+    node_spec = pl.BlockSpec((per, width_y, width_z), lambda i: (i, 0, 0))
+    plane_spec = pl.BlockSpec((SPAN, width_y, width_z), lambda i: (i, 0, 0))
     return pl.pallas_call(
         strip_kernel,
-        grid=(nodes,),
+        grid=(steps,),
         in_specs=[
-            pl.BlockSpec((1, width_y, width_z), lambda i: (jnp.maximum(i * KNOT - 1, 0), 0, 0)),
+            pl.BlockSpec((1, width_y, width_z), lambda i: (jnp.maximum(i * SPAN - 1, 0), 0, 0)),
             plane_spec,
             pl.BlockSpec((1, width_y, width_z),
-                         lambda i: (jnp.minimum(i * KNOT + KNOT, depth_x - 1), 0, 0)),
+                         lambda i: (jnp.minimum(i * SPAN + SPAN, depth_x - 1), 0, 0)),
             pl.BlockSpec(memory_space=pltpu.VMEM),
             pl.BlockSpec(memory_space=pltpu.VMEM),
-            pl.BlockSpec((3, KNOT, width_y, width_z), lambda i: (0, i, 0, 0)),
+            pl.BlockSpec((3, SPAN, width_y, width_z), lambda i: (0, i, 0, 0)),
             plane_spec,
             node_spec,
             node_spec,
@@ -242,11 +247,11 @@
             block_sum,
             block_sum,
             block_sum,
-            jax.ShapeDtypeStruct((nodes, ROWS, LANES), f32),
+            jax.ShapeDtypeStruct((steps, ROWS, LANES), f32),
         ],
         scratch_shapes=[
             pltpu.VMEM((width_y + rows.shape[1], width_z + cols.shape[2]), f32),
-            pltpu.VMEM((KNOT + 2, 9, width_y, width_z), f32),
+            pltpu.VMEM((SPAN + 2, 9, width_y, width_z), f32),
         ],
         compiler_params=pltpu.CompilerParams(
             dimension_semantics=("arbitrary",), vmem_limit_bytes=60 * 1024 * 1024),

time: 108 us -> 107 us (level)
  Pallas kernels: 75.4 us -> 74 us
    pallas_call x1, Pallas kernels: 41.7 us -> 40.3 us  [strip_sums(): pl.pallas_call(strip_kernel, grid=(steps,), in_specs=[pl.BlockSpec((1, wi...]
where the time goes in v15:
time: 107 us; the launch traced here: 106 us
  Pallas kernels  74 us (69%)
  other arithmetic  16.8 us (16%)
  local copies, waits for them, and re-layouts  11.4 us (11%)
  between operations  2.3 us (2%)
  matrix products  1.86 us (2%)
    pallas_call x1, Pallas kernels, strip_sums(): pl.pallas_call(strip_kernel, grid=(steps,), in_specs=[pl.BlockSpec((1, wi...  40.3 us
    pallas_call x1, Pallas kernels, both_sums(): pl.pallas_call(functools.partial(both_sums_kernel, nz, ny, plane_row, dep...  19.7 us
    pallas_call x1, Pallas kernels, swap_halos(): pl.pallas_call(functools.partial(halo_kernel, ny, nz), out_shape=[jax.Sha...  13.9 us
    reduce_sum x3, other arithmetic, node_sums(): return field.reshape(nodes, width_y // KNOT, KNOT, width_z).sum(axis=2)  4.48 us
    select_n x1, other arithmetic, halo_blocks(): jnp.where(lanes == 0, side_high[:, :, None], jnp.where(lanes == 127, side...  2.58 us

profile of v15, /device:TPU:1, one launch (start us, length us, event | category | flops | bytes accessed | tf_op | source)
XLA Modules:
  0.0 106.3 jit_solution(2372374884489364532)
XLA Ops:
  0.6 1.4 %fusion.21 = (bf16[64,1,512]{2,1,0:T(2,128)(2,1)S(1)}, bf16[64,1,512]{2,1,0:T(2,128)(2,1)S(1)}) fusion(bf16[64,64,512]{2,1,0:T(8,128)(2,1)} %next_ref.1), kind=kLoop, calls=%fused_computation.76 | loop fusion | bytes 262144 | tf_op jit(solution)/shard_map/slice | solution.py:90
  2.1 0.7 pad_maximum_fusion.2.rows_ref
  2.7 2.1 %fusion.20 = (bf16[64,64,1]{2,1,0:T(8,128)(2,1)S(1)}, bf16[64,64,1]{2,1,0:T(8,128)(2,1)S(1)}) fusion(bf16[64,64,512]{2,1,0:T(8,128)(2,1)} %next_ref.1), kind=kLoop, calls=%fused_computation.75 | loop fusion | bytes 32768 | tf_op jit(solution)/shard_map/slice | solution.py:91
  4.8 0.5 copy.46
  5.3 0.5 copy.47
  5.8 0.6 pad_maximum_fusion.3.cols_ref
  6.4 13.9 %shard_map.76 = (bf16[2,64,512]{2,1,0:T(8,128)(2,1)}, bf16[6,64,64]{2,1,0:T(8,128)(2,1)}) custom-call(bf16[2,64,512]{2,1,0:T(8,128)(2,1)} %pad_maximum_fusion.2.rows_ref, bf16[2,64,64]{2,1,0:T(8,128)(2,1)} %pad_maximum_fusion.3.cols_ref), custom_call_target="tpu_custom_call" | custom-call | tf_op jit(solution)/shard_map/pallas_call | solution.py:69
  20.3 0.8 multiply_bitcast_fusion.3
  21.6 2.6 %select_select_fusion.cols_ref = bf16[64,72,128]{2,1,0:T(8,128)(2,1)} fusion(pred[128]{0:T(512)(128)(4,1)S(1)} %get-tuple-element.48, pred[128]{0:T(512)(128)(4,1)S(1)} %get-tuple-element.49, bf16[64,72]{1,0:T(8,128)(2,1)S(1)} %get-tuple-element.45, bf16[64,72]{1,0:T(8,128)(2,1)S(1)} %get-tuple-element.44), kind=kLoop, calls=%fused_computation | loop fusion | flops 1179648 | bytes 1198336 | tf_op jit(solution)/shard_map/jit(_where)/select_n | solution.py:112
  24.1 0.9 multiply_bitcast_fusion.1
  25.3 1.2 %pad_maximum_fusion.rows_ref = bf16[64,8,512]{2,1,0:T(8,128)(2,1)} fusion(bf16[64,1,512]{2,1,0:T(2,128)(2,1)S(1)} %copy.39, bf16[64,1,512]{2,1,0:T(2,128)(2,1)S(1)} %copy.38, bf16[8]{0:T(256)(128)(2,1)S(1)} %pad.40.clone), kind=kLoop, calls=%fused_computation.9 | loop fusion | flops 1572864 | bytes 655376 | tf_op jit(solution)/shard_map/concatenate | solution.py:107
  26.5 0.3 fusion.4
  26.9 1.6 %broadcast_bitcast_fusion = (f32[8,64,512]{2,1,0:T(8,128)}, f32[8,64,512]{2,1,0:T(8,128)}) fusion(f32[8,8,512]{2,1,0:T(8,128)S(1)} %get-tuple-element.34, f32[8,8,512]{2,1,0:T(8,128)S(1)} %get-tuple-element.35), kind=kLoop, calls=%fused_computation.10 | loop fusion | bytes 2359296 | tf_op jit(solution)/shard_map/broadcast_in_dim | solution.py:379
  28.5 40.3 %shard_map.77 = (bf16[64,64,512]{2,1,0:T(8,128)(2,1)}, f32[8,64,512]{2,1,0:T(8,128)}, f32[8,64,512]{2,1,0:T(8,128)}, f32[8,64,512]{2,1,0:T(8,128)}, f32[4,16,256]{2,1,0:T(8,128)}) custom-call(bf16[64,64,512]{2,1,0:T(8,128)(2,1)} %next_ref.1, bf16[64,64,512]{2,1,0:T(8,128)(2,1)} %next_ref.1, bf16[64,64,512]{2,1,0:T(8,128)(2,1)} %next_ref.1, ...), custom_call_target="tpu_custom_call" | custom-call | tf_op jit(solution)/shard_map/pallas_call | solution.py:223
  68.8 1.5 %bitcast_reduce_fusion.1 = f32[8,8,512]{2,1,0:T(8,128)S(1)} fusion(f32[8,64,512]{2,1,0:T(8,128)} %get-tuple-element.16), kind=kLoop, calls=%fused_computation.7 | loop fusion | flops 229376 | bytes 1179648 | tf_op jit(solution)/shard_map/reduce_sum | solution.py:263
  70.3 0.3 convolution_bitcast_fusion.1
  70.6 1.5 %bitcast_reduce_fusion.2 = f32[8,8,512]{2,1,0:T(8,128)S(1)} fusion(f32[8,64,512]{2,1,0:T(8,128)} %get-tuple-element.15), kind=kLoop, calls=%fused_computation.8 | loop fusion | flops 229376 | bytes 1179648 | tf_op jit(solution)/shard_map/reduce_sum | solution.py:263
  72.0 0.3 convolution_bitcast_fusion.2
  72.4 1.5 %bitcast_reduce_fusion = f32[8,8,512]{2,1,0:T(8,128)S(1)} fusion(f32[8,64,512]{2,1,0:T(8,128)} %get-tuple-element.17), kind=kLoop, calls=%fused_computation.6 | loop fusion | flops 229376 | bytes 1179648 | tf_op jit(solution)/shard_map/reduce_sum | solution.py:263
  73.9 0.3 convolution_bitcast_fusion
  74.2 0.6 reduce_sum.68
  74.8 0.7 select_maximum_fusion
  75.6 0.8 maximum_maximum_fusion.depth_ref
  78.0 0.7 maximum_maximum_fusion.1.plane_ref
  78.7 19.7 %shard_map.78 = (f32[8,8,128]{2,1,0:T(8,128)}, f32[16,32,128]{2,1,0:T(8,128)}) custom-call(f32[8,8,128]{2,1,0:T(8,128)} %maximum_maximum_fusion.1.plane_ref, f32[16,32,128]{2,1,0:T(8,128)} %maximum_maximum_fusion.depth_ref), custom_call_target="tpu_custom_call" | custom-call | tf_op jit(solution)/shard_map/pallas_call | solution.py:356
  98.5 0.9 slice.143
  99.5 0.7 slice_bitcast_fusion.6
  100.3 1.4 %slice_reduce_fusion = f32[]{:T(128)} fusion(f32[8,8,128]{2,1,0:T(8,128)} %get-tuple-element.19), kind=kLoop, calls=%fused_computation.66 | loop fusion | flops 7 | bytes 36 | tf_op jit(solution)/shard_map/reduce_sum | solution.py:412
  102.4 0.7 fusion.2
  103.0 1.0 slice.138
  104.0 0.7 slice_bitcast_fusion.7
  105.6 0.8 copy.42
  (49 shorter events, 2.7 us)
Async XLA Ops:
  2.7 23.7 %copy-start = (f32[2,32,512]{2,1,0:T(8,128)S(1)}, f32[2,32,512]{2,1,0:T(8,128)}, u32[]{:S(2)}) copy-start(f32[2,32,512]{2,1,0:T(8,128)} %param.9) | copy-start | bytes 393220
  2.7 23.7 %copy-start.1 = (f32[2,32,8,8]{1,3,2,0:T(8,128)S(1)}, f32[2,32,8,8]{1,3,2,0:T(8,128)}, u32[]{:S(2)}) copy-start(f32[2,32,8,8]{1,3,2,0:T(8,128)} %param.8) | copy-start | bytes 49156
  68.8 5.4 %copy-start.2 = (f32[4,16,256]{2,1,0:T(8,128)S(1)}, f32[4,16,256]{2,1,0:T(8,128)}, u32[]{:S(2)}) copy-start(f32[4,16,256]{2,1,0:T(8,128)} %get-tuple-element.18) | copy-start | bytes 196612

commit v16 on v15

--- a/solution.py
+++ b/solution.py
@@ -147,7 +147,7 @@
         source_plane(p, main_ref[p - 1])
         return carry
 
-    lax.fori_loop(1, SPAN + 1, inner_plane, 0, unroll=2)
+    lax.fori_loop(1, SPAN + 1, inner_plane, 0, unroll=4)
     source_plane(SPAN + 1, next_ref[0])
 
     chunks_y = width_y // ROWS
@@ -332,6 +332,13 @@
         arrival("gz", nz, mz, d, plane_summed, plane_gathered, zr2).wait_recv()
         source = lax.rem(mz + nz - d, nz)
         plane_out[source] = plane_gathered[source]
+    gathered = plane_out[...]
+    chunk_row = lax.broadcasted_iota(jnp.int32, gathered.shape, 1)
+    chunk_lane = lax.broadcasted_iota(jnp.int32, gathered.shape, 2)
+    total_energy = jnp.sum(jnp.where(
+        jnp.logical_and(chunk_row == plane_row, chunk_lane == RANK), gathered, 0.0))
+    plane_out[0] = jnp.where(jnp.logical_and(rows == plane_row, lanes == RANK + 1),
+                             total_energy, gathered[0])
     for d in range(1, ny):
         arrival("gy", ny, my, d, depth_summed, depth_gathered, yr2).wait_recv()
         source = lax.rem(my + ny - d, ny)
@@ -409,7 +416,7 @@
     first_depth = depth_terms[grad_depth.size : grad_depth.size + first_depth.size].reshape(first_depth.shape)
     depth_level = plane_summed[0, plane_rows, :RANK]
     level_sum = depth_summed[0, depth_rows, :RANK]
-    energy = jnp.sum(plane_summed[:, plane_rows, RANK])
+    energy = plane_summed[0, plane_rows, RANK + 1]
 
     nodes_x = plane_factors.shape[2]
     nodes_y = plane_factors.shape[3] * lax.axis_size("gy")

time: 107 us -> 106 us (level)
  other arithmetic: 16.8 us -> 15.3 us
  local copies, waits for them, and re-layouts: 11.4 us -> 12.7 us
  Pallas kernels: 74 us -> 72.9 us
    reduce_sum x1 -> x0, other arithmetic: 1.44 us -> none  [local(): energy = jnp.sum(plane_summed[:, plane_rows, RANK])]
    slice x0 -> x1, local copies, waits for them, and re-layouts: none -> 1.26 us  [local(): energy = plane_summed[0, plane_rows, RANK + 1]]
where the time goes in v16:
time: 106 us; the launch traced here: 105 us
  Pallas kernels  72.9 us (69%)
  other arithmetic  15.3 us (14%)
  local copies, waits for them, and re-layouts  12.7 us (12%)
  between operations  2.3 us (2%)
  matrix products  1.87 us (2%)
    pallas_call x1, Pallas kernels, strip_sums(): pl.pallas_call(strip_kernel, grid=(steps,), in_specs=[pl.BlockSpec((1, wi...  39.3 us
    pallas_call x1, Pallas kernels, both_sums(): pl.pallas_call(functools.partial(both_sums_kernel, nz, ny, plane_row, dep...  19.7 us
    pallas_call x1, Pallas kernels, swap_halos(): pl.pallas_call(functools.partial(halo_kernel, ny, nz), out_shape=[jax.Sha...  13.9 us
    reduce_sum x3, other arithmetic, node_sums(): return field.reshape(nodes, width_y // KNOT, KNOT, width_z).sum(axis=2)  4.48 us
    select_n x1, other arithmetic, halo_blocks(): jnp.where(lanes == 0, side_high[:, :, None], jnp.where(lanes == 127, side...  2.58 us

profile of v16, /device:TPU:1, one launch (start us, length us, event | category | flops | bytes accessed | tf_op | source)
XLA Modules:
  0.0 105.1 jit_solution(1541103311734718052)
XLA Ops:
  0.6 1.4 %fusion.21 = (bf16[64,1,512]{2,1,0:T(2,128)(2,1)S(1)}, bf16[64,1,512]{2,1,0:T(2,128)(2,1)S(1)}) fusion(bf16[64,64,512]{2,1,0:T(8,128)(2,1)} %next_ref.1), kind=kLoop, calls=%fused_computation.75 | loop fusion | bytes 262144 | tf_op jit(solution)/shard_map/slice | solution.py:90
  2.1 0.7 pad_maximum_fusion.2.rows_ref
  2.7 2.1 %fusion.20 = (bf16[64,64,1]{2,1,0:T(8,128)(2,1)S(1)}, bf16[64,64,1]{2,1,0:T(8,128)(2,1)S(1)}) fusion(bf16[64,64,512]{2,1,0:T(8,128)(2,1)} %next_ref.1), kind=kLoop, calls=%fused_computation.74 | loop fusion | bytes 32768 | tf_op jit(solution)/shard_map/slice | solution.py:91
  4.8 0.5 copy.46
  5.3 0.5 copy.47
  5.8 0.6 pad_maximum_fusion.3.cols_ref
  6.4 13.9 %shard_map.76 = (bf16[2,64,512]{2,1,0:T(8,128)(2,1)}, bf16[6,64,64]{2,1,0:T(8,128)(2,1)}) custom-call(bf16[2,64,512]{2,1,0:T(8,128)(2,1)} %pad_maximum_fusion.2.rows_ref, bf16[2,64,64]{2,1,0:T(8,128)(2,1)} %pad_maximum_fusion.3.cols_ref), custom_call_target="tpu_custom_call" | custom-call | tf_op jit(solution)/shard_map/pallas_call | solution.py:69
  20.3 0.8 multiply_bitcast_fusion.3
  21.6 2.6 %select_select_fusion.cols_ref = bf16[64,72,128]{2,1,0:T(8,128)(2,1)} fusion(pred[128]{0:T(512)(128)(4,1)S(1)} %get-tuple-element.48, pred[128]{0:T(512)(128)(4,1)S(1)} %get-tuple-element.49, bf16[64,72]{1,0:T(8,128)(2,1)S(1)} %get-tuple-element.45, bf16[64,72]{1,0:T(8,128)(2,1)S(1)} %get-tuple-element.44), kind=kLoop, calls=%fused_computation | loop fusion | flops 1179648 | bytes 1198336 | tf_op jit(solution)/shard_map/jit(_where)/select_n | solution.py:112
  24.1 0.9 multiply_bitcast_fusion.1
  25.3 1.2 %pad_maximum_fusion.rows_ref = bf16[64,8,512]{2,1,0:T(8,128)(2,1)} fusion(bf16[64,1,512]{2,1,0:T(2,128)(2,1)S(1)} %copy.39, bf16[64,1,512]{2,1,0:T(2,128)(2,1)S(1)} %copy.38, bf16[8]{0:T(256)(128)(2,1)S(1)} %pad.40.clone), kind=kLoop, calls=%fused_computation.9 | loop fusion | flops 1572864 | bytes 655376 | tf_op jit(solution)/shard_map/concatenate | solution.py:107
  26.5 0.3 fusion.4
  26.9 1.6 %broadcast_bitcast_fusion = (f32[8,64,512]{2,1,0:T(8,128)}, f32[8,64,512]{2,1,0:T(8,128)}) fusion(f32[8,8,512]{2,1,0:T(8,128)S(1)} %get-tuple-element.34, f32[8,8,512]{2,1,0:T(8,128)S(1)} %get-tuple-element.35), kind=kLoop, calls=%fused_computation.10 | loop fusion | bytes 2359296 | tf_op jit(solution)/shard_map/broadcast_in_dim | solution.py:386
  28.5 39.3 %shard_map.77 = (bf16[64,64,512]{2,1,0:T(8,128)(2,1)}, f32[8,64,512]{2,1,0:T(8,128)}, f32[8,64,512]{2,1,0:T(8,128)}, f32[8,64,512]{2,1,0:T(8,128)}, f32[4,16,256]{2,1,0:T(8,128)}) custom-call(bf16[64,64,512]{2,1,0:T(8,128)(2,1)} %next_ref.1, bf16[64,64,512]{2,1,0:T(8,128)(2,1)} %next_ref.1, bf16[64,64,512]{2,1,0:T(8,128)(2,1)} %next_ref.1, ...), custom_call_target="tpu_custom_call" | custom-call | tf_op jit(solution)/shard_map/pallas_call | solution.py:223
  67.8 1.5 %bitcast_reduce_fusion.1 = f32[8,8,512]{2,1,0:T(8,128)S(1)} fusion(f32[8,64,512]{2,1,0:T(8,128)} %get-tuple-element.16), kind=kLoop, calls=%fused_computation.7 | loop fusion | flops 229376 | bytes 1179648 | tf_op jit(solution)/shard_map/reduce_sum | solution.py:263
  69.5 1.5 %bitcast_reduce_fusion.2 = f32[8,8,512]{2,1,0:T(8,128)S(1)} fusion(f32[8,64,512]{2,1,0:T(8,128)} %get-tuple-element.15), kind=kLoop, calls=%fused_computation.8 | loop fusion | flops 229376 | bytes 1179648 | tf_op jit(solution)/shard_map/reduce_sum | solution.py:263
  71.0 0.3 convolution_bitcast_fusion.2
  71.3 1.5 %bitcast_reduce_fusion = f32[8,8,512]{2,1,0:T(8,128)S(1)} fusion(f32[8,64,512]{2,1,0:T(8,128)} %get-tuple-element.17), kind=kLoop, calls=%fused_computation.6 | loop fusion | flops 229376 | bytes 1179648 | tf_op jit(solution)/shard_map/reduce_sum | solution.py:263
  72.8 0.3 convolution_bitcast_fusion
  73.2 0.6 reduce_sum.59
  73.8 0.7 select_maximum_fusion
  74.6 0.8 maximum_maximum_fusion.depth_ref
  76.2 0.3 fusion.6
  77.0 0.7 maximum_maximum_fusion.1.plane_ref
  77.7 19.7 %shard_map.78 = (f32[8,8,128]{2,1,0:T(8,128)}, f32[16,32,128]{2,1,0:T(8,128)}) custom-call(f32[8,8,128]{2,1,0:T(8,128)} %maximum_maximum_fusion.1.plane_ref, f32[16,32,128]{2,1,0:T(8,128)} %maximum_maximum_fusion.depth_ref), custom_call_target="tpu_custom_call" | custom-call | tf_op jit(solution)/shard_map/pallas_call | solution.py:363
  97.5 0.9 slice.143
  98.5 0.7 slice_bitcast_fusion.6
  99.2 1.3 %slice.142 = f32[1,1,1]{2,1,0:T(1,128)} slice(f32[8,8,128]{2,1,0:T(8,128)} %get-tuple-element.19), slice={[0:1], [6:7], [33:34]} | slice | bytes 8 | tf_op jit(solution)/shard_map/slice | solution.py:419
  101.2 0.7 fusion.2
  101.9 1.0 slice.138
  102.9 0.7 slice_bitcast_fusion.7
  104.4 0.8 copy.42
  (49 shorter events, 2.7 us)
Async XLA Ops:
  2.7 23.7 %copy-start = (f32[2,32,512]{2,1,0:T(8,128)S(1)}, f32[2,32,512]{2,1,0:T(8,128)}, u32[]{:S(2)}) copy-start(f32[2,32,512]{2,1,0:T(8,128)} %param.9) | copy-start | bytes 393220
  2.7 23.7 %copy-start.1 = (f32[2,32,8,8]{1,3,2,0:T(8,128)S(1)}, f32[2,32,8,8]{1,3,2,0:T(8,128)}, u32[]{:S(2)}) copy-start(f32[2,32,8,8]{1,3,2,0:T(8,128)} %param.8) | copy-start | bytes 49156
  67.7 5.4 %copy-start.2 = (f32[4,16,256]{2,1,0:T(8,128)S(1)}, f32[4,16,256]{2,1,0:T(8,128)}, u32[]{:S(2)}) copy-start(f32[4,16,256]{2,1,0:T(8,128)} %get-tuple-element.18) | copy-start | bytes 196612

commit v17 on v16

--- a/solution.py
+++ b/solution.py
@@ -88,7 +88,7 @@
     ny, nz = lax.axis_size("gy"), lax.axis_size("gz")
     my, mz = lax.axis_index("gy"), lax.axis_index("gz")
     rows_send = jnp.stack([deformed[:, 0, :], deformed[:, width_y - 1, :]])
-    cols_send = jnp.stack([deformed[:, :, 0], deformed[:, :, width_z - 1]])
+    cols_send = jnp.transpose(deformed[:, :, :: width_z - 1], (2, 0, 1))
     rows_got, cols_got = swap_halos(rows_send, cols_send)
     held = deformed.dtype
     has_up = (my < ny - 1).astype(held)

time: 106 us -> 108 us (1.019)
  local copies, waits for them, and re-layouts: 12.7 us -> 18.5 us
  other arithmetic: 15.3 us -> 11.4 us
    slice x1, local copies, waits for them, and re-layouts: 2.06 us -> 8.76 us  [halo_blocks(): cols_send = jnp.transpose(deformed[:, :, ::width_z - 1], (2, 0, 1))]
    reduce_sum x3, other arithmetic: 4.48 us -> 2.07 us  [node_sums(): return field.reshape(nodes, width_y // KNOT, KNOT, width_z).sum(axis=2)]
    unnamed x11 -> x18, local copies, waits for them, and re-layouts: 1.77 us -> 2.31 us
where the time goes in v17:
time: 108 us; the launch traced here: 107 us
  Pallas kernels  73 us (68%)
  local copies, waits for them, and re-layouts  18.5 us (17%)
  other arithmetic  11.4 us (11%)
  between operations  2.36 us (2%)
  matrix products  1.86 us (2%)
    pallas_call x1, Pallas kernels, strip_sums(): pl.pallas_call(strip_kernel, grid=(steps,), in_specs=[pl.BlockSpec((1, wi...  39.3 us
    pallas_call x1, Pallas kernels, both_sums(): pl.pallas_call(functools.partial(both_sums_kernel, nz, ny, plane_row, dep...  19.8 us
    pallas_call x1, Pallas kernels, swap_halos(): pl.pallas_call(functools.partial(halo_kernel, ny, nz), out_shape=[jax.Sha...  13.9 us
    slice x1, local copies, waits for them, and re-layouts, halo_blocks(): cols_send = jnp.transpose(deformed[:, :, ::width_z - 1], (2, 0, 1))  8.76 us
    select_n x1, other arithmetic, halo_blocks(): jnp.where(lanes == 0, side_high[:, :, None], jnp.where(lanes == 127, side...  2.58 us
    unnamed x18, local copies, waits for them, and re-layouts  2.31 us

profile of v17, /device:TPU:1, one launch (start us, length us, event | category | flops | bytes accessed | tf_op | source)
XLA Modules:
  0.0 107.1 jit_solution(6000922935706072991)
XLA Ops:
  0.6 1.4 %fusion.20 = (bf16[64,1,512]{2,1,0:T(2,128)(2,1)S(1)}, bf16[64,1,512]{2,1,0:T(2,128)(2,1)S(1)}) fusion(bf16[64,64,512]{2,1,0:T(8,128)(2,1)} %next_ref.1), kind=kLoop, calls=%fused_computation.73 | loop fusion | bytes 262144 | tf_op jit(solution)/shard_map/slice | solution.py:90
  2.1 0.7 pad_maximum_fusion.2.rows_ref
  2.7 8.8 %slice.112 = bf16[64,64,2]{2,1,0:T(8,128)(2,1)S(1)} slice(bf16[64,64,512]{2,1,0:T(8,128)(2,1)} %next_ref.1), slice={[0:64:1], [0:64:1], [0:512:511]} | slice | bytes 32768 | tf_op jit(solution)/shard_map/slice | solution.py:91
  11.5 1.1 %copy.42 = bf16[64,64,2]{1,0,2:T(8,128)(2,1)} copy(bf16[64,64,2]{2,1,0:T(8,128)(2,1)S(1)} %slice.112) | data formatting | bytes 32768
  12.6 13.9 %shard_map.76 = (bf16[2,64,512]{2,1,0:T(8,128)(2,1)}, bf16[6,64,64]{2,1,0:T(8,128)(2,1)}) custom-call(bf16[2,64,512]{2,1,0:T(8,128)(2,1)} %pad_maximum_fusion.2.rows_ref, bf16[2,64,64]{2,1,0:T(8,128)(2,1)} %bitcast.118), custom_call_target="tpu_custom_call" | custom-call | tf_op jit(solution)/shard_map/pallas_call | solution.py:69
  26.6 0.8 multiply_bitcast_fusion.3
  27.9 2.6 %select_select_fusion.cols_ref = bf16[64,72,128]{2,1,0:T(8,128)(2,1)} fusion(pred[128]{0:T(512)(128)(4,1)S(1)} %get-tuple-element.46, pred[128]{0:T(512)(128)(4,1)S(1)} %get-tuple-element.47, bf16[64,72]{1,0:T(8,128)(2,1)S(1)} %get-tuple-element.43, bf16[64,72]{1,0:T(8,128)(2,1)S(1)} %get-tuple-element.42), kind=kLoop, calls=%fused_computation | loop fusion | flops 1179648 | bytes 1198336 | tf_op jit(solution)/shard_map/jit(_where)/select_n | solution.py:112
  30.8 1.1 %pad_maximum_fusion.rows_ref = bf16[64,8,512]{2,1,0:T(8,128)(2,1)} fusion(bf16[64,1,512]{2,1,0:T(2,128)(2,1)S(1)} %copy.35, bf16[64,1,512]{2,1,0:T(2,128)(2,1)S(1)} %copy.34, bf16[8]{0:T(256)(128)(2,1)S(1)} %pad.40.clone), kind=kLoop, calls=%fused_computation.9 | loop fusion | flops 1572864 | bytes 655376 | tf_op jit(solution)/shard_map/concatenate | solution.py:107
  31.9 0.3 fusion.4
  32.3 1.6 %broadcast_bitcast_fusion = (f32[8,64,512]{2,1,0:T(8,128)}, f32[8,64,512]{2,1,0:T(8,128)}) fusion(f32[8,8,512]{2,1,0:T(8,128)S(1)} %get-tuple-element.32, f32[8,8,512]{2,1,0:T(8,128)S(1)} %get-tuple-element.33), kind=kLoop, calls=%fused_computation.10 | loop fusion | bytes 2359296 | tf_op jit(solution)/shard_map/broadcast_in_dim | solution.py:386
  33.9 39.3 %shard_map.77 = (bf16[64,64,512]{2,1,0:T(8,128)(2,1)}, f32[8,64,512]{2,1,0:T(8,128)}, f32[8,64,512]{2,1,0:T(8,128)}, f32[8,64,512]{2,1,0:T(8,128)}, f32[4,16,256]{2,1,0:T(8,128)}) custom-call(bf16[64,64,512]{2,1,0:T(8,128)(2,1)} %next_ref.1, bf16[64,64,512]{2,1,0:T(8,128)(2,1)} %next_ref.1, bf16[64,64,512]{2,1,0:T(8,128)(2,1)} %next_ref.1, ...), custom_call_target="tpu_custom_call" | custom-call | tf_op jit(solution)/shard_map/pallas_call | solution.py:223
  73.2 1.6 %bitcast_reduce_fusion.1 = f32[8,8,512]{2,1,0:T(8,128)S(1)} fusion(f32[8,64,512]{2,1,0:T(8,128)} %get-tuple-element.16), kind=kLoop, calls=%fused_computation.7 | loop fusion | flops 229376 | bytes 1179648 | tf_op jit(solution)/shard_map/reduce_sum | solution.py:263
  74.8 0.3 convolution_bitcast_fusion.1
  75.1 0.3 bitcast_reduce_fusion.2
  75.3 0.3 convolution_bitcast_fusion.2
  75.7 0.3 copy-done.1
  76.0 0.3 bitcast_reduce_fusion
  76.3 0.3 convolution_bitcast_fusion
  76.6 0.6 reduce_sum.59
  77.2 0.7 select_maximum_fusion
  78.0 0.8 maximum_maximum_fusion.depth_ref
  78.8 0.2 convolution_bitcast_fusion.3
  79.1 0.3 convolution_bitcast_fusion.4
  79.7 0.3 fusion.6
  80.5 0.7 maximum_maximum_fusion.1.plane_ref
  81.2 19.8 %shard_map.78 = (f32[8,8,128]{2,1,0:T(8,128)}, f32[16,32,128]{2,1,0:T(8,128)}) custom-call(f32[8,8,128]{2,1,0:T(8,128)} %maximum_maximum_fusion.1.plane_ref, f32[16,32,128]{2,1,0:T(8,128)} %maximum_maximum_fusion.depth_ref), custom_call_target="tpu_custom_call" | custom-call | tf_op jit(solution)/shard_map/pallas_call | solution.py:363
  100.9 0.9 slice.139
  101.9 0.7 slice_bitcast_fusion.6
  102.7 1.3 %slice.138 = f32[1,1,1]{2,1,0:T(1,128)} slice(f32[8,8,128]{2,1,0:T(8,128)} %get-tuple-element.19), slice={[0:1], [6:7], [33:34]} | slice | bytes 8 | tf_op jit(solution)/shard_map/slice | solution.py:419
  104.6 0.7 fusion.2
  105.3 0.2 slice.134
  106.4 0.8 copy.38
  (55 shorter events, 2.0 us)
Async XLA Ops:
  26.6 3.9 %copy-start.4 = (bf16[2,64,512]{2,1,0:T(8,128)(2,1)S(1)}, bf16[2,64,512]{2,1,0:T(8,128)(2,1)}, u32[]{:S(2)}) copy-start(bf16[2,64,512]{2,1,0:T(8,128)(2,1)} %get-tuple-element.12) | copy-start | bytes 393220
  27.8 4.1 %copy-start = (f32[2,32,512]{2,1,0:T(8,128)S(1)}, f32[2,32,512]{2,1,0:T(8,128)}, u32[]{:S(2)}) copy-start(f32[2,32,512]{2,1,0:T(8,128)} %param.9) | copy-start | bytes 393220
  27.9 4.1 %copy-start.3 = (f32[2,32,8,8]{1,3,2,0:T(8,128)S(1)}, f32[2,32,8,8]{1,3,2,0:T(8,128)}, u32[]{:S(2)}) copy-start(f32[2,32,8,8]{1,3,2,0:T(8,128)} %param.8) | copy-start | bytes 49156
  73.2 1.9 %copy-start.2 = (f32[8,64,512]{2,1,0:T(8,128)S(1)}, f32[8,64,512]{2,1,0:T(8,128)}, u32[]{:S(2)}) copy-start(f32[8,64,512]{2,1,0:T(8,128)} %get-tuple-element.15) | copy-start | bytes 3145732
  74.8 1.2 %copy-start.1 = (f32[8,64,512]{2,1,0:T(8,128)S(1)}, f32[8,64,512]{2,1,0:T(8,128)}, u32[]{:S(2)}) copy-start(f32[8,64,512]{2,1,0:T(8,128)} %get-tuple-element.17) | copy-start | bytes 3145732
  75.6 1.0 copy-start.5
  100.9 4.4 %copy-start.6 = (f32[8,8,128]{2,1,0:T(8,128)S(1)}, f32[8,8,128]{2,1,0:T(8,128)}, u32[]{:S(2)}) copy-start(f32[8,8,128]{2,1,0:T(8,128)} %get-tuple-element.19) | copy-start | bytes 98308

commit v18 on v16

--- a/solution.py
+++ b/solution.py
@@ -119,7 +119,7 @@
 
 
 def strip_kernel(prev_ref, main_ref, next_ref, rows_ref, cols_ref, disp_ref, image_ref,
-                 contrast_ref, bright_ref,
+                 fields_ref,
                  res_ref, prod_ref, mis_ref, sq_ref, energy_ref, pad_ref, shifts_ref):
     block = pl.program_id(0)
     depth_x = rows_ref.shape[0]
@@ -158,8 +158,16 @@
         c0 = pl.multiple_of((k % chunks_z) * LANES, LANES)
         rs = pl.ds(r0, ROWS)
         cs = pl.ds(c0, LANES)
-        contrast = contrast_ref[n, rs, cs]
-        bright = bright_ref[n, rs, cs]
+        j0 = r0 // KNOT
+        upper = lax.broadcasted_iota(jnp.int32, (ROWS, LANES), 0) < KNOT
+        node = lax.broadcasted_iota(jnp.int32, (KNOT, LANES), 0)
+
+        def node_row(kind, j):
+            return jnp.sum(jnp.where(node == j, fields_ref[kind, n, :, cs], 0.0),
+                           axis=0, keepdims=True)
+
+        contrast = jnp.where(upper, node_row(0, j0), node_row(0, j0 + 1))
+        bright = jnp.where(upper, node_row(1, j0), node_row(1, j0 + 1))
 
         def plane(step, acc):
             xl = n * KNOT + step
@@ -211,7 +219,7 @@
     energy_ref[0] = energy
 
 
-def strip_sums(deformed, rows, cols, displacement, image, contrast_y, bright_y):
+def strip_sums(deformed, rows, cols, displacement, image, fields):
     depth_x, width_y, width_z = image.shape
     nodes = depth_x // KNOT
     steps = depth_x // SPAN
@@ -232,8 +240,7 @@
             pl.BlockSpec(memory_space=pltpu.VMEM),
             pl.BlockSpec((3, SPAN, width_y, width_z), lambda i: (0, i, 0, 0)),
             plane_spec,
-            node_spec,
-            node_spec,
+            pl.BlockSpec((2, per) + fields.shape[2:], lambda i: (0, i, 0, 0)),
         ],
         out_specs=[
             plane_spec,
@@ -255,7 +262,7 @@
         ],
         compiler_params=pltpu.CompilerParams(
             dimension_semantics=("arbitrary",), vmem_limit_bytes=60 * 1024 * 1024),
-    )(deformed, deformed, deformed, rows, cols, displacement, image, contrast_y, bright_y)
+    )(deformed, deformed, deformed, rows, cols, displacement, image, fields)
 
 
 def node_sums(field):
@@ -383,9 +390,8 @@
 def local(reference_image, deformed, displacement, plane_factors, depth_factors):
     rows, cols = halo_blocks(deformed)
     fields = jnp.einsum("krij,krz->kijz", plane_factors, depth_factors, precision=highest)
-    fields = jnp.repeat(fields, KNOT, axis=2)
     residual, prod, mis, sq, energy_parts = strip_sums(
-        deformed, rows, cols, displacement, reference_image, fields[0], fields[1])
+        deformed, rows, cols, displacement, reference_image, fields)
     prod, mis, sq = node_sums(prod), node_sums(mis), node_sums(sq)
     local_energy = jnp.sum(energy_parts)
 

time: 106 us -> 105 us (level)
  local copies, waits for them, and re-layouts: 12.7 us -> 11.1 us
    broadcast_in_dim x1 -> x0, local copies, waits for them, and re-layouts: 1.6 us -> none  [local(): fields = jnp.repeat(fields, KNOT, axis=2)]
where the time goes in v18:
time: 105 us
  Pallas kernels  73.5 us (70%)
  other arithmetic  15.3 us (15%)
  local copies, waits for them, and re-layouts  11.1 us (11%)
  matrix products  2.6 us (2%)
  between operations  2.28 us (2%)
    pallas_call x1, Pallas kernels, strip_sums(): pl.pallas_call(strip_kernel, grid=(steps,), in_specs=[pl.BlockSpec((1, wi...  39.8 us
    pallas_call x1, Pallas kernels, both_sums(): pl.pallas_call(functools.partial(both_sums_kernel, nz, ny, plane_row, dep...  19.7 us
    pallas_call x1, Pallas kernels, swap_halos(): pl.pallas_call(functools.partial(halo_kernel, ny, nz), out_shape=[jax.Sha...  13.9 us
    reduce_sum x3, other arithmetic, node_sums(): return field.reshape(nodes, width_y // KNOT, KNOT, width_z).sum(axis=2)  4.48 us
    select_n x1, other arithmetic, halo_blocks(): jnp.where(lanes == 0, side_high[:, :, None], jnp.where(lanes == 127, side...  2.58 us

profile of v18, /device:TPU:1, one launch (start us, length us, event | category | flops | bytes accessed | tf_op | source)
XLA Modules:
  0.0 104.8 jit_solution(10699614488859180630)
XLA Ops:
  0.6 1.4 %fusion.21 = (bf16[64,1,512]{2,1,0:T(2,128)(2,1)S(1)}, bf16[64,1,512]{2,1,0:T(2,128)(2,1)S(1)}) fusion(bf16[64,64,512]{2,1,0:T(8,128)(2,1)} %next_ref.1), kind=kLoop, calls=%fused_computation.71 | loop fusion | bytes 262144 | tf_op jit(solution)/shard_map/slice | solution.py:90
  2.1 0.7 pad_maximum_fusion.2.rows_ref
  2.7 2.1 %fusion.20 = (bf16[64,64,1]{2,1,0:T(8,128)(2,1)S(1)}, bf16[64,64,1]{2,1,0:T(8,128)(2,1)S(1)}) fusion(bf16[64,64,512]{2,1,0:T(8,128)(2,1)} %next_ref.1), kind=kLoop, calls=%fused_computation.70 | loop fusion | bytes 32768 | tf_op jit(solution)/shard_map/slice | solution.py:91
  4.8 0.5 copy.46
  5.3 0.5 copy.47
  5.8 0.6 pad_maximum_fusion.3.cols_ref
  6.4 13.9 %shard_map.76 = (bf16[2,64,512]{2,1,0:T(8,128)(2,1)}, bf16[6,64,64]{2,1,0:T(8,128)(2,1)}) custom-call(bf16[2,64,512]{2,1,0:T(8,128)(2,1)} %pad_maximum_fusion.2.rows_ref, bf16[2,64,64]{2,1,0:T(8,128)(2,1)} %pad_maximum_fusion.3.cols_ref), custom_call_target="tpu_custom_call" | custom-call | tf_op jit(solution)/shard_map/pallas_call | solution.py:69
  20.3 0.8 multiply_bitcast_fusion.3
  21.6 2.6 %select_select_fusion.cols_ref = bf16[64,72,128]{2,1,0:T(8,128)(2,1)} fusion(pred[128]{0:T(512)(128)(4,1)S(1)} %get-tuple-element.46, pred[128]{0:T(512)(128)(4,1)S(1)} %get-tuple-element.47, bf16[64,72]{1,0:T(8,128)(2,1)S(1)} %get-tuple-element.43, bf16[64,72]{1,0:T(8,128)(2,1)S(1)} %get-tuple-element.42), kind=kLoop, calls=%fused_computation | loop fusion | flops 1179648 | bytes 1198336 | tf_op jit(solution)/shard_map/jit(_where)/select_n | solution.py:112
  24.1 0.9 multiply_bitcast_fusion.1
  25.3 1.1 %pad_maximum_fusion.rows_ref = bf16[64,8,512]{2,1,0:T(8,128)(2,1)} fusion(bf16[64,1,512]{2,1,0:T(2,128)(2,1)S(1)} %copy.39, bf16[64,1,512]{2,1,0:T(2,128)(2,1)S(1)} %copy.38, bf16[8]{0:T(256)(128)(2,1)S(1)} %pad.40.clone), kind=kLoop, calls=%fused_computation.9 | loop fusion | flops 1572864 | bytes 655376 | tf_op jit(solution)/shard_map/concatenate | solution.py:107
  26.5 1.1 %fusion.4.fields_ref = f32[2,8,8,512]{3,2,1,0:T(8,128)} fusion(f32[2,32,8,8]{1,3,2,0:T(8,128)S(1)} %copy-done.1, f32[2,32,512]{2,1,0:T(8,128)S(1)} %copy-done), kind=kOutput, calls=%fused_computation.22 | convolution fusion | flops 25165824 | bytes 409600 | tf_op jit(solution)/shard_map/krij,krz->kijz/dot_general | solution.py:392
  27.5 39.8 %shard_map.77 = (bf16[64,64,512]{2,1,0:T(8,128)(2,1)}, f32[8,64,512]{2,1,0:T(8,128)}, f32[8,64,512]{2,1,0:T(8,128)}, f32[8,64,512]{2,1,0:T(8,128)}, f32[4,16,256]{2,1,0:T(8,128)}) custom-call(bf16[64,64,512]{2,1,0:T(8,128)(2,1)} %next_ref.1, bf16[64,64,512]{2,1,0:T(8,128)(2,1)} %next_ref.1, bf16[64,64,512]{2,1,0:T(8,128)(2,1)} %next_ref.1, ...), custom_call_target="tpu_custom_call" | custom-call | tf_op jit(solution)/shard_map/pallas_call | solution.py:231
  67.4 1.5 %bitcast_reduce_fusion.1 = f32[8,8,512]{2,1,0:T(8,128)S(1)} fusion(f32[8,64,512]{2,1,0:T(8,128)} %get-tuple-element.16), kind=kLoop, calls=%fused_computation.7 | loop fusion | flops 229376 | bytes 1179648 | tf_op jit(solution)/shard_map/reduce_sum | solution.py:270
  68.9 0.3 convolution_bitcast_fusion.1
  69.2 1.5 %bitcast_reduce_fusion.2 = f32[8,8,512]{2,1,0:T(8,128)S(1)} fusion(f32[8,64,512]{2,1,0:T(8,128)} %get-tuple-element.15), kind=kLoop, calls=%fused_computation.8 | loop fusion | flops 229376 | bytes 1179648 | tf_op jit(solution)/shard_map/reduce_sum | solution.py:270
  70.7 0.3 convolution_bitcast_fusion.2
  71.0 1.5 %bitcast_reduce_fusion = f32[8,8,512]{2,1,0:T(8,128)S(1)} fusion(f32[8,64,512]{2,1,0:T(8,128)} %get-tuple-element.17), kind=kLoop, calls=%fused_computation.6 | loop fusion | flops 229376 | bytes 1179648 | tf_op jit(solution)/shard_map/reduce_sum | solution.py:270
  72.5 0.3 convolution_bitcast_fusion
  72.8 0.6 reduce_sum.59
  73.5 0.7 select_maximum_fusion
  74.3 0.8 maximum_maximum_fusion.depth_ref
  75.9 0.3 fusion.6
  76.7 0.7 maximum_maximum_fusion.1.plane_ref
  77.4 19.7 %shard_map.78 = (f32[8,8,128]{2,1,0:T(8,128)}, f32[16,32,128]{2,1,0:T(8,128)}) custom-call(f32[8,8,128]{2,1,0:T(8,128)} %maximum_maximum_fusion.1.plane_ref, f32[16,32,128]{2,1,0:T(8,128)} %maximum_maximum_fusion.depth_ref), custom_call_target="tpu_custom_call" | custom-call | tf_op jit(solution)/shard_map/pallas_call | solution.py:370
  97.1 0.9 slice.125
  98.1 0.7 slice_bitcast_fusion.4
  98.9 1.3 %slice.124 = f32[1,1,1]{2,1,0:T(1,128)} slice(f32[8,8,128]{2,1,0:T(8,128)} %get-tuple-element.19), slice={[0:1], [6:7], [33:34]} | slice | bytes 8 | tf_op jit(solution)/shard_map/slice | solution.py:425
  100.8 0.7 fusion.2
  101.5 1.0 slice.120
  102.5 0.7 slice_bitcast_fusion.5
  104.0 0.8 copy.42
  (47 shorter events, 2.5 us)
Async XLA Ops:
  2.7 23.7 %copy-start = (f32[2,32,512]{2,1,0:T(8,128)S(1)}, f32[2,32,512]{2,1,0:T(8,128)}, u32[]{:S(2)}) copy-start(f32[2,32,512]{2,1,0:T(8,128)} %param.9) | copy-start | bytes 393220
  2.7 23.7 %copy-start.1 = (f32[2,32,8,8]{1,3,2,0:T(8,128)S(1)}, f32[2,32,8,8]{1,3,2,0:T(8,128)}, u32[]{:S(2)}) copy-start(f32[2,32,8,8]{1,3,2,0:T(8,128)} %param.8) | copy-start | bytes 49156
  67.4 5.4 %copy-start.2 = (f32[4,16,256]{2,1,0:T(8,128)S(1)}, f32[4,16,256]{2,1,0:T(8,128)}, u32[]{:S(2)}) copy-start(f32[4,16,256]{2,1,0:T(8,128)} %get-tuple-element.18) | copy-start | bytes 196612

commit v19 on v16

--- a/solution.py
+++ b/solution.py
@@ -147,7 +147,7 @@
         source_plane(p, main_ref[p - 1])
         return carry
 
-    lax.fori_loop(1, SPAN + 1, inner_plane, 0, unroll=4)
+    lax.fori_loop(1, SPAN + 1, inner_plane, 0, unroll=8)
     source_plane(SPAN + 1, next_ref[0])
 
     chunks_y = width_y // ROWS

time: 106 us -> 105 us (level)
  no operation moved by 1% of the time
where the time goes in v19:
time: 105 us
  Pallas kernels  72.6 us (69%)
  other arithmetic  15.3 us (15%)
  local copies, waits for them, and re-layouts  12.7 us (12%)
  between operations  2.3 us (2%)
  matrix products  1.87 us (2%)
    pallas_call x1, Pallas kernels, strip_sums(): pl.pallas_call(strip_kernel, grid=(steps,), in_specs=[pl.BlockSpec((1, wi...  39 us
    pallas_call x1, Pallas kernels, both_sums(): pl.pallas_call(functools.partial(both_sums_kernel, nz, ny, plane_row, dep...  19.7 us
    pallas_call x1, Pallas kernels, swap_halos(): pl.pallas_call(functools.partial(halo_kernel, ny, nz), out_shape=[jax.Sha...  13.9 us
    reduce_sum x3, other arithmetic, node_sums(): return field.reshape(nodes, width_y // KNOT, KNOT, width_z).sum(axis=2)  4.48 us
    select_n x1, other arithmetic, halo_blocks(): jnp.where(lanes == 0, side_high[:, :, None], jnp.where(lanes == 127, side...  2.58 us

profile of v19, /device:TPU:1, one launch (start us, length us, event | category | flops | bytes accessed | tf_op | source)
XLA Modules:
  0.0 104.8 jit_solution(13772655587638398091)
XLA Ops:
  0.6 1.4 %fusion.21 = (bf16[64,1,512]{2,1,0:T(2,128)(2,1)S(1)}, bf16[64,1,512]{2,1,0:T(2,128)(2,1)S(1)}) fusion(bf16[64,64,512]{2,1,0:T(8,128)(2,1)} %next_ref.1), kind=kLoop, calls=%fused_computation.75 | loop fusion | bytes 262144 | tf_op jit(solution)/shard_map/slice | solution.py:90
  2.1 0.7 pad_maximum_fusion.2.rows_ref
  2.7 2.1 %fusion.20 = (bf16[64,64,1]{2,1,0:T(8,128)(2,1)S(1)}, bf16[64,64,1]{2,1,0:T(8,128)(2,1)S(1)}) fusion(bf16[64,64,512]{2,1,0:T(8,128)(2,1)} %next_ref.1), kind=kLoop, calls=%fused_computation.74 | loop fusion | bytes 32768 | tf_op jit(solution)/shard_map/slice | solution.py:91
  4.8 0.5 copy.46
  5.3 0.5 copy.47
  5.8 0.6 pad_maximum_fusion.3.cols_ref
  6.4 13.9 %shard_map.76 = (bf16[2,64,512]{2,1,0:T(8,128)(2,1)}, bf16[6,64,64]{2,1,0:T(8,128)(2,1)}) custom-call(bf16[2,64,512]{2,1,0:T(8,128)(2,1)} %pad_maximum_fusion.2.rows_ref, bf16[2,64,64]{2,1,0:T(8,128)(2,1)} %pad_maximum_fusion.3.cols_ref), custom_call_target="tpu_custom_call" | custom-call | tf_op jit(solution)/shard_map/pallas_call | solution.py:69
  20.3 0.8 multiply_bitcast_fusion.3
  21.6 2.6 %select_select_fusion.cols_ref = bf16[64,72,128]{2,1,0:T(8,128)(2,1)} fusion(pred[128]{0:T(512)(128)(4,1)S(1)} %get-tuple-element.48, pred[128]{0:T(512)(128)(4,1)S(1)} %get-tuple-element.49, bf16[64,72]{1,0:T(8,128)(2,1)S(1)} %get-tuple-element.45, bf16[64,72]{1,0:T(8,128)(2,1)S(1)} %get-tuple-element.44), kind=kLoop, calls=%fused_computation | loop fusion | flops 1179648 | bytes 1198336 | tf_op jit(solution)/shard_map/jit(_where)/select_n | solution.py:112
  24.1 0.9 multiply_bitcast_fusion.1
  25.3 1.2 %pad_maximum_fusion.rows_ref = bf16[64,8,512]{2,1,0:T(8,128)(2,1)} fusion(bf16[64,1,512]{2,1,0:T(2,128)(2,1)S(1)} %copy.39, bf16[64,1,512]{2,1,0:T(2,128)(2,1)S(1)} %copy.38, bf16[8]{0:T(256)(128)(2,1)S(1)} %pad.40.clone), kind=kLoop, calls=%fused_computation.9 | loop fusion | flops 1572864 | bytes 655376 | tf_op jit(solution)/shard_map/concatenate | solution.py:107
  26.5 0.3 fusion.4
  26.9 1.6 %broadcast_bitcast_fusion = (f32[8,64,512]{2,1,0:T(8,128)}, f32[8,64,512]{2,1,0:T(8,128)}) fusion(f32[8,8,512]{2,1,0:T(8,128)S(1)} %get-tuple-element.34, f32[8,8,512]{2,1,0:T(8,128)S(1)} %get-tuple-element.35), kind=kLoop, calls=%fused_computation.10 | loop fusion | bytes 2359296 | tf_op jit(solution)/shard_map/broadcast_in_dim | solution.py:386
  28.5 39.0 %shard_map.77 = (bf16[64,64,512]{2,1,0:T(8,128)(2,1)}, f32[8,64,512]{2,1,0:T(8,128)}, f32[8,64,512]{2,1,0:T(8,128)}, f32[8,64,512]{2,1,0:T(8,128)}, f32[4,16,256]{2,1,0:T(8,128)}) custom-call(bf16[64,64,512]{2,1,0:T(8,128)(2,1)} %next_ref.1, bf16[64,64,512]{2,1,0:T(8,128)(2,1)} %next_ref.1, bf16[64,64,512]{2,1,0:T(8,128)(2,1)} %next_ref.1, ...), custom_call_target="tpu_custom_call" | custom-call | tf_op jit(solution)/shard_map/pallas_call | solution.py:223
  67.4 1.5 %bitcast_reduce_fusion.1 = f32[8,8,512]{2,1,0:T(8,128)S(1)} fusion(f32[8,64,512]{2,1,0:T(8,128)} %get-tuple-element.16), kind=kLoop, calls=%fused_computation.7 | loop fusion | flops 229376 | bytes 1179648 | tf_op jit(solution)/shard_map/reduce_sum | solution.py:263
  69.2 1.5 %bitcast_reduce_fusion.2 = f32[8,8,512]{2,1,0:T(8,128)S(1)} fusion(f32[8,64,512]{2,1,0:T(8,128)} %get-tuple-element.15), kind=kLoop, calls=%fused_computation.8 | loop fusion | flops 229376 | bytes 1179648 | tf_op jit(solution)/shard_map/reduce_sum | solution.py:263
  70.7 0.3 convolution_bitcast_fusion.2
  71.0 1.5 %bitcast_reduce_fusion = f32[8,8,512]{2,1,0:T(8,128)S(1)} fusion(f32[8,64,512]{2,1,0:T(8,128)} %get-tuple-element.17), kind=kLoop, calls=%fused_computation.6 | loop fusion | flops 229376 | bytes 1179648 | tf_op jit(solution)/shard_map/reduce_sum | solution.py:263
  72.5 0.3 convolution_bitcast_fusion
  72.8 0.6 reduce_sum.59
  73.5 0.7 select_maximum_fusion
  74.3 0.8 maximum_maximum_fusion.depth_ref
  75.9 0.3 fusion.6
  76.7 0.7 maximum_maximum_fusion.1.plane_ref
  77.4 19.7 %shard_map.78 = (f32[8,8,128]{2,1,0:T(8,128)}, f32[16,32,128]{2,1,0:T(8,128)}) custom-call(f32[8,8,128]{2,1,0:T(8,128)} %maximum_maximum_fusion.1.plane_ref, f32[16,32,128]{2,1,0:T(8,128)} %maximum_maximum_fusion.depth_ref), custom_call_target="tpu_custom_call" | custom-call | tf_op jit(solution)/shard_map/pallas_call | solution.py:363
  97.2 0.9 slice.143
  98.2 0.7 slice_bitcast_fusion.6
  98.9 1.3 %slice.142 = f32[1,1,1]{2,1,0:T(1,128)} slice(f32[8,8,128]{2,1,0:T(8,128)} %get-tuple-element.19), slice={[0:1], [6:7], [33:34]} | slice | bytes 8 | tf_op jit(solution)/shard_map/slice | solution.py:419
  100.9 0.7 fusion.2
  101.5 1.0 slice.138
  102.5 0.7 slice_bitcast_fusion.7
  104.1 0.8 copy.42
  (49 shorter events, 2.7 us)
Async XLA Ops:
  2.7 23.7 %copy-start = (f32[2,32,512]{2,1,0:T(8,128)S(1)}, f32[2,32,512]{2,1,0:T(8,128)}, u32[]{:S(2)}) copy-start(f32[2,32,512]{2,1,0:T(8,128)} %param.9) | copy-start | bytes 393220
  2.7 23.7 %copy-start.1 = (f32[2,32,8,8]{1,3,2,0:T(8,128)S(1)}, f32[2,32,8,8]{1,3,2,0:T(8,128)}, u32[]{:S(2)}) copy-start(f32[2,32,8,8]{1,3,2,0:T(8,128)} %param.8) | copy-start | bytes 49156
  67.4 5.4 %copy-start.2 = (f32[4,16,256]{2,1,0:T(8,128)S(1)}, f32[4,16,256]{2,1,0:T(8,128)}, u32[]{:S(2)}) copy-start(f32[4,16,256]{2,1,0:T(8,128)} %get-tuple-element.18) | copy-start | bytes 196612
